TPU v7x, 256 devices: a whole 4x4x8 slice. The times are simulated.
256 devices in a mesh: tx: 16 (over z, core), ty: 8 (over x_hi, y), mode: 2 (over x_lo).
Axes of the slice: x: 4 (x_hi: 2, x_lo: 2; x = x_hi * 2 + x_lo), y: 4, z: 8, core: 2. Of those that a mesh axis runs over, the one named last changes fastest.
Arguments:
- obj: float32 [2, 4096, 8192], P(None, 'tx', 'ty'), may hold values from -4 to 4
- probe: float32 [4, 2, 256, 256], P('mode'), may hold values from -4 to 4
- intensity: float32 [16, 8, 2, 256, 256], P('tx', 'ty'), may hold values from 0 to 2
- offsets: int32 [16, 8, 2, 2], P('tx', 'ty'), may hold values from 0 to 1023, as said below
- counts: int32 [16, 8], P('tx', 'ty'), may hold values from 1 to 2, as said below
- patch_filters: float32 [16, 4], replicated, may hold values from -2 to 2
Outputs:
- new_obj: float32 [2, 4096, 8192], P(None, 'tx', 'ty')
Inputs may be any that keep to these rules, and one draw needn't show every extreme that they name: Row offsets are below 256, column offsets below 1024; a pattern may reach into the tiles below and to the right. Slots from counts[a,b] on are empty.
All inputs are finite; a program needn't handle non-finite values.
Results may differ from a plain program's by a relative error of at most 0.00012.
Values sent between devices are 32-bit elements; how exact they have to be, the bound alone decides.
No kernel may reach another device: no remote copies, remote signals or barrier semaphores. Data moves between devices by JAX's collectives and lax.ppermute only.
A program may use at most 128 MiB of HBM per device.

v0:
```python
import functools
import math

import jax
import jax.numpy as jnp
import numpy as np
from jax import lax
from jax.experimental import pallas as pl
from jax.experimental.pallas import tpu as pltpu
from jax.sharding import PartitionSpec as P


W = 256
axes = ("tx", "ty", "mode")
step_size = 0.25
f32 = jnp.float32
bf16 = jnp.bfloat16
VMEM = pl.BlockSpec(memory_space=pltpu.VMEM)
SMEM = pl.BlockSpec(memory_space=pltpu.SMEM)


def rings(mesh):
    n_tx, n_ty = mesh.shape["tx"], mesh.shape["ty"]
    half = n_ty // 2

    def lin(a, b, m):
        return (a * n_ty + b) * 2 + m

    def perm(move):
        return [
            (lin(a, b, m), lin(*move(a, b, m)))
            for a in range(n_tx)
            for b in range(n_ty)
            for m in range(2)
        ]

    def side(b, d, m):
        other = (b + d) % n_ty
        return other, (1 - m if b // half != other // half else m)

    return {
        "up": perm(lambda a, b, m: ((a - 1) % n_tx, b, m)),
        "down": perm(lambda a, b, m: ((a + 1) % n_tx, b, m)),
        "left": perm(lambda a, b, m: (a, *side(b, -1, m))),
        "right": perm(lambda a, b, m: (a, *side(b, 1, m))),
        "core": perm(lambda a, b, m: (a ^ 1, b, m)),
        "swap": perm(lambda a, b, m: (a, b, 1 - m)),
    }


def split(x):
    high = x.astype(bf16)
    return high, (x - high.astype(f32)).astype(bf16)


def tables():
    half = W // 2
    k, l = np.arange(half)[:, None], np.arange(half)[None, :]
    out = []
    for shift in (0, 1):
        angle = (k * (2 * l + shift) % W) * (2.0 * math.pi / W)
        re, im = np.cos(angle) / math.sqrt(W), -np.sin(angle) / math.sqrt(W)
        block = np.block([[re, im], [-im, re]])
        for mat in (block, block.T):
            high = mat.astype(jnp.bfloat16)
            out += [high, (mat - high.astype(np.float64)).astype(jnp.bfloat16)]
    return out


def dot(a, b):
    return jnp.dot(a, b, preferred_element_type=f32)


def rows_times(x, table):
    xh, xl = split(x)
    high, low = table
    return dot(xh, high) + dot(xh, low) + dot(xl, high)


def cols_times(table, x):
    xh, xl = split(x)
    high, low = table
    return dot(high, xh) + dot(low, xh) + dot(high, xl)


def forward(re, im, even, even_t, odd, odd_t):
    h = W // 2

    def lanes(x, y):
        return jnp.concatenate([x, y], axis=1)

    def stack(x, y):
        return jnp.concatenate([x, y], axis=0)

    e = rows_times(lanes(re[:, :h] + re[:, h:], im[:, :h] + im[:, h:]), even)
    o = rows_times(lanes(re[:, :h] - re[:, h:], im[:, :h] - im[:, h:]), odd)
    re, im = lanes(e[:, :h], o[:, :h]), lanes(e[:, h:], o[:, h:])
    e = cols_times(even_t, stack(re[:h] + re[h:], im[:h] + im[h:]))
    o = cols_times(odd_t, stack(re[:h] - re[h:], im[:h] - im[h:]))
    return stack(e[:h], o[:h]), stack(e[h:], o[h:])


def backward(re, im, even, even_t, odd, odd_t):
    h = W // 2

    def lanes(x, y):
        return jnp.concatenate([x, y], axis=1)

    def stack(x, y):
        return jnp.concatenate([x, y], axis=0)

    a = rows_times(lanes(re[:, :h], im[:, :h]), even_t)
    b = rows_times(lanes(re[:, h:], im[:, h:]), odd_t)
    p, n = a + b, a - b
    re, im = lanes(p[:, :h], n[:, :h]), lanes(p[:, h:], n[:, h:])
    a = cols_times(even, stack(re[:h], im[:h]))
    b = cols_times(odd, stack(re[h:], im[h:]))
    p, n = a + b, a - b
    return stack(p[:h], n[:h]), stack(p[h:], n[h:])


def iota(axis):
    return lax.broadcasted_iota(jnp.int32, (W, W), axis)


def window(obj, c, right, q, s):
    lane = iota(1)
    last = lax.axis_index("ty") == lax.axis_size("ty") - 1
    here = obj[c, :, pl.ds(pl.multiple_of(q * W, W), W)]
    nxt = obj[c, :, pl.ds(pl.multiple_of(jnp.minimum(q + 1, 3) * W, W), W)]
    nxt = jnp.where(q == 3, jnp.where(last, 0.0, right[...]), nxt)
    return jnp.where(lane >= s, here, nxt)


def place(table, slot):
    col0 = table[slot, 1]
    return table[slot, 0], col0 // W, lax.rem(col0, W)


def rim_rows(obj, c, row, right, left):
    last = lax.axis_index("ty") == lax.axis_size("ty") - 1
    first = lax.axis_index("ty") == 0
    edge = jnp.where(first, 0.0, left[c, row : row + 1, :])
    parts = [obj[c, row : row + 1, k * W : (k + 1) * W] for k in range(4)]
    parts.append(jnp.where(last, 0.0, right[row : row + 1, :]))
    parts.append(jnp.concatenate([edge, edge], axis=1))
    return parts


def send_body(c, above, obj, right, out):
    _, q, s = place(above, lax.axis_index("mode"))
    out[...] = window(obj, c, right, q, s)


def rim_body(obj, left, right_0, right_1, up_out, down_out):
    for c, right in enumerate((right_0, right_1)):
        for row, out in ((0, up_out), (W - 1, down_out)):
            for k, part in enumerate(rim_rows(obj, c, row, right, left)):
                out[c, k : k + 1, :] = part
            out[c, 6:8, :] = jnp.zeros((2, W), f32)


def main_body(offs, counts, obj, right_0, right_1, below_0, below_1, probe_a, probe_b, probe_c, meas, *refs):
    mats, (grad_0, grad_1, wave) = refs[:8], refs[8:]
    m = lax.axis_index("mode")
    last_tx = lax.axis_index("tx") == lax.axis_size("tx") - 1
    row0, q, s = place(offs, m)
    live = jnp.where(m < counts[0, 0], 1.0, 0.0).astype(f32)
    lane, row = iota(1), iota(0)
    patch = []
    for c, right, below in ((0, right_0, below_0), (1, right_1, below_1)):
        low = jnp.where(last_tx, 0.0, below[...])
        rolled = jnp.where(row >= row0, window(obj, c, right, q, s), low)
        rolled = pltpu.roll(rolled, lax.rem(W - row0, W), 0)
        patch.append(pltpu.roll(rolled, lax.rem(W - s, W), 1))

    def probe(k, c):
        return (probe_a[0, c], probe_a[1, c], probe_b[0, c], probe_c[0, c])[k]

    tabs = [(mats[2 * k][...], mats[2 * k + 1][...]) for k in range(4)]
    power = jnp.zeros((W, W), f32)
    for k in range(4):
        pr, pi = probe(k, 0), probe(k, 1)
        wr, wi = forward(pr * patch[0] - pi * patch[1], pr * patch[1] + pi * patch[0], *tabs)
        wave[k, 0] = wr
        wave[k, 1] = wi
        power = power + wr * wr + wi * wi
    resid = power - meas[...]
    grad = [jnp.zeros((W, W), f32), jnp.zeros((W, W), f32)]
    for k in range(4):
        pr, pi = probe(k, 0), probe(k, 1)
        br, bi = backward(resid * wave[k, 0], resid * wave[k, 1], *tabs)
        grad[0] = grad[0] + pr * br + pi * bi
        grad[1] = grad[1] + pr * bi - pi * br
    for g, out in ((grad[0], grad_0), (grad[1], grad_1)):
        out[...] = pltpu.roll(pltpu.roll(g * live, row0, 0), s, 1)


def sort_body(meas, out):
    m = lax.axis_index("mode")
    h = W // 2
    lane, row = iota(1), iota(0)

    def nth(k):
        return jnp.where(k < h, 2 * k, 2 * k - W + 1)

    pick_cols = jnp.where(row == nth(lane), 1.0, 0.0).astype(bf16)
    pick_rows = jnp.where(lane == nth(row), 1.0, 0.0).astype(bf16)

    def parts(x):
        for _ in range(3):
            part = x.astype(bf16)
            x = x - part.astype(f32)
            yield part

    x = sum(dot(part, pick_cols) for part in parts(meas[0, 0, m]))
    out[...] = sum(dot(pick_rows, part) for part in parts(x))


def spill_body(n, offs, above, *refs):
    m = lax.axis_index("mode")
    tx = lax.axis_index("tx")
    lane, row = iota(1), iota(0)
    total = jnp.zeros((W, W), f32)
    for k, slot in enumerate((m, 1 - m)[:n]):
        row0, q, s = place(offs, slot)
        total = total + jnp.where((q == 3) & (lane < s) & (row >= row0), refs[k][...], 0.0)
        row0, q, s = place(above, slot)
        keep = (q == 3) & (lane < s) & (row < row0) & (tx > 0)
        total = total + jnp.where(keep, refs[n + k][...], 0.0)
    refs[2 * n][...] = total


def take(out, ref, spot, rows):
    _, q, s = spot
    lane = iota(1)
    value = ref[...]
    here = pl.ds(pl.multiple_of(q * W, W), W)
    out[:, here] = out[:, here] - step_size * jnp.where(rows & (lane >= s), value, 0.0)
    nxt = pl.ds(pl.multiple_of(jnp.minimum(q + 1, 3) * W, W), W)
    keep = rows & (lane < s) & (q < 3)
    out[:, nxt] = out[:, nxt] - step_size * jnp.where(keep, value, 0.0)


def prior_body(c, filt, offs, obj, right, left, up, down, own, out):
    tx, ty = lax.axis_index("tx"), lax.axis_index("ty")
    n_tx, n_ty = lax.axis_size("tx"), lax.axis_size("ty")
    cols = obj.shape[2]
    shape = (W, cols)
    lane = lax.broadcasted_iota(jnp.int32, shape, 1)
    row = lax.broadcasted_iota(jnp.int32, shape, 0)
    taps = [[filt[i, k] for i in range(4)] for k in range(filt.shape[1])]
    g = [[sum(tap[i] * tap[j] for tap in taps) for j in range(4)] for i in range(4)]

    def beside(x, before, after):
        one_left = jnp.where(lane == 0, before, pltpu.roll(x, 1, 1))
        one_right = jnp.where(lane == cols - 1, after, pltpu.roll(x, cols - 1, 1))
        return one_left, one_right

    spot = place(offs, lax.axis_index("mode"))
    x = obj[c]
    after = jnp.where(ty == n_ty - 1, 0.0, right[:, 0:1])
    before = jnp.where(ty == 0, 0.0, left[c, :, 127:128])

    def line(rim, flag):
        rim = jnp.where(flag, 0.0, rim)
        whole = jnp.concatenate([rim[k : k + 1, :] for k in range(4)], axis=1)
        return whole, rim[5:6, W - 1 : W], rim[4:5, 0:1]

    u_mid, u_left, u_right = line(up[c], tx == 0)
    d_mid, d_left, d_right = line(down[c], tx == n_tx - 1)
    xl, xr = beside(x, before, after)

    def above(mid, edge):
        return jnp.where(row == 0, edge, pltpu.roll(mid, 1, 0))

    def under(mid, edge):
        return jnp.where(row == W - 1, edge, pltpu.roll(mid, W - 1, 0))

    def shift_line(mid, b, a):
        l1 = lax.broadcasted_iota(jnp.int32, (1, cols), 1)
        return (
            jnp.where(l1 == 0, b, pltpu.roll(mid, 1, 1)),
            jnp.where(l1 == cols - 1, a, pltpu.roll(mid, cols - 1, 1)),
        )

    ul, ur = shift_line(u_mid, u_left, u_right)
    dl, dr = shift_line(d_mid, d_left, d_right)
    xu, xd = above(x, u_mid), under(x, d_mid)
    xul, xur = above(xl, ul), above(xr, ur)
    xdl, xdr = under(xl, dl), under(xr, dr)
    in_col = (lane > 0) | (ty > 0)
    in_row = (row > 0) | (tx > 0)
    total = g[0][0] * x + g[0][1] * xr + g[0][2] * xd + g[0][3] * xdr
    total += jnp.where(in_col, g[1][0] * xl + g[1][1] * x + g[1][2] * xdl + g[1][3] * xd, 0.0)
    total += jnp.where(in_row, g[2][0] * xu + g[2][1] * xur + g[2][2] * x + g[2][3] * xr, 0.0)
    total += jnp.where(
        in_row & in_col, g[3][0] * xul + g[3][1] * xu + g[3][2] * xl + g[3][3] * x, 0.0
    )
    out[...] = x - step_size * total
    take(out, own, spot, iota(0) >= spot[0])


def mid_body(offs, above, base_0, base_1, own_0, own_1, up_m0, up_m1, up_p0, up_p1, left_0, out, first):
    m = lax.axis_index("mode")
    tx, ty = lax.axis_index("tx"), lax.axis_index("ty")
    row = iota(0)
    mine, from_m, from_p = place(offs, 1 - m), place(above, m), place(above, 1 - m)
    for c, base, own_p, up_m, up_p in (
        (0, base_0, own_0, up_m0, up_p0),
        (1, base_1, own_1, up_m1, up_p1),
    ):
        part = out.at[c]
        part[...] = base[...]
        take(part, own_p, mine, row >= mine[0])
        take(part, up_m, from_m, (row < from_m[0]) & (tx > 0))
        take(part, up_p, from_p, (row < from_p[0]) & (tx > 0))
        value = part[:, 0:W]
        if c == 0:
            value = value - step_size * jnp.where(ty > 0, left_0[...], 0.0)
        first[c] = value


def final_body(mid, first, left_0, left_1, out, buf, sems):
    ty = lax.axis_index("ty")
    stores = [pltpu.make_async_copy(buf.at[c], out.at[c, :, 0:W], sems.at[c]) for c in range(2)]
    for c, left in enumerate((left_0, left_1)):
        buf[c] = first[c] - step_size * jnp.where(ty > 0, left[...], 0.0)
        stores[c].start()
    for store in stores:
        store.wait()


def call(body, shapes, in_specs, limit, flops, bytes_accessed, scratch=(), out_spec=VMEM, aliases={}):
    many = isinstance(shapes, list)
    outs = [jax.ShapeDtypeStruct(s, f32) for s in (shapes if many else [shapes])]
    return pl.pallas_call(
        body,
        out_shape=outs if many else outs[0],
        in_specs=in_specs,
        out_specs=[out_spec] * len(outs) if many else out_spec,
        scratch_shapes=list(scratch),
        input_output_aliases=aliases,
        compiler_params=pltpu.CompilerParams(vmem_limit_bytes=limit << 20),
        cost_estimate=pl.CostEstimate(flops=flops, bytes_accessed=bytes_accessed, transcendentals=0),
    )


def local(ring, obj, probe, intensity, offsets, counts, filters):
    def go(value, where):
        return lax.ppermute(value, axes, ring[where])

    tabs = [jnp.asarray(t) for t in tables()]

    rows, cols = obj.shape[1:]
    piece = (W, W)
    whole = (2, rows, cols)
    offs = offsets.reshape(2, 2)
    right = [go(obj[0, :, :W], "left")]
    right.append(go(lax.optimization_barrier(obj)[1, :, :W], "left"))
    core = lax.rem(lax.axis_index("tx"), 2)
    probe_b = go(lax.dynamic_slice_in_dim(probe, core, 1, 0), "swap")
    probe_c = go(probe_b, "core")
    above = go(offs, "down")
    left = go(obj[:, :, cols - 128 :], "right")
    filt = filters.T
    meas = call(sort_body, piece, [VMEM], 8, 1 << 26, 3 << 18)(intensity)
    below = [
        go(
            call(functools.partial(send_body, c), piece, [SMEM] + [VMEM] * 2, 8, 1 << 20, 2 << 20)(
                above, obj, right[c]
            ),
            "up",
        )
        for c in (0, 1)
    ]
    rims = call(rim_body, [(2, 8, W)] * 2, [VMEM] * 4, 8, 1 << 16, 2 << 20)(obj, left, *right)
    under, over = go(rims[0], "up"), go(rims[1], "down")
    g0, g1 = call(
        main_body,
        [piece] * 2,
        [SMEM, SMEM] + [VMEM] * 17,
        16,
        5 << 30,
        12 << 20,
        [pltpu.VMEM((4, 2, W, W), f32)],
    )(offs, counts, obj, *right, *below, probe, probe_b, probe_c, meas, *tabs)
    p1, b0 = go(g1, "swap"), go(g0, "down")
    p0, b1 = go(g0, "swap"), go(g1, "down")
    base = [
        call(
            functools.partial(prior_body, c), (rows, cols), [SMEM, SMEM] + [VMEM] * 6, 12, 1 << 27, 8 << 20
        )(filt, offs, obj, right[c], left, over, under, g)
        for c, g in ((0, g0), (1, g1))
    ]
    c1, c0 = go(p1, "down"), go(p0, "down")

    def spill(n, *args):
        specs = [SMEM, SMEM] + [VMEM] * (2 * n)
        kernel = call(functools.partial(spill_body, n), piece, specs, 8, 1 << 18, 1 << 20)
        return kernel(offs, above, *args)

    left_m0 = go(spill(1, g0, b0), "right")
    left_p0 = go(left_m0, "swap")
    left_1 = go(spill(2, g1, p1, b1, c1), "right")
    any_space = pl.BlockSpec(memory_space=pl.ANY)
    mid, first = call(
        mid_body, [whole, (2, W, W)], [SMEM, SMEM] + [VMEM] * 9, 12, 1 << 24, 10 << 20
    )(offs, above, *base, p0, p1, b0, b1, c0, c1, left_m0)
    return call(
        final_body,
        whole,
        [any_space] + [VMEM] * 3,
        8,
        1 << 18,
        2 << 20,
        [pltpu.VMEM((2, W, W), f32), pltpu.SemaphoreType.DMA((2,))],
        any_space,
        {0: 0},
    )(mid, first, left_p0, left_1)


def solution(mesh):
    placed = (
        P(None, "tx", "ty"),
        P("mode", None, None, None),
        P("tx", "ty", None, None, None),
        P("tx", "ty", None, None),
        P("tx", "ty"),
        P(),
    )

    def body(*args):
        return local(rings(mesh), *args)

    return jax.shard_map(
        body, mesh=mesh, in_specs=placed, out_specs=P(None, "tx", "ty"), check_vma=False
    )
```

profile of v0, /device:TPU:97, one launch (start us, length us, event | category | flops | bytes accessed | tf_op | source)
XLA Modules:
  0.0 78.7 jit_solution(1160312581672782883)
XLA Ops:
  0.0 1.2 %constant_dynamic-slice_fusion = f32[1,2,256,256]{3,2,1,0:T(8,128)S(1)} fusion(f32[2,2,256,256]{3,2,1,0:T(8,128)} %probe_a.1, s32[]{:T(128)S(6)} %select_n.3), kind=kLoop, calls=%fused_computation.2 | loop fusion | bytes 1048580 | tf_op jit(solution)/shard_map/dynamic_slice | solution.py:362
  1.2 1.3 %collective-permute-start.8 = (f32[1,2,256,256]{3,2,1,0:T(8,128)S(1)}, f32[1,2,256,256]{3,2,1,0:T(8,128)S(1)}, u32[]{:S(2)}, u32[]{:S(2)}) collective-permute-start(f32[1,2,256,256]{3,2,1,0:T(8,128)S(1)} %constant_dynamic-slice_fusion), channel_id=1, source_target_pairs={{0,1},{1,0},{2,3},{3,2},{4,5},{5,4},{6,7},{7,6},{8,9},{9,8},{10,11... | collective-permute-start | bytes 1572872 | tf_op jit(solution)/shard_map/ppermute | solution.py:351
  2.5 1.0 %slice_bitcast_fusion.1 = f32[256,256]{1,0:T(8,128)S(1)} fusion(f32[2,256,1024]{2,1,0:T(8,128)} %obj.11), kind=kLoop, calls=%fused_computation.1 | loop fusion | bytes 524288 | tf_op jit(solution)/shard_map/squeeze | solution.py:359
  3.5 4.3 %collective-permute-start.1 = (f32[256,256]{1,0:T(8,128)S(1)}, f32[256,256]{1,0:T(8,128)S(1)}, u32[]{:S(2)}, u32[]{:S(2)}) collective-permute-start(f32[256,256]{1,0:T(8,128)S(1)} %slice_bitcast_fusion.1), channel_id=1, source_target_pairs={{0,15},{1,14},{2,0},{3,1},{4,2},{5,3},{6,4},{7,5},{8,7},{9,6},{10,... | collective-permute-start | bytes 786440 | tf_op jit(solution)/shard_map/ppermute | solution.py:351
  7.9 1.0 %slice_bitcast_fusion = f32[256,256]{1,0:T(8,128)S(1)} fusion(f32[2,256,1024]{2,1,0:T(8,128)} %obj.11), kind=kLoop, calls=%fused_computation | loop fusion | bytes 524288 | tf_op jit(solution)/shard_map/squeeze | solution.py:360
  8.8 0.5 collective-permute-start.3
  9.4 4.8 %collective-permute-done.8.probe_b = f32[1,2,256,256]{3,2,1,0:T(8,128)S(1)} collective-permute-done((f32[1,2,256,256]{3,2,1,0:T(8,128)S(1)}, f32[1,2,256,256]{3,2,1,0:T(8,128)S(1)}, u32[]{:S(2)}, u32[]{:S(2)}) %collective-permute-start.8) | collective-permute-done | bytes 524320 | tf_op jit(solution)/shard_map/ppermute | solution.py:351
  14.1 1.5 %collective-permute-start.9 = (f32[1,2,256,256]{3,2,1,0:T(8,128)S(1)}, f32[1,2,256,256]{3,2,1,0:T(8,128)S(1)}, u32[]{:S(2)}, u32[]{:S(2)}) collective-permute-start(f32[1,2,256,256]{3,2,1,0:T(8,128)S(1)} %collective-permute-done.8.probe_b), channel_id=1, source_target_pairs={{0,16},{1,17},{2,18},{3,19},{4,20},{5,21},{6,22},{7,23},{8,24},{9,... | collective-permute-start | bytes 1572872 | tf_op jit(solution)/shard_map/ppermute | solution.py:351
  15.7 2.8 %collective-permute-start = (s32[2,2]{1,0:T(2,128)S(1)}, s32[2,2]{1,0:T(2,128)S(1)}, u32[]{:S(2)}, u32[]{:S(2)}) collective-permute-start(s32[2,2]{1,0:T(2,128)S(1)} %bitcast.6), channel_id=1, source_target_pairs={{0,16},{1,17},{2,18},{3,19},{4,20},{5,21},{6,22},{7,23},{8,24},{9,... | collective-permute-start | bytes 56 | tf_op jit(solution)/shard_map/ppermute | solution.py:351
  18.4 0.7 collective-permute-done.above
  19.2 0.6 shard_map.137
  19.8 0.0 copy-start.2
  19.8 0.0 copy-start.5
  19.8 0.0 copy-start.6
  19.8 0.0 copy-start.7
  19.8 0.0 copy-start.8
  19.9 0.0 copy-start.9
  19.9 0.0 copy-start.10
  19.9 0.0 copy-start.11
  19.9 0.0 copy-start.12
  19.9 0.0 collective-permute-start.6
  19.9 0.6 shard_map.138
  20.6 0.1 collective-permute-start.7
  21.3 0.7 shard_map.139.meas
  22.0 5.5 %collective-permute-done.6.below_0 = f32[256,256]{1,0:T(8,128)S(1)} collective-permute-done((f32[256,256]{1,0:T(8,128)S(1)}, f32[256,256]{1,0:T(8,128)S(1)}, u32[]{:S(2)}, u32[]{:S(2)}) %collective-permute-start.6) | collective-permute-done | bytes 262176 | tf_op jit(solution)/shard_map/ppermute | solution.py:351
  27.5 2.8 %collective-permute-done.7.below_1 = f32[256,256]{1,0:T(8,128)S(1)} collective-permute-done((f32[256,256]{1,0:T(8,128)S(1)}, f32[256,256]{1,0:T(8,128)S(1)}, u32[]{:S(2)}, u32[]{:S(2)}) %collective-permute-start.7) | collective-permute-done | bytes 262176 | tf_op jit(solution)/shard_map/ppermute | solution.py:351
  30.3 7.0 %shard_map.140 = (f32[256,256]{1,0:T(8,128)S(1)}, f32[256,256]{1,0:T(8,128)S(1)}) custom-call(s32[2,2]{1,0:T(2,128)S(1)} %bitcast.7, s32[1,1]{1,0:T(1,128)S(6)} %copy.17.counts, f32[2,256,1024]{2,1,0:T(8,128)S(1)} %copy-done, f32[256,256]{1,0:T(8,128)S(1)} %collective-permute-done.1.right_0.right, f32[256,256]{1,0:T(8,128)S(1)} %collective-permute-done.3.right_1.right, ...), custom_call_target="tpu_custom_call" | custom-call | flops 5368709120 | bytes 12582912 | tf_op jit(solution)/shard_map/pallas_call | solution.py:379
  37.3 1.3 %collective-permute-start.11 = (f32[256,256]{1,0:T(8,128)S(1)}, f32[256,256]{1,0:T(8,128)S(1)}, u32[]{:S(2)}, u32[]{:S(2)}) collective-permute-start(f32[256,256]{1,0:T(8,128)S(1)} %get-tuple-element.14.own.refs_0_), channel_id=1, source_target_pairs={{0,1},{1,0},{2,3},{3,2},{4,5},{5,4},{6,7},{7,6},{8,9},{9,8},{10,11... | collective-permute-start | bytes 786440 | tf_op jit(solution)/shard_map/ppermute | solution.py:351
  38.6 0.1 collective-permute-start.12
  38.7 0.3 collective-permute-start.10
  39.0 0.3 collective-permute-start.13
  39.3 4.3 %collective-permute-done.11.own_1.refs_1_ = f32[256,256]{1,0:T(8,128)S(1)} collective-permute-done((f32[256,256]{1,0:T(8,128)S(1)}, f32[256,256]{1,0:T(8,128)S(1)}, u32[]{:S(2)}, u32[]{:S(2)}) %collective-permute-start.11) | collective-permute-done | bytes 262176 | tf_op jit(solution)/shard_map/ppermute | solution.py:351
  43.6 2.9 %collective-permute-start.15 = (f32[256,256]{1,0:T(8,128)S(1)}, f32[256,256]{1,0:T(8,128)S(1)}, u32[]{:S(2)}, u32[]{:S(2)}) collective-permute-start(f32[256,256]{1,0:T(8,128)S(1)} %collective-permute-done.11.own_1.refs_1_), channel_id=1, source_target_pairs={{0,16},{1,17},{2,18},{3,19},{4,20},{5,21},{6,22},{7,23},{8,24},{9,... | collective-permute-start | bytes 786440 | tf_op jit(solution)/shard_map/ppermute | solution.py:351
  46.4 0.7 shard_map.143
  47.1 1.4 %collective-permute-start.16 = (f32[256,256]{1,0:T(8,128)S(1)}, f32[256,256]{1,0:T(8,128)S(1)}, u32[]{:S(2)}, u32[]{:S(2)}) collective-permute-start(f32[256,256]{1,0:T(8,128)S(1)} %shard_map.143), channel_id=1, source_target_pairs={{0,2},{1,3},{2,4},{3,5},{4,6},{5,7},{6,9},{7,8},{8,10},{9,11},{10,... | collective-permute-start | bytes 786440 | tf_op jit(solution)/shard_map/ppermute | solution.py:351
  48.5 1.4 %collective-permute-start.2 = (f32[2,256,128]{2,1,0:T(8,128)S(1)}, f32[2,256,128]{2,1,0:T(8,128)S(1)}, u32[]{:S(2)}, u32[]{:S(2)}) collective-permute-start(f32[2,256,128]{2,1,0:T(8,128)S(1)} %slice.10), channel_id=1, source_target_pairs={{0,2},{1,3},{2,4},{3,5},{4,6},{5,7},{6,9},{7,8},{8,10},{9,11},{10,... | collective-permute-start | bytes 786440 | tf_op jit(solution)/shard_map/ppermute | solution.py:351
  49.9 1.4 %collective-permute-start.14 = (f32[256,256]{1,0:T(8,128)S(1)}, f32[256,256]{1,0:T(8,128)S(1)}, u32[]{:S(2)}, u32[]{:S(2)}) collective-permute-start(f32[256,256]{1,0:T(8,128)S(1)} %collective-permute-done.10.own_0), channel_id=1, source_target_pairs={{0,16},{1,17},{2,18},{3,19},{4,20},{5,21},{6,22},{7,23},{8,24},{9,... | collective-permute-start | bytes 786440 | tf_op jit(solution)/shard_map/ppermute | solution.py:351
  51.3 0.7 shard_map.145
  52.1 1.5 %collective-permute-start.18 = (f32[256,256]{1,0:T(8,128)S(1)}, f32[256,256]{1,0:T(8,128)S(1)}, u32[]{:S(2)}, u32[]{:S(2)}) collective-permute-start(f32[256,256]{1,0:T(8,128)S(1)} %shard_map.145), channel_id=1, source_target_pairs={{0,2},{1,3},{2,4},{3,5},{4,6},{5,7},{6,9},{7,8},{8,10},{9,11},{10,... | collective-permute-start | bytes 786440 | tf_op jit(solution)/shard_map/ppermute | solution.py:351
  53.6 5.3 %collective-permute-done.16.left_0 = f32[256,256]{1,0:T(8,128)S(1)} collective-permute-done((f32[256,256]{1,0:T(8,128)S(1)}, f32[256,256]{1,0:T(8,128)S(1)}, u32[]{:S(2)}, u32[]{:S(2)}) %collective-permute-start.16) | collective-permute-done | bytes 262176 | tf_op jit(solution)/shard_map/ppermute | solution.py:351
  58.9 5.6 %collective-permute-done.2.left = f32[2,256,128]{2,1,0:T(8,128)S(1)} collective-permute-done((f32[2,256,128]{2,1,0:T(8,128)S(1)}, f32[2,256,128]{2,1,0:T(8,128)S(1)}, u32[]{:S(2)}, u32[]{:S(2)}) %collective-permute-start.2) | collective-permute-done | bytes 262176 | tf_op jit(solution)/shard_map/ppermute | solution.py:351
  64.6 0.7 collective-permute-start.4
  65.3 0.9 %collective-permute-done.4.up = f32[2,8,256]{2,1,0:T(8,128)S(1)} collective-permute-done((f32[2,8,256]{2,1,0:T(8,128)S(1)}, f32[2,8,256]{2,1,0:T(8,128)S(1)}, u32[]{:S(2)}, u32[]{:S(2)}) %collective-permute-start.4) | collective-permute-done | bytes 16416 | tf_op jit(solution)/shard_map/ppermute | solution.py:351
  66.2 3.5 %collective-permute-done.5.down = f32[2,8,256]{2,1,0:T(8,128)S(1)} collective-permute-done((f32[2,8,256]{2,1,0:T(8,128)S(1)}, f32[2,8,256]{2,1,0:T(8,128)S(1)}, u32[]{:S(2)}, u32[]{:S(2)}) %collective-permute-start.5) | collective-permute-done | bytes 16416 | tf_op jit(solution)/shard_map/ppermute | solution.py:351
  69.7 2.5 %shard_map.142.base_1 = f32[256,1024]{1,0:T(8,128)S(1)} custom-call(f32[4,16]{1,0:T(4,128)S(1)} %bitcast.13, s32[2,2]{1,0:T(2,128)S(1)} %bitcast.10, f32[2,256,1024]{2,1,0:T(8,128)S(1)} %copy-done, f32[256,256]{1,0:T(8,128)S(1)} %collective-permute-done.3.right_1.right, f32[2,256,128]{2,1,0:T(8,128)S(1)} %collective-permute-done.2.left, ...), custom_call_target="tpu_custom_call" | custom-call | flops 134217728 | bytes 8388608 | tf_op jit(solution)/shard_map/pallas_call | solution.py:391
  72.3 2.5 %shard_map.141.base_0 = f32[256,1024]{1,0:T(8,128)S(1)} custom-call(f32[4,16]{1,0:T(4,128)S(1)} %bitcast.14, s32[2,2]{1,0:T(2,128)S(1)} %bitcast.11, f32[2,256,1024]{2,1,0:T(8,128)S(1)} %copy-done, f32[256,256]{1,0:T(8,128)S(1)} %collective-permute-done.1.right_0.right, f32[2,256,128]{2,1,0:T(8,128)S(1)} %collective-permute-done.2.left, ...), custom_call_target="tpu_custom_call" | custom-call | flops 134217728 | bytes 8388608 | tf_op jit(solution)/shard_map/pallas_call | solution.py:391
  74.8 2.8 %shard_map.144 = (f32[2,256,1024]{2,1,0:T(8,128)}, f32[2,256,256]{2,1,0:T(8,128)S(1)}) custom-call(s32[2,2]{1,0:T(2,128)S(1)} %bitcast.12, s32[2,2]{1,0:T(2,128)S(1)} %collective-permute-done.above, f32[256,1024]{1,0:T(8,128)S(1)} %shard_map.141.base_0, f32[256,1024]{1,0:T(8,128)S(1)} %shard_map.142.base_1, f32[256,256]{1,0:T(8,128)S(1)} %collective-permute-done.10.own_0, ...), custom_call_target="tpu_custom_call" | custom-call | flops 16777216 | bytes 10485760 | tf_op jit(solution)/shard_map/pallas_call | solution.py:407
  77.6 0.8 %shard_map.146 = f32[2,256,1024]{2,1,0:T(8,128)} custom-call(f32[2,256,1024]{2,1,0:T(8,128)} %get-tuple-element.15.mid, f32[2,256,256]{2,1,0:T(8,128)S(1)} %get-tuple-element.16.first, f32[256,256]{1,0:T(8,128)S(1)} %collective-permute-done.17.left_0, f32[256,256]{1,0:T(8,128)S(1)} %collective-permute-done.18.left_1), custom_call_target="tpu_custom_call", output_to_operand_aliasing={{}: (0, {})} | custom-call | flops 262144 | bytes 2097152 | tf_op jit(solution)/shard_map/pallas_call | solution.py:410
  (31 shorter events, 0.1 us)
Async XLA Ops:
  0.0 19.2 %copy-start = (f32[2,256,1024]{2,1,0:T(8,128)S(1)}, f32[2,256,1024]{2,1,0:T(8,128)}, u32[]{:S(2)}) copy-start(f32[2,256,1024]{2,1,0:T(8,128)} %obj.11) | copy-start | bytes 6291460
  0.0 15.7 %copy-start.3 = (s32[1,1,2,2]{3,2,1,0:T(2,128)S(1)}, s32[1,1,2,2]{3,2,1,0:T(2,128)}, u32[]{:S(2)}) copy-start(s32[1,1,2,2]{3,2,1,0:T(2,128)} %param.17) | copy-start | bytes 52
  1.2 12.9 %collective-permute-start.8 = (f32[1,2,256,256]{3,2,1,0:T(8,128)S(1)}, f32[1,2,256,256]{3,2,1,0:T(8,128)S(1)}, u32[]{:S(2)}, u32[]{:S(2)}) collective-permute-start(f32[1,2,256,256]{3,2,1,0:T(8,128)S(1)} %constant_dynamic-slice_fusion), channel_id=1, source_target_pairs={{0,1},{1,0},{2,3},{3,2},{4,5},{5,4},{6,7},{7,6},{8,9},{9,8},{10,11... | collective-permute-start | bytes 1572872 | tf_op jit(solution)/shard_map/ppermute | solution.py:351
  3.5 15.6 %collective-permute-start.1 = (f32[256,256]{1,0:T(8,128)S(1)}, f32[256,256]{1,0:T(8,128)S(1)}, u32[]{:S(2)}, u32[]{:S(2)}) collective-permute-start(f32[256,256]{1,0:T(8,128)S(1)} %slice_bitcast_fusion.1), channel_id=1, source_target_pairs={{0,15},{1,14},{2,0},{3,1},{4,2},{5,3},{6,4},{7,5},{8,7},{9,6},{10,... | collective-permute-start | bytes 786440 | tf_op jit(solution)/shard_map/ppermute | solution.py:351
  8.8 11.1 %collective-permute-start.3 = (f32[256,256]{1,0:T(8,128)S(1)}, f32[256,256]{1,0:T(8,128)S(1)}, u32[]{:S(2)}, u32[]{:S(2)}) collective-permute-start(f32[256,256]{1,0:T(8,128)S(1)} %slice_bitcast_fusion), channel_id=1, source_target_pairs={{0,15},{1,14},{2,0},{3,1},{4,2},{5,3},{6,4},{7,5},{8,7},{9,6},{10,... | collective-permute-start | bytes 786440 | tf_op jit(solution)/shard_map/ppermute | solution.py:351
  14.1 16.1 %collective-permute-start.9 = (f32[1,2,256,256]{3,2,1,0:T(8,128)S(1)}, f32[1,2,256,256]{3,2,1,0:T(8,128)S(1)}, u32[]{:S(2)}, u32[]{:S(2)}) collective-permute-start(f32[1,2,256,256]{3,2,1,0:T(8,128)S(1)} %collective-permute-done.8.probe_b), channel_id=1, source_target_pairs={{0,16},{1,17},{2,18},{3,19},{4,20},{5,21},{6,22},{7,23},{8,24},{9,... | collective-permute-start | bytes 1572872 | tf_op jit(solution)/shard_map/ppermute | solution.py:351
  15.7 5.6 %copy-start.1 = (f32[1,1,2,256,256]{4,3,2,1,0:T(8,128)S(1)}, f32[1,1,2,256,256]{4,3,2,1,0:T(8,128)}, u32[]{:S(2)}) copy-start(f32[1,1,2,256,256]{4,3,2,1,0:T(8,128)} %meas.1) | copy-start | bytes 1572868
  15.7 3.5 %collective-permute-start = (s32[2,2]{1,0:T(2,128)S(1)}, s32[2,2]{1,0:T(2,128)S(1)}, u32[]{:S(2)}, u32[]{:S(2)}) collective-permute-start(s32[2,2]{1,0:T(2,128)S(1)} %bitcast.6), channel_id=1, source_target_pairs={{0,16},{1,17},{2,18},{3,19},{4,20},{5,21},{6,22},{7,23},{8,24},{9,... | collective-permute-start | bytes 56 | tf_op jit(solution)/shard_map/ppermute | solution.py:351
  19.8 10.5 %copy-start.2 = (f32[2,2,256,256]{3,2,1,0:T(8,128)S(1)}, f32[2,2,256,256]{3,2,1,0:T(8,128)}, u32[]{:S(2)}) copy-start(f32[2,2,256,256]{3,2,1,0:T(8,128)} %probe_a.1) | copy-start | bytes 3145732
  19.8 10.5 %copy-start.5 = (bf16[256,256]{1,0:T(8,128)(2,1)S(1)}, bf16[256,256]{1,0:T(8,128)(2,1)}, u32[]{:S(2)}) copy-start(bf16[256,256]{1,0:T(8,128)(2,1)} %constant.28.clone.refs_0_) | copy-start | bytes 393220
  19.8 10.5 %copy-start.6 = (bf16[256,256]{1,0:T(8,128)(2,1)S(1)}, bf16[256,256]{1,0:T(8,128)(2,1)}, u32[]{:S(2)}) copy-start(bf16[256,256]{1,0:T(8,128)(2,1)} %constant.29.clone.refs_1_) | copy-start | bytes 393220
  19.8 10.5 %copy-start.7 = (bf16[256,256]{1,0:T(8,128)(2,1)S(1)}, bf16[256,256]{1,0:T(8,128)(2,1)}, u32[]{:S(2)}) copy-start(bf16[256,256]{1,0:T(8,128)(2,1)} %constant.30.clone.refs_2_) | copy-start | bytes 393220
  19.8 10.5 %copy-start.8 = (bf16[256,256]{1,0:T(8,128)(2,1)S(1)}, bf16[256,256]{1,0:T(8,128)(2,1)}, u32[]{:S(2)}) copy-start(bf16[256,256]{1,0:T(8,128)(2,1)} %constant.31.clone.refs_3_) | copy-start | bytes 393220
  19.9 10.5 %copy-start.9 = (bf16[256,256]{1,0:T(8,128)(2,1)S(1)}, bf16[256,256]{1,0:T(8,128)(2,1)}, u32[]{:S(2)}) copy-start(bf16[256,256]{1,0:T(8,128)(2,1)} %constant.32.clone.refs_4_) | copy-start | bytes 393220
  19.9 10.5 %copy-start.10 = (bf16[256,256]{1,0:T(8,128)(2,1)S(1)}, bf16[256,256]{1,0:T(8,128)(2,1)}, u32[]{:S(2)}) copy-start(bf16[256,256]{1,0:T(8,128)(2,1)} %constant.33.clone.refs_5_) | copy-start | bytes 393220
  19.9 10.5 %copy-start.11 = (bf16[256,256]{1,0:T(8,128)(2,1)S(1)}, bf16[256,256]{1,0:T(8,128)(2,1)}, u32[]{:S(2)}) copy-start(bf16[256,256]{1,0:T(8,128)(2,1)} %constant.34.clone.refs_6_) | copy-start | bytes 393220
  19.9 10.4 %copy-start.12 = (bf16[256,256]{1,0:T(8,128)(2,1)S(1)}, bf16[256,256]{1,0:T(8,128)(2,1)}, u32[]{:S(2)}) copy-start(bf16[256,256]{1,0:T(8,128)(2,1)} %constant.35.clone.refs_7_) | copy-start | bytes 393220
  19.9 7.6 %collective-permute-start.6 = (f32[256,256]{1,0:T(8,128)S(1)}, f32[256,256]{1,0:T(8,128)S(1)}, u32[]{:S(2)}, u32[]{:S(2)}) collective-permute-start(f32[256,256]{1,0:T(8,128)S(1)} %shard_map.137), channel_id=1, source_target_pairs={{0,240},{1,241},{2,242},{3,243},{4,244},{5,245},{6,246},{7,247},{8... | collective-permute-start | bytes 786440 | tf_op jit(solution)/shard_map/ppermute | solution.py:351
  20.6 9.7 %collective-permute-start.7 = (f32[256,256]{1,0:T(8,128)S(1)}, f32[256,256]{1,0:T(8,128)S(1)}, u32[]{:S(2)}, u32[]{:S(2)}) collective-permute-start(f32[256,256]{1,0:T(8,128)S(1)} %shard_map.138), channel_id=1, source_target_pairs={{0,240},{1,241},{2,242},{3,243},{4,244},{5,245},{6,246},{7,247},{8... | collective-permute-start | bytes 786440 | tf_op jit(solution)/shard_map/ppermute | solution.py:351
  37.3 6.2 %collective-permute-start.11 = (f32[256,256]{1,0:T(8,128)S(1)}, f32[256,256]{1,0:T(8,128)S(1)}, u32[]{:S(2)}, u32[]{:S(2)}) collective-permute-start(f32[256,256]{1,0:T(8,128)S(1)} %get-tuple-element.14.own.refs_0_), channel_id=1, source_target_pairs={{0,1},{1,0},{2,3},{3,2},{4,5},{5,4},{6,7},{7,6},{8,9},{9,8},{10,11... | collective-permute-start | bytes 786440 | tf_op jit(solution)/shard_map/ppermute | solution.py:351
  38.6 7.8 %collective-permute-start.12 = (f32[256,256]{1,0:T(8,128)S(1)}, f32[256,256]{1,0:T(8,128)S(1)}, u32[]{:S(2)}, u32[]{:S(2)}) collective-permute-start(f32[256,256]{1,0:T(8,128)S(1)} %get-tuple-element.13.own.refs_0_), channel_id=1, source_target_pairs={{0,16},{1,17},{2,18},{3,19},{4,20},{5,21},{6,22},{7,23},{8,24},{9,... | collective-permute-start | bytes 786440 | tf_op jit(solution)/shard_map/ppermute | solution.py:351
  38.7 11.2 %collective-permute-start.10 = (f32[256,256]{1,0:T(8,128)S(1)}, f32[256,256]{1,0:T(8,128)S(1)}, u32[]{:S(2)}, u32[]{:S(2)}) collective-permute-start(f32[256,256]{1,0:T(8,128)S(1)} %get-tuple-element.13.own.refs_0_), channel_id=1, source_target_pairs={{0,1},{1,0},{2,3},{3,2},{4,5},{5,4},{6,7},{7,6},{8,9},{9,8},{10,11... | collective-permute-start | bytes 786440 | tf_op jit(solution)/shard_map/ppermute | solution.py:351
  39.0 12.3 %collective-permute-start.13 = (f32[256,256]{1,0:T(8,128)S(1)}, f32[256,256]{1,0:T(8,128)S(1)}, u32[]{:S(2)}, u32[]{:S(2)}) collective-permute-start(f32[256,256]{1,0:T(8,128)S(1)} %get-tuple-element.14.own.refs_0_), channel_id=1, source_target_pairs={{0,16},{1,17},{2,18},{3,19},{4,20},{5,21},{6,22},{7,23},{8,24},{9,... | collective-permute-start | bytes 786440 | tf_op jit(solution)/shard_map/ppermute | solution.py:351
  43.6 7.8 %collective-permute-start.15 = (f32[256,256]{1,0:T(8,128)S(1)}, f32[256,256]{1,0:T(8,128)S(1)}, u32[]{:S(2)}, u32[]{:S(2)}) collective-permute-start(f32[256,256]{1,0:T(8,128)S(1)} %collective-permute-done.11.own_1.refs_1_), channel_id=1, source_target_pairs={{0,16},{1,17},{2,18},{3,19},{4,20},{5,21},{6,22},{7,23},{8,24},{9,... | collective-permute-start | bytes 786440 | tf_op jit(solution)/shard_map/ppermute | solution.py:351
  47.1 11.8 %collective-permute-start.16 = (f32[256,256]{1,0:T(8,128)S(1)}, f32[256,256]{1,0:T(8,128)S(1)}, u32[]{:S(2)}, u32[]{:S(2)}) collective-permute-start(f32[256,256]{1,0:T(8,128)S(1)} %shard_map.143), channel_id=1, source_target_pairs={{0,2},{1,3},{2,4},{3,5},{4,6},{5,7},{6,9},{7,8},{8,10},{9,11},{10,... | collective-permute-start | bytes 786440 | tf_op jit(solution)/shard_map/ppermute | solution.py:351
  48.5 21.2 %copy-start.4 = (f32[16,4]{0,1:T(4,128)S(1)}, f32[16,4]{0,1:T(4,128)}, u32[]{:S(2)}) copy-start(f32[16,4]{0,1:T(4,128)} %param.19) | copy-start | bytes 772
  48.5 16.0 %collective-permute-start.2 = (f32[2,256,128]{2,1,0:T(8,128)S(1)}, f32[2,256,128]{2,1,0:T(8,128)S(1)}, u32[]{:S(2)}, u32[]{:S(2)}) collective-permute-start(f32[2,256,128]{2,1,0:T(8,128)S(1)} %slice.10), channel_id=1, source_target_pairs={{0,2},{1,3},{2,4},{3,5},{4,6},{5,7},{6,9},{7,8},{8,10},{9,11},{10,... | collective-permute-start | bytes 786440 | tf_op jit(solution)/shard_map/ppermute | solution.py:351
  49.9 24.9 %collective-permute-start.14 = (f32[256,256]{1,0:T(8,128)S(1)}, f32[256,256]{1,0:T(8,128)S(1)}, u32[]{:S(2)}, u32[]{:S(2)}) collective-permute-start(f32[256,256]{1,0:T(8,128)S(1)} %collective-permute-done.10.own_0), channel_id=1, source_target_pairs={{0,16},{1,17},{2,18},{3,19},{4,20},{5,21},{6,22},{7,23},{8,24},{9,... | collective-permute-start | bytes 786440 | tf_op jit(solution)/shard_map/ppermute | solution.py:351
  52.1 25.6 %collective-permute-start.18 = (f32[256,256]{1,0:T(8,128)S(1)}, f32[256,256]{1,0:T(8,128)S(1)}, u32[]{:S(2)}, u32[]{:S(2)}) collective-permute-start(f32[256,256]{1,0:T(8,128)S(1)} %shard_map.145), channel_id=1, source_target_pairs={{0,2},{1,3},{2,4},{3,5},{4,6},{5,7},{6,9},{7,8},{8,10},{9,11},{10,... | collective-permute-start | bytes 786440 | tf_op jit(solution)/shard_map/ppermute | solution.py:351
  58.9 18.7 %collective-permute-start.17 = (f32[256,256]{1,0:T(8,128)S(1)}, f32[256,256]{1,0:T(8,128)S(1)}, u32[]{:S(2)}, u32[]{:S(2)}) collective-permute-start(f32[256,256]{1,0:T(8,128)S(1)} %collective-permute-done.16.left_0), channel_id=1, source_target_pairs={{0,1},{1,0},{2,3},{3,2},{4,5},{5,4},{6,7},{7,6},{8,9},{9,8},{10,11... | collective-permute-start | bytes 786440 | tf_op jit(solution)/shard_map/ppermute | solution.py:351
  64.6 1.6 %collective-permute-start.4 = (f32[2,8,256]{2,1,0:T(8,128)S(1)}, f32[2,8,256]{2,1,0:T(8,128)S(1)}, u32[]{:S(2)}, u32[]{:S(2)}) collective-permute-start(f32[2,8,256]{2,1,0:T(8,128)S(1)} %get-tuple-element.11), channel_id=1, source_target_pairs={{0,16},{1,17},{2,18},{3,19},{4,20},{5,21},{6,22},{7,23},{8,24},{9,... | collective-permute-start | bytes 49160 | tf_op jit(solution)/shard_map/ppermute | solution.py:351
  65.3 4.4 %collective-permute-start.5 = (f32[2,8,256]{2,1,0:T(8,128)S(1)}, f32[2,8,256]{2,1,0:T(8,128)S(1)}, u32[]{:S(2)}, u32[]{:S(2)}) collective-permute-start(f32[2,8,256]{2,1,0:T(8,128)S(1)} %get-tuple-element.12), channel_id=1, source_target_pairs={{0,240},{1,241},{2,242},{3,243},{4,244},{5,245},{6,246},{7,247},{8... | collective-permute-start | bytes 49160 | tf_op jit(solution)/shard_map/ppermute | solution.py:351
where the time goes:
time: 78.8 us; the launch traced here: 78.7 us
  waiting for transfers between devices  33.4 us (42%)
  starting transfers between devices  21.8 us (28%)
  Pallas kernels  19.1 us (24%)
  local copies, waits for them, and re-layouts  3.29 us (4%)
  between operations  1.07 us (1%)
    ppermute x19, waiting for transfers between devices, go(): return lax.ppermute(value, axes, ring[where])  33.4 us
    ppermute x19, starting transfers between devices, go(): return lax.ppermute(value, axes, ring[where])  21.8 us
    pallas_call x1, Pallas kernels, local(): call(main_body, [piece] * 2, [SMEM, SMEM] + [VMEM] * 17, 16, 5 << 30, 12...  6.99 us
    pallas_call x2, Pallas kernels, local(): call(functools.partial(prior_body, c), (rows, cols), [SMEM, SMEM] + [VMEM...  5.1 us
    pallas_call x1, Pallas kernels, local(): call(mid_body, [whole, (2, W, W)], [SMEM, SMEM] + [VMEM] * 9, 12, 1 << 24...  2.8 us
  transfers between devices with their start and end apart: 19, of which 9 were waited for; matrix products, arithmetic and copies ran while one was open for 3% of the time, Pallas kernels for 14%

commit v1 on v0

--- a/solution.py
+++ b/solution.py
@@ -137,30 +137,33 @@
     return table[slot, 0], col0 // W, lax.rem(col0, W)
 
 
-def rim_rows(obj, c, row, right, left):
+def rim_rows(out, at, obj, c, row, right, left):
     last = lax.axis_index("ty") == lax.axis_size("ty") - 1
     first = lax.axis_index("ty") == 0
-    edge = jnp.where(first, 0.0, left[c, row : row + 1, :])
-    parts = [obj[c, row : row + 1, k * W : (k + 1) * W] for k in range(4)]
-    parts.append(jnp.where(last, 0.0, right[row : row + 1, :]))
-    parts.append(jnp.concatenate([edge, edge], axis=1))
-    return parts
-
-
-def send_body(c, above, obj, right, out):
+    for k in range(4):
+        out[at + k : at + k + 1, :] = obj[c, row : row + 1, k * W : (k + 1) * W]
+    out[at + 4 : at + 5, :] = jnp.where(last, 0.0, right[row : row + 1, :])
+    out[at + 5 : at + 6, :] = jnp.where(first, 0.0, left[c : c + 1, :])
+    out[at + 6 : at + 8, :] = jnp.zeros((2, W), f32)
+
+
+def edge_body(obj, out):
+    cols = obj.shape[2]
+    for c in range(2):
+        out[c : c + 1, :] = obj[c, :, cols - 128 : cols].T[127:128, :]
+    out[2:8, :] = jnp.zeros((6, W), f32)
+
+
+def send_body(c, above, obj, *refs):
     _, q, s = place(above, lax.axis_index("mode"))
-    out[...] = window(obj, c, right, q, s)
-
-
-def rim_body(obj, left, right_0, right_1, up_out, down_out):
-    for c, right in enumerate((right_0, right_1)):
-        for row, out in ((0, up_out), (W - 1, down_out)):
-            for k, part in enumerate(rim_rows(obj, c, row, right, left)):
-                out[c, k : k + 1, :] = part
-            out[c, 6:8, :] = jnp.zeros((2, W), f32)
-
-
-def main_body(offs, counts, obj, right_0, right_1, below_0, below_1, probe_a, probe_b, probe_c, meas, *refs):
+    out = refs[-1]
+    out[0:W, :] = window(obj, c, refs[c], q, s)
+    if c == 1:
+        for d in range(2):
+            rim_rows(out, W + 8 * d, obj, d, 0, refs[d], refs[2])
+
+
+def main_body(offs, counts, obj, left, right_0, right_1, below_0, below_1, probe_a, probe_b, probe_c, meas, *refs):
     mats, (grad_0, grad_1, wave) = refs[:8], refs[8:]
     m = lax.axis_index("mode")
     last_tx = lax.axis_index("tx") == lax.axis_size("tx") - 1
@@ -169,7 +172,7 @@
     lane, row = iota(1), iota(0)
     patch = []
     for c, right, below in ((0, right_0, below_0), (1, right_1, below_1)):
-        low = jnp.where(last_tx, 0.0, below[...])
+        low = jnp.where(last_tx, 0.0, below[0:W, :])
         rolled = jnp.where(row >= row0, window(obj, c, right, q, s), low)
         rolled = pltpu.roll(rolled, lax.rem(W - row0, W), 0)
         patch.append(pltpu.roll(rolled, lax.rem(W - s, W), 1))
@@ -192,8 +195,9 @@
         br, bi = backward(resid * wave[k, 0], resid * wave[k, 1], *tabs)
         grad[0] = grad[0] + pr * br + pi * bi
         grad[1] = grad[1] + pr * bi - pi * br
-    for g, out in ((grad[0], grad_0), (grad[1], grad_1)):
-        out[...] = pltpu.roll(pltpu.roll(g * live, row0, 0), s, 1)
+    for c, right, out in ((0, right_0, grad_0), (1, right_1, grad_1)):
+        out[0:W, :] = pltpu.roll(pltpu.roll(grad[c] * live, row0, 0), s, 1)
+        rim_rows(out, W, obj, c, W - 1, right, left)
 
 
 def sort_body(meas, out):
@@ -224,17 +228,17 @@
     total = jnp.zeros((W, W), f32)
     for k, slot in enumerate((m, 1 - m)[:n]):
         row0, q, s = place(offs, slot)
-        total = total + jnp.where((q == 3) & (lane < s) & (row >= row0), refs[k][...], 0.0)
+        total = total + jnp.where((q == 3) & (lane < s) & (row >= row0), refs[k][0:W, :], 0.0)
         row0, q, s = place(above, slot)
         keep = (q == 3) & (lane < s) & (row < row0) & (tx > 0)
-        total = total + jnp.where(keep, refs[n + k][...], 0.0)
+        total = total + jnp.where(keep, refs[n + k][0:W, :], 0.0)
     refs[2 * n][...] = total
 
 
 def take(out, ref, spot, rows):
     _, q, s = spot
     lane = iota(1)
-    value = ref[...]
+    value = ref[0:W, :]
     here = pl.ds(pl.multiple_of(q * W, W), W)
     out[:, here] = out[:, here] - step_size * jnp.where(rows & (lane >= s), value, 0.0)
     nxt = pl.ds(pl.multiple_of(jnp.minimum(q + 1, 3) * W, W), W)
@@ -242,7 +246,7 @@
     out[:, nxt] = out[:, nxt] - step_size * jnp.where(keep, value, 0.0)
 
 
-def prior_body(c, filt, offs, obj, right, left, up, down, own, out):
+def prior_body(c, filt, offs, above, obj, right, left, up, down, own, out):
     tx, ty = lax.axis_index("tx"), lax.axis_index("ty")
     n_tx, n_ty = lax.axis_size("tx"), lax.axis_size("ty")
     cols = obj.shape[2]
@@ -260,18 +264,19 @@
     spot = place(offs, lax.axis_index("mode"))
     x = obj[c]
     after = jnp.where(ty == n_ty - 1, 0.0, right[:, 0:1])
-    before = jnp.where(ty == 0, 0.0, left[c, :, 127:128])
-
-    def line(rim, flag):
+    edge = jnp.broadcast_to(left[c : c + 1, :], (128, W)).T
+    before = jnp.where(ty == 0, 0.0, edge[:, 0:1])
+
+    def line(rim, flag, at):
         rim = jnp.where(flag, 0.0, rim)
         whole = jnp.concatenate([rim[k : k + 1, :] for k in range(4)], axis=1)
-        return whole, rim[5:6, W - 1 : W], rim[4:5, 0:1]
-
-    u_mid, u_left, u_right = line(up[c], tx == 0)
-    d_mid, d_left, d_right = line(down[c], tx == n_tx - 1)
+        return whole, rim[5:6, at : at + 1], rim[4:5, 0:1]
+
+    u_mid, u_left, u_right = line(up[W : W + 8, :], tx == 0, W - 1)
+    d_mid, d_left, d_right = line(down[W + 8 * c : W + 8 * c + 8, :], tx == n_tx - 1, 0)
     xl, xr = beside(x, before, after)
 
-    def above(mid, edge):
+    def over(mid, edge):
         return jnp.where(row == 0, edge, pltpu.roll(mid, 1, 0))
 
     def under(mid, edge):
@@ -286,8 +291,8 @@
 
     ul, ur = shift_line(u_mid, u_left, u_right)
     dl, dr = shift_line(d_mid, d_left, d_right)
-    xu, xd = above(x, u_mid), under(x, d_mid)
-    xul, xur = above(xl, ul), above(xr, ur)
+    xu, xd = over(x, u_mid), under(x, d_mid)
+    xul, xur = over(xl, ul), over(xr, ur)
     xdl, xdr = under(xl, dl), under(xr, dr)
     in_col = (lane > 0) | (ty > 0)
     in_row = (row > 0) | (tx > 0)
@@ -299,26 +304,25 @@
     )
     out[...] = x - step_size * total
     take(out, own, spot, iota(0) >= spot[0])
-
-
-def mid_body(offs, above, base_0, base_1, own_0, own_1, up_m0, up_m1, up_p0, up_p1, left_0, out, first):
-    m = lax.axis_index("mode")
-    tx, ty = lax.axis_index("tx"), lax.axis_index("ty")
+    spot = place(above, lax.axis_index("mode"))
+    take(out, up, spot, (iota(0) < spot[0]) & (tx > 0))
+
+
+def fold_body(offs, above, base, own_p, up_p, out):
+    slot = 1 - lax.axis_index("mode")
     row = iota(0)
-    mine, from_m, from_p = place(offs, 1 - m), place(above, m), place(above, 1 - m)
-    for c, base, own_p, up_m, up_p in (
-        (0, base_0, own_0, up_m0, up_p0),
-        (1, base_1, own_1, up_m1, up_p1),
-    ):
-        part = out.at[c]
-        part[...] = base[...]
-        take(part, own_p, mine, row >= mine[0])
-        take(part, up_m, from_m, (row < from_m[0]) & (tx > 0))
-        take(part, up_p, from_p, (row < from_p[0]) & (tx > 0))
-        value = part[:, 0:W]
-        if c == 0:
-            value = value - step_size * jnp.where(ty > 0, left_0[...], 0.0)
-        first[c] = value
+    mine, over = place(offs, slot), place(above, slot)
+    out[...] = base[...]
+    take(out, own_p, mine, row >= mine[0])
+    take(out, up_p, over, (row < over[0]) & (lax.axis_index("tx") > 0))
+
+
+def mid_body(offs, above, base, own_p, up_p, left_0, done, out, first):
+    part = out.at[0]
+    fold_body(offs, above, base, own_p, up_p, part)
+    first[0] = part[:, 0:W] - step_size * jnp.where(lax.axis_index("ty") > 0, left_0[...], 0.0)
+    out[1] = done[...]
+    first[1] = done[:, 0:W]
 
 
 def final_body(mid, first, left_0, left_1, out, buf, sems):
@@ -362,36 +366,34 @@
     probe_b = go(lax.dynamic_slice_in_dim(probe, core, 1, 0), "swap")
     probe_c = go(probe_b, "core")
     above = go(offs, "down")
-    left = go(obj[:, :, cols - 128 :], "right")
+    edge = call(edge_body, (8, W), [VMEM], 8, 1 << 16, 1 << 18)(obj)
+    left = go(edge, "right")
     filt = filters.T
     meas = call(sort_body, piece, [VMEM], 8, 1 << 26, 3 << 18)(intensity)
-    below = [
-        go(
-            call(functools.partial(send_body, c), piece, [SMEM] + [VMEM] * 2, 8, 1 << 20, 2 << 20)(
-                above, obj, right[c]
-            ),
-            "up",
-        )
-        for c in (0, 1)
-    ]
-    rims = call(rim_body, [(2, 8, W)] * 2, [VMEM] * 4, 8, 1 << 16, 2 << 20)(obj, left, *right)
-    under, over = go(rims[0], "up"), go(rims[1], "down")
+    up_0 = call(
+        functools.partial(send_body, 0), piece, [SMEM] + [VMEM] * 2, 8, 1 << 20, 2 << 20
+    )(above, obj, right[0])
+    below_0 = go(up_0, "up")
+    up_1 = call(
+        functools.partial(send_body, 1), (W + 16, W), [SMEM] + [VMEM] * 4, 8, 1 << 20, 2 << 20
+    )(above, obj, *right, left)
+    below_1 = go(up_1, "up")
     g0, g1 = call(
         main_body,
-        [piece] * 2,
-        [SMEM, SMEM] + [VMEM] * 17,
+        [(W + 8, W)] * 2,
+        [SMEM, SMEM] + [VMEM] * 18,
         16,
         5 << 30,
         12 << 20,
         [pltpu.VMEM((4, 2, W, W), f32)],
-    )(offs, counts, obj, *right, *below, probe, probe_b, probe_c, meas, *tabs)
+    )(offs, counts, obj, left, *right, below_0, below_1, probe, probe_b, probe_c, meas, *tabs)
     p1, b0 = go(g1, "swap"), go(g0, "down")
     p0, b1 = go(g0, "swap"), go(g1, "down")
     base = [
         call(
-            functools.partial(prior_body, c), (rows, cols), [SMEM, SMEM] + [VMEM] * 6, 12, 1 << 27, 8 << 20
-        )(filt, offs, obj, right[c], left, over, under, g)
-        for c, g in ((0, g0), (1, g1))
+            functools.partial(prior_body, c), (rows, cols), [SMEM] * 3 + [VMEM] * 6, 12, 1 << 27, 8 << 20
+        )(filt, offs, above, obj, right[c], left, b, below_1, g)
+        for c, g, b in ((0, g0, b0), (1, g1, b1))
     ]
     c1, c0 = go(p1, "down"), go(p0, "down")
 
@@ -404,9 +406,12 @@
     left_p0 = go(left_m0, "swap")
     left_1 = go(spill(2, g1, p1, b1, c1), "right")
     any_space = pl.BlockSpec(memory_space=pl.ANY)
+    fold = call(fold_body, (rows, cols), [SMEM, SMEM] + [VMEM] * 3, 8, 1 << 20, 4 << 20)(
+        offs, above, base[1], p1, c1
+    )
     mid, first = call(
-        mid_body, [whole, (2, W, W)], [SMEM, SMEM] + [VMEM] * 9, 12, 1 << 24, 10 << 20
-    )(offs, above, *base, p0, p1, b0, b1, c0, c1, left_m0)
+        mid_body, [whole, (2, W, W)], [SMEM, SMEM] + [VMEM] * 5, 12, 1 << 24, 10 << 20
+    )(offs, above, base[0], p0, c0, left_m0, fold)
     return call(
         final_body,
         whole,

time: 78.8 us -> 74.8 us (0.949)
  the two profiles are of different devices: /device:TPU:97 before, /device:TPU:120 now
where the time goes in v1:
time: 74.8 us; the launch traced here: 74.7 us
  starting transfers between devices  27.8 us (37%)
  waiting for transfers between devices  22.4 us (30%)
  Pallas kernels  20.1 us (27%)
  local copies, waits for them, and re-layouts  3.24 us (4%)
  between operations  1.07 us (1%)
    ppermute x17, starting transfers between devices, go(): return lax.ppermute(value, axes, ring[where])  27.8 us
    ppermute x17, waiting for transfers between devices, go(): return lax.ppermute(value, axes, ring[where])  22.4 us
    pallas_call x1, Pallas kernels, local(): call(main_body, [(W + 8, W)] * 2, [SMEM, SMEM] + [VMEM] * 18, 16, 5 << 30...  6.99 us
    pallas_call x2, Pallas kernels, local(): call(functools.partial(prior_body, c), (rows, cols), [SMEM] * 3 + [VMEM]...  5.56 us
    pallas_call x1, Pallas kernels, local(): call(mid_body, [whole, (2, W, W)], [SMEM, SMEM] + [VMEM] * 5, 12, 1 << 24...  2.35 us
  transfers between devices with their start and end apart: 17, of which 5 were waited for; matrix products, arithmetic and copies ran while one was open for 3% of the time, Pallas kernels for 16%

profile of v1, /device:TPU:120, one launch (start us, length us, event | category | flops | bytes accessed | tf_op | source)
XLA Modules:
  0.0 74.7 jit_solution(3299797442018477311)
XLA Ops:
  0.0 1.2 %constant_dynamic-slice_fusion = f32[1,2,256,256]{3,2,1,0:T(8,128)S(1)} fusion(f32[2,2,256,256]{3,2,1,0:T(8,128)} %probe_a.1, s32[]{:T(128)S(6)} %select_n.3), kind=kLoop, calls=%fused_computation.2 | loop fusion | bytes 1048580 | tf_op jit(solution)/shard_map/dynamic_slice | solution.py:366
  1.2 1.6 %collective-permute-start.6 = (f32[1,2,256,256]{3,2,1,0:T(8,128)S(1)}, f32[1,2,256,256]{3,2,1,0:T(8,128)S(1)}, u32[]{:S(2)}, u32[]{:S(2)}) collective-permute-start(f32[1,2,256,256]{3,2,1,0:T(8,128)S(1)} %constant_dynamic-slice_fusion), channel_id=1, source_target_pairs={{0,1},{1,0},{2,3},{3,2},{4,5},{5,4},{6,7},{7,6},{8,9},{9,8},{10,11... | collective-permute-start | bytes 1572872 | tf_op jit(solution)/shard_map/ppermute | solution.py:355
  2.8 1.0 %slice_bitcast_fusion.1 = f32[256,256]{1,0:T(8,128)S(1)} fusion(f32[2,256,1024]{2,1,0:T(8,128)} %obj.11), kind=kLoop, calls=%fused_computation.1 | loop fusion | bytes 524288 | tf_op jit(solution)/shard_map/squeeze | solution.py:363
  3.8 0.8 %collective-permute-start.1 = (f32[256,256]{1,0:T(8,128)S(1)}, f32[256,256]{1,0:T(8,128)S(1)}, u32[]{:S(2)}, u32[]{:S(2)}) collective-permute-start(f32[256,256]{1,0:T(8,128)S(1)} %slice_bitcast_fusion.1), channel_id=1, source_target_pairs={{0,15},{1,14},{2,0},{3,1},{4,2},{5,3},{6,4},{7,5},{8,7},{9,6},{10,... | collective-permute-start | bytes 786440 | tf_op jit(solution)/shard_map/ppermute | solution.py:355
  4.6 1.0 %slice_bitcast_fusion = f32[256,256]{1,0:T(8,128)S(1)} fusion(f32[2,256,1024]{2,1,0:T(8,128)} %obj.11), kind=kLoop, calls=%fused_computation | loop fusion | bytes 524288 | tf_op jit(solution)/shard_map/squeeze | solution.py:364
  5.6 0.5 collective-permute-start.3
  6.1 8.9 %collective-permute-done.6.probe_b = f32[1,2,256,256]{3,2,1,0:T(8,128)S(1)} collective-permute-done((f32[1,2,256,256]{3,2,1,0:T(8,128)S(1)}, f32[1,2,256,256]{3,2,1,0:T(8,128)S(1)}, u32[]{:S(2)}, u32[]{:S(2)}) %collective-permute-start.6) | collective-permute-done | bytes 524320 | tf_op jit(solution)/shard_map/ppermute | solution.py:355
  15.0 0.0 collective-permute-start.7
  15.0 0.1 shard_map.136
  15.1 2.5 %collective-permute-start.2 = (f32[8,256]{1,0:T(8,128)S(1)}, f32[8,256]{1,0:T(8,128)S(1)}, u32[]{:S(2)}, u32[]{:S(2)}) collective-permute-start(f32[8,256]{1,0:T(8,128)S(1)} %shard_map.136), channel_id=1, source_target_pairs={{0,2},{1,3},{2,4},{3,5},{4,6},{5,7},{6,9},{7,8},{8,10},{9,11},{10,... | collective-permute-start | bytes 24584 | tf_op jit(solution)/shard_map/ppermute | solution.py:355
  17.6 0.2 collective-permute-start
  17.9 2.8 %collective-permute-done.above = s32[2,2]{1,0:T(2,128)S(1)} collective-permute-done((s32[2,2]{1,0:T(2,128)S(1)}, s32[2,2]{1,0:T(2,128)S(1)}, u32[]{:S(2)}, u32[]{:S(2)}) %collective-permute-start) | collective-permute-done | bytes 48 | tf_op jit(solution)/shard_map/ppermute | solution.py:355
  20.6 0.0 collective-permute-done.3.refs_1_.right_1.right
  20.6 0.6 shard_map.138
  21.3 0.0 copy-start.2
  21.3 0.0 copy-start.5
  21.3 0.0 copy-start.6
  21.3 0.0 copy-start.7
  21.3 0.0 copy-start.8
  21.3 0.0 copy-start.9
  21.3 0.0 copy-start.10
  21.4 0.0 copy-start.11
  21.4 0.0 copy-start.12
  21.4 0.0 collective-permute-start.5
  21.4 0.6 shard_map.137
  22.0 0.2 collective-permute-start.4
  22.9 0.7 shard_map.139.meas
  23.6 4.7 %collective-permute-done.4.below_0 = f32[256,256]{1,0:T(8,128)S(1)} collective-permute-done((f32[256,256]{1,0:T(8,128)S(1)}, f32[256,256]{1,0:T(8,128)S(1)}, u32[]{:S(2)}, u32[]{:S(2)}) %collective-permute-start.4) | collective-permute-done | bytes 262176 | tf_op jit(solution)/shard_map/ppermute | solution.py:355
  28.3 0.0 collective-permute-done.5.below_1.down
  28.4 7.0 %shard_map.140 = (f32[264,256]{1,0:T(8,128)S(1)}, f32[264,256]{1,0:T(8,128)S(1)}) custom-call(s32[2,2]{1,0:T(2,128)S(1)} %bitcast.7, s32[1,1]{1,0:T(1,128)S(6)} %copy.17.counts, f32[2,256,1024]{2,1,0:T(8,128)S(1)} %copy-done, f32[8,256]{1,0:T(8,128)S(1)} %collective-permute-done.2.refs_2_.left, f32[256,256]{1,0:T(8,128)S(1)} %collective-permute-done.1.refs_0_.right_0.right, ...), custom_call_target="tpu_custom_call" | custom-call | flops 5368709120 | bytes 12582912 | tf_op jit(solution)/shard_map/pallas_call | solution.py:381
  35.4 0.0 copy-start.4
  35.4 0.3 collective-permute-start.13
  35.7 4.4 %collective-permute-start.8 = (f32[264,256]{1,0:T(8,128)S(1)}, f32[264,256]{1,0:T(8,128)S(1)}, u32[]{:S(2)}, u32[]{:S(2)}) collective-permute-start(f32[264,256]{1,0:T(8,128)S(1)} %get-tuple-element.9.own.refs_0_), channel_id=1, source_target_pairs={{0,16},{1,17},{2,18},{3,19},{4,20},{5,21},{6,22},{7,23},{8,24},{9,... | collective-permute-start | bytes 811016 | tf_op jit(solution)/shard_map/ppermute | solution.py:355
  40.1 1.7 %collective-permute-start.9 = (f32[264,256]{1,0:T(8,128)S(1)}, f32[264,256]{1,0:T(8,128)S(1)}, u32[]{:S(2)}, u32[]{:S(2)}) collective-permute-start(f32[264,256]{1,0:T(8,128)S(1)} %get-tuple-element.9.own.refs_0_), channel_id=1, source_target_pairs={{0,1},{1,0},{2,3},{3,2},{4,5},{5,4},{6,7},{7,6},{8,9},{9,8},{10,11... | collective-permute-start | bytes 811016 | tf_op jit(solution)/shard_map/ppermute | solution.py:355
  41.8 0.1 collective-permute-done.13.own_p.refs_1_
  41.9 5.7 %collective-permute-start.14 = (f32[264,256]{1,0:T(8,128)S(1)}, f32[264,256]{1,0:T(8,128)S(1)}, u32[]{:S(2)}, u32[]{:S(2)}) collective-permute-start(f32[264,256]{1,0:T(8,128)S(1)} %collective-permute-done.13.own_p.refs_1_), channel_id=1, source_target_pairs={{0,16},{1,17},{2,18},{3,19},{4,20},{5,21},{6,22},{7,23},{8,24},{9,... | collective-permute-start | bytes 811016 | tf_op jit(solution)/shard_map/ppermute | solution.py:355
  47.6 0.6 shard_map.142
  48.2 3.7 %collective-permute-start.11 = (f32[256,256]{1,0:T(8,128)S(1)}, f32[256,256]{1,0:T(8,128)S(1)}, u32[]{:S(2)}, u32[]{:S(2)}) collective-permute-start(f32[256,256]{1,0:T(8,128)S(1)} %shard_map.142), channel_id=1, source_target_pairs={{0,2},{1,3},{2,4},{3,5},{4,6},{5,7},{6,9},{7,8},{8,10},{9,11},{10,... | collective-permute-start | bytes 786440 | tf_op jit(solution)/shard_map/ppermute | solution.py:355
  52.0 0.2 collective-permute-start.10
  52.2 6.0 %collective-permute-done.11.left_0 = f32[256,256]{1,0:T(8,128)S(1)} collective-permute-done((f32[256,256]{1,0:T(8,128)S(1)}, f32[256,256]{1,0:T(8,128)S(1)}, u32[]{:S(2)}, u32[]{:S(2)}) %collective-permute-start.11) | collective-permute-done | bytes 262176 | tf_op jit(solution)/shard_map/ppermute | solution.py:355
  58.2 0.0 collective-permute-start.15
  58.2 0.7 shard_map.146
  58.9 5.9 %collective-permute-start.16 = (f32[256,256]{1,0:T(8,128)S(1)}, f32[256,256]{1,0:T(8,128)S(1)}, u32[]{:S(2)}, u32[]{:S(2)}) collective-permute-start(f32[256,256]{1,0:T(8,128)S(1)} %shard_map.146), channel_id=1, source_target_pairs={{0,2},{1,3},{2,4},{3,5},{4,6},{5,7},{6,9},{7,8},{8,10},{9,11},{10,... | collective-permute-start | bytes 786440 | tf_op jit(solution)/shard_map/ppermute | solution.py:355
  64.8 2.8 %shard_map.143.base = f32[256,1024]{1,0:T(8,128)S(1)} custom-call(f32[4,16]{1,0:T(4,128)S(1)} %bitcast.14, s32[2,2]{1,0:T(2,128)S(1)} %bitcast.10, s32[2,2]{1,0:T(2,128)S(1)} %collective-permute-done.above, f32[2,256,1024]{2,1,0:T(8,128)S(1)} %copy-done, f32[256,256]{1,0:T(8,128)S(1)} %collective-permute-done.3.refs_1_.right_1.right, ...), custom_call_target="tpu_custom_call" | custom-call | flops 134217728 | bytes 8388608 | tf_op jit(solution)/shard_map/pallas_call | solution.py:393
  67.6 2.8 %shard_map.141.base = f32[256,1024]{1,0:T(8,128)S(1)} custom-call(f32[4,16]{1,0:T(4,128)S(1)} %bitcast.15, s32[2,2]{1,0:T(2,128)S(1)} %bitcast.11, s32[2,2]{1,0:T(2,128)S(1)} %collective-permute-done.above, f32[2,256,1024]{2,1,0:T(8,128)S(1)} %copy-done, f32[256,256]{1,0:T(8,128)S(1)} %collective-permute-done.1.refs_0_.right_0.right, ...), custom_call_target="tpu_custom_call" | custom-call | flops 134217728 | bytes 8388608 | tf_op jit(solution)/shard_map/pallas_call | solution.py:393
  70.4 0.9 %shard_map.144.done = f32[256,1024]{1,0:T(8,128)S(1)} custom-call(s32[2,2]{1,0:T(2,128)S(1)} %bitcast.12, s32[2,2]{1,0:T(2,128)S(1)} %collective-permute-done.above, f32[256,1024]{1,0:T(8,128)S(1)} %shard_map.143.base, f32[264,256]{1,0:T(8,128)S(1)} %collective-permute-done.13.own_p.refs_1_, f32[264,256]{1,0:T(8,128)S(1)} %collective-permute-done.14.up_p.refs_3_), custom_call_target="tpu_custom_call" | custom-call | flops 1048576 | bytes 4194304 | tf_op jit(solution)/shard_map/pallas_call | solution.py:409
  71.3 2.3 %shard_map.145 = (f32[2,256,1024]{2,1,0:T(8,128)}, f32[2,256,256]{2,1,0:T(8,128)S(1)}) custom-call(s32[2,2]{1,0:T(2,128)S(1)} %bitcast.13, s32[2,2]{1,0:T(2,128)S(1)} %collective-permute-done.above, f32[256,1024]{1,0:T(8,128)S(1)} %shard_map.141.base, f32[264,256]{1,0:T(8,128)S(1)} %collective-permute-done.9.own_p, ...), custom_call_target="tpu_custom_call" | custom-call | flops 16777216 | bytes 10485760 | tf_op jit(solution)/shard_map/pallas_call | solution.py:412
  73.7 0.8 %shard_map.147 = f32[2,256,1024]{2,1,0:T(8,128)} custom-call(f32[2,256,1024]{2,1,0:T(8,128)} %get-tuple-element.11.mid, f32[2,256,256]{2,1,0:T(8,128)S(1)} %get-tuple-element.12.first, f32[256,256]{1,0:T(8,128)S(1)} %collective-permute-done.15.left_0, f32[256,256]{1,0:T(8,128)S(1)} %collective-permute-done.16.left_1), custom_call_target="tpu_custom_call", output_to_operand_aliasing={{}: (0, {})} | custom-call | flops 262144 | bytes 2097152 | tf_op jit(solution)/shard_map/pallas_call | solution.py:415
  (27 shorter events, 0.1 us)
Async XLA Ops:
  0.0 15.0 %copy-start = (f32[2,256,1024]{2,1,0:T(8,128)S(1)}, f32[2,256,1024]{2,1,0:T(8,128)}, u32[]{:S(2)}) copy-start(f32[2,256,1024]{2,1,0:T(8,128)} %obj.11) | copy-start | bytes 6291460
  0.0 17.6 %copy-start.3 = (s32[1,1,2,2]{3,2,1,0:T(2,128)S(1)}, s32[1,1,2,2]{3,2,1,0:T(2,128)}, u32[]{:S(2)}) copy-start(s32[1,1,2,2]{3,2,1,0:T(2,128)} %param.17) | copy-start | bytes 52
  1.2 13.8 %collective-permute-start.6 = (f32[1,2,256,256]{3,2,1,0:T(8,128)S(1)}, f32[1,2,256,256]{3,2,1,0:T(8,128)S(1)}, u32[]{:S(2)}, u32[]{:S(2)}) collective-permute-start(f32[1,2,256,256]{3,2,1,0:T(8,128)S(1)} %constant_dynamic-slice_fusion), channel_id=1, source_target_pairs={{0,1},{1,0},{2,3},{3,2},{4,5},{5,4},{6,7},{7,6},{8,9},{9,8},{10,11... | collective-permute-start | bytes 1572872 | tf_op jit(solution)/shard_map/ppermute | solution.py:355
  3.8 16.8 %collective-permute-start.1 = (f32[256,256]{1,0:T(8,128)S(1)}, f32[256,256]{1,0:T(8,128)S(1)}, u32[]{:S(2)}, u32[]{:S(2)}) collective-permute-start(f32[256,256]{1,0:T(8,128)S(1)} %slice_bitcast_fusion.1), channel_id=1, source_target_pairs={{0,15},{1,14},{2,0},{3,1},{4,2},{5,3},{6,4},{7,5},{8,7},{9,6},{10,... | collective-permute-start | bytes 786440 | tf_op jit(solution)/shard_map/ppermute | solution.py:355
  5.6 15.1 %collective-permute-start.3 = (f32[256,256]{1,0:T(8,128)S(1)}, f32[256,256]{1,0:T(8,128)S(1)}, u32[]{:S(2)}, u32[]{:S(2)}) collective-permute-start(f32[256,256]{1,0:T(8,128)S(1)} %slice_bitcast_fusion), channel_id=1, source_target_pairs={{0,15},{1,14},{2,0},{3,1},{4,2},{5,3},{6,4},{7,5},{8,7},{9,6},{10,... | collective-permute-start | bytes 786440 | tf_op jit(solution)/shard_map/ppermute | solution.py:355
  15.0 13.3 %collective-permute-start.7 = (f32[1,2,256,256]{3,2,1,0:T(8,128)S(1)}, f32[1,2,256,256]{3,2,1,0:T(8,128)S(1)}, u32[]{:S(2)}, u32[]{:S(2)}) collective-permute-start(f32[1,2,256,256]{3,2,1,0:T(8,128)S(1)} %collective-permute-done.6.probe_b), channel_id=1, source_target_pairs={{0,16},{1,17},{2,18},{3,19},{4,20},{5,21},{6,22},{7,23},{8,24},{9,... | collective-permute-start | bytes 1572872 | tf_op jit(solution)/shard_map/ppermute | solution.py:355
  15.1 5.5 %collective-permute-start.2 = (f32[8,256]{1,0:T(8,128)S(1)}, f32[8,256]{1,0:T(8,128)S(1)}, u32[]{:S(2)}, u32[]{:S(2)}) collective-permute-start(f32[8,256]{1,0:T(8,128)S(1)} %shard_map.136), channel_id=1, source_target_pairs={{0,2},{1,3},{2,4},{3,5},{4,6},{5,7},{6,9},{7,8},{8,10},{9,11},{10,... | collective-permute-start | bytes 24584 | tf_op jit(solution)/shard_map/ppermute | solution.py:355
  17.6 5.3 %copy-start.1 = (f32[1,1,2,256,256]{4,3,2,1,0:T(8,128)S(1)}, f32[1,1,2,256,256]{4,3,2,1,0:T(8,128)}, u32[]{:S(2)}) copy-start(f32[1,1,2,256,256]{4,3,2,1,0:T(8,128)} %meas.1) | copy-start | bytes 1572868
  17.6 3.0 %collective-permute-start = (s32[2,2]{1,0:T(2,128)S(1)}, s32[2,2]{1,0:T(2,128)S(1)}, u32[]{:S(2)}, u32[]{:S(2)}) collective-permute-start(s32[2,2]{1,0:T(2,128)S(1)} %bitcast.6), channel_id=1, source_target_pairs={{0,16},{1,17},{2,18},{3,19},{4,20},{5,21},{6,22},{7,23},{8,24},{9,... | collective-permute-start | bytes 56 | tf_op jit(solution)/shard_map/ppermute | solution.py:355
  21.3 7.0 %copy-start.2 = (f32[2,2,256,256]{3,2,1,0:T(8,128)S(1)}, f32[2,2,256,256]{3,2,1,0:T(8,128)}, u32[]{:S(2)}) copy-start(f32[2,2,256,256]{3,2,1,0:T(8,128)} %probe_a.1) | copy-start | bytes 3145732
  21.3 7.0 %copy-start.5 = (bf16[256,256]{1,0:T(8,128)(2,1)S(1)}, bf16[256,256]{1,0:T(8,128)(2,1)}, u32[]{:S(2)}) copy-start(bf16[256,256]{1,0:T(8,128)(2,1)} %constant.28.clone.refs_0_) | copy-start | bytes 393220
  21.3 7.0 %copy-start.6 = (bf16[256,256]{1,0:T(8,128)(2,1)S(1)}, bf16[256,256]{1,0:T(8,128)(2,1)}, u32[]{:S(2)}) copy-start(bf16[256,256]{1,0:T(8,128)(2,1)} %constant.29.clone.refs_1_) | copy-start | bytes 393220
  21.3 7.0 %copy-start.7 = (bf16[256,256]{1,0:T(8,128)(2,1)S(1)}, bf16[256,256]{1,0:T(8,128)(2,1)}, u32[]{:S(2)}) copy-start(bf16[256,256]{1,0:T(8,128)(2,1)} %constant.30.clone.refs_2_) | copy-start | bytes 393220
  21.3 7.0 %copy-start.8 = (bf16[256,256]{1,0:T(8,128)(2,1)S(1)}, bf16[256,256]{1,0:T(8,128)(2,1)}, u32[]{:S(2)}) copy-start(bf16[256,256]{1,0:T(8,128)(2,1)} %constant.31.clone.refs_3_) | copy-start | bytes 393220
  21.3 7.0 %copy-start.9 = (bf16[256,256]{1,0:T(8,128)(2,1)S(1)}, bf16[256,256]{1,0:T(8,128)(2,1)}, u32[]{:S(2)}) copy-start(bf16[256,256]{1,0:T(8,128)(2,1)} %constant.32.clone.refs_4_) | copy-start | bytes 393220
  21.3 7.0 %copy-start.10 = (bf16[256,256]{1,0:T(8,128)(2,1)S(1)}, bf16[256,256]{1,0:T(8,128)(2,1)}, u32[]{:S(2)}) copy-start(bf16[256,256]{1,0:T(8,128)(2,1)} %constant.33.clone.refs_5_) | copy-start | bytes 393220
  21.4 7.0 %copy-start.11 = (bf16[256,256]{1,0:T(8,128)(2,1)S(1)}, bf16[256,256]{1,0:T(8,128)(2,1)}, u32[]{:S(2)}) copy-start(bf16[256,256]{1,0:T(8,128)(2,1)} %constant.34.clone.refs_6_) | copy-start | bytes 393220
  21.4 7.0 %copy-start.12 = (bf16[256,256]{1,0:T(8,128)(2,1)S(1)}, bf16[256,256]{1,0:T(8,128)(2,1)}, u32[]{:S(2)}) copy-start(bf16[256,256]{1,0:T(8,128)(2,1)} %constant.35.clone.refs_7_) | copy-start | bytes 393220
  21.4 6.9 %collective-permute-start.5 = (f32[272,256]{1,0:T(8,128)S(1)}, f32[272,256]{1,0:T(8,128)S(1)}, u32[]{:S(2)}, u32[]{:S(2)}) collective-permute-start(f32[272,256]{1,0:T(8,128)S(1)} %shard_map.138), channel_id=1, source_target_pairs={{0,240},{1,241},{2,242},{3,243},{4,244},{5,245},{6,246},{7,247},{8... | collective-permute-start | bytes 835592 | tf_op jit(solution)/shard_map/ppermute | solution.py:355
  22.0 6.2 %collective-permute-start.4 = (f32[256,256]{1,0:T(8,128)S(1)}, f32[256,256]{1,0:T(8,128)S(1)}, u32[]{:S(2)}, u32[]{:S(2)}) collective-permute-start(f32[256,256]{1,0:T(8,128)S(1)} %shard_map.137), channel_id=1, source_target_pairs={{0,240},{1,241},{2,242},{3,243},{4,244},{5,245},{6,246},{7,247},{8... | collective-permute-start | bytes 786440 | tf_op jit(solution)/shard_map/ppermute | solution.py:355
  35.4 29.4 %copy-start.4 = (f32[16,4]{0,1:T(4,128)S(1)}, f32[16,4]{0,1:T(4,128)}, u32[]{:S(2)}) copy-start(f32[16,4]{0,1:T(4,128)} %param.19) | copy-start | bytes 772
  35.4 6.5 %collective-permute-start.13 = (f32[264,256]{1,0:T(8,128)S(1)}, f32[264,256]{1,0:T(8,128)S(1)}, u32[]{:S(2)}, u32[]{:S(2)}) collective-permute-start(f32[264,256]{1,0:T(8,128)S(1)} %get-tuple-element.10.own.refs_0_), channel_id=1, source_target_pairs={{0,1},{1,0},{2,3},{3,2},{4,5},{5,4},{6,7},{7,6},{8,9},{9,8},{10,11... | collective-permute-start | bytes 811016 | tf_op jit(solution)/shard_map/ppermute | solution.py:355
  35.7 11.9 %collective-permute-start.8 = (f32[264,256]{1,0:T(8,128)S(1)}, f32[264,256]{1,0:T(8,128)S(1)}, u32[]{:S(2)}, u32[]{:S(2)}) collective-permute-start(f32[264,256]{1,0:T(8,128)S(1)} %get-tuple-element.9.own.refs_0_), channel_id=1, source_target_pairs={{0,16},{1,17},{2,18},{3,19},{4,20},{5,21},{6,22},{7,23},{8,24},{9,... | collective-permute-start | bytes 811016 | tf_op jit(solution)/shard_map/ppermute | solution.py:355
  40.1 11.9 %collective-permute-start.9 = (f32[264,256]{1,0:T(8,128)S(1)}, f32[264,256]{1,0:T(8,128)S(1)}, u32[]{:S(2)}, u32[]{:S(2)}) collective-permute-start(f32[264,256]{1,0:T(8,128)S(1)} %get-tuple-element.9.own.refs_0_), channel_id=1, source_target_pairs={{0,1},{1,0},{2,3},{3,2},{4,5},{5,4},{6,7},{7,6},{8,9},{9,8},{10,11... | collective-permute-start | bytes 811016 | tf_op jit(solution)/shard_map/ppermute | solution.py:355
  41.8 16.3 %collective-permute-start.12 = (f32[264,256]{1,0:T(8,128)S(1)}, f32[264,256]{1,0:T(8,128)S(1)}, u32[]{:S(2)}, u32[]{:S(2)}) collective-permute-start(f32[264,256]{1,0:T(8,128)S(1)} %get-tuple-element.10.own.refs_0_), channel_id=1, source_target_pairs={{0,16},{1,17},{2,18},{3,19},{4,20},{5,21},{6,22},{7,23},{8,24},{9,... | collective-permute-start | bytes 811016 | tf_op jit(solution)/shard_map/ppermute | solution.py:355
  41.9 16.3 %collective-permute-start.14 = (f32[264,256]{1,0:T(8,128)S(1)}, f32[264,256]{1,0:T(8,128)S(1)}, u32[]{:S(2)}, u32[]{:S(2)}) collective-permute-start(f32[264,256]{1,0:T(8,128)S(1)} %collective-permute-done.13.own_p.refs_1_), channel_id=1, source_target_pairs={{0,16},{1,17},{2,18},{3,19},{4,20},{5,21},{6,22},{7,23},{8,24},{9,... | collective-permute-start | bytes 811016 | tf_op jit(solution)/shard_map/ppermute | solution.py:355
  48.2 9.9 %collective-permute-start.11 = (f32[256,256]{1,0:T(8,128)S(1)}, f32[256,256]{1,0:T(8,128)S(1)}, u32[]{:S(2)}, u32[]{:S(2)}) collective-permute-start(f32[256,256]{1,0:T(8,128)S(1)} %shard_map.142), channel_id=1, source_target_pairs={{0,2},{1,3},{2,4},{3,5},{4,6},{5,7},{6,9},{7,8},{8,10},{9,11},{10,... | collective-permute-start | bytes 786440 | tf_op jit(solution)/shard_map/ppermute | solution.py:355
  52.0 19.3 %collective-permute-start.10 = (f32[264,256]{1,0:T(8,128)S(1)}, f32[264,256]{1,0:T(8,128)S(1)}, u32[]{:S(2)}, u32[]{:S(2)}) collective-permute-start(f32[264,256]{1,0:T(8,128)S(1)} %collective-permute-done.9.own_p), channel_id=1, source_target_pairs={{0,16},{1,17},{2,18},{3,19},{4,20},{5,21},{6,22},{7,23},{8,24},{9,... | collective-permute-start | bytes 811016 | tf_op jit(solution)/shard_map/ppermute | solution.py:355
  58.2 15.5 %collective-permute-start.15 = (f32[256,256]{1,0:T(8,128)S(1)}, f32[256,256]{1,0:T(8,128)S(1)}, u32[]{:S(2)}, u32[]{:S(2)}) collective-permute-start(f32[256,256]{1,0:T(8,128)S(1)} %collective-permute-done.11.left_0), channel_id=1, source_target_pairs={{0,1},{1,0},{2,3},{3,2},{4,5},{5,4},{6,7},{7,6},{8,9},{9,8},{10,11... | collective-permute-start | bytes 786440 | tf_op jit(solution)/shard_map/ppermute | solution.py:355
  58.9 14.7 %collective-permute-start.16 = (f32[256,256]{1,0:T(8,128)S(1)}, f32[256,256]{1,0:T(8,128)S(1)}, u32[]{:S(2)}, u32[]{:S(2)}) collective-permute-start(f32[256,256]{1,0:T(8,128)S(1)} %shard_map.146), channel_id=1, source_target_pairs={{0,2},{1,3},{2,4},{3,5},{4,6},{5,7},{6,9},{7,8},{8,10},{9,11},{10,... | collective-permute-start | bytes 786440 | tf_op jit(solution)/shard_map/ppermute | solution.py:355

commit v2 on v1

--- a/solution.py
+++ b/solution.py
@@ -156,14 +156,15 @@
 
 def send_body(c, above, obj, *refs):
     _, q, s = place(above, lax.axis_index("mode"))
-    out = refs[-1]
+    out = refs[c + 1 + c]
     out[0:W, :] = window(obj, c, refs[c], q, s)
     if c == 1:
         for d in range(2):
             rim_rows(out, W + 8 * d, obj, d, 0, refs[d], refs[2])
-
-
-def main_body(offs, counts, obj, left, right_0, right_1, below_0, below_1, probe_a, probe_b, probe_c, meas, *refs):
+            rim_rows(refs[4], 8 * d, obj, d, W - 1, refs[d], refs[2])
+
+
+def main_body(offs, counts, obj, right_0, right_1, below_0, below_1, probe_a, probe_b, probe_c, meas, *refs):
     mats, (grad_0, grad_1, wave) = refs[:8], refs[8:]
     m = lax.axis_index("mode")
     last_tx = lax.axis_index("tx") == lax.axis_size("tx") - 1
@@ -195,9 +196,8 @@
         br, bi = backward(resid * wave[k, 0], resid * wave[k, 1], *tabs)
         grad[0] = grad[0] + pr * br + pi * bi
         grad[1] = grad[1] + pr * bi - pi * br
-    for c, right, out in ((0, right_0, grad_0), (1, right_1, grad_1)):
-        out[0:W, :] = pltpu.roll(pltpu.roll(grad[c] * live, row0, 0), s, 1)
-        rim_rows(out, W, obj, c, W - 1, right, left)
+    for g, out in ((grad[0], grad_0), (grad[1], grad_1)):
+        out[...] = pltpu.roll(pltpu.roll(g * live, row0, 0), s, 1)
 
 
 def sort_body(meas, out):
@@ -228,17 +228,17 @@
     total = jnp.zeros((W, W), f32)
     for k, slot in enumerate((m, 1 - m)[:n]):
         row0, q, s = place(offs, slot)
-        total = total + jnp.where((q == 3) & (lane < s) & (row >= row0), refs[k][0:W, :], 0.0)
+        total = total + jnp.where((q == 3) & (lane < s) & (row >= row0), refs[k][...], 0.0)
         row0, q, s = place(above, slot)
         keep = (q == 3) & (lane < s) & (row < row0) & (tx > 0)
-        total = total + jnp.where(keep, refs[n + k][0:W, :], 0.0)
+        total = total + jnp.where(keep, refs[n + k][...], 0.0)
     refs[2 * n][...] = total
 
 
 def take(out, ref, spot, rows):
     _, q, s = spot
     lane = iota(1)
-    value = ref[0:W, :]
+    value = ref[...]
     here = pl.ds(pl.multiple_of(q * W, W), W)
     out[:, here] = out[:, here] - step_size * jnp.where(rows & (lane >= s), value, 0.0)
     nxt = pl.ds(pl.multiple_of(jnp.minimum(q + 1, 3) * W, W), W)
@@ -246,7 +246,19 @@
     out[:, nxt] = out[:, nxt] - step_size * jnp.where(keep, value, 0.0)
 
 
-def prior_body(c, filt, offs, above, obj, right, left, up, down, own, out):
+def take_all(out, offs, above, refs, skip=0):
+    m = lax.axis_index("mode")
+    row = iota(0)
+    n = len(refs) // 2
+    for k, slot in enumerate((m, 1 - m)[skip : skip + n]):
+        spot = place(offs, slot)
+        take(out, refs[k], spot, row >= spot[0])
+        spot = place(above, slot)
+        take(out, refs[n + k], spot, (row < spot[0]) & (lax.axis_index("tx") > 0))
+
+
+def prior_body(c, filt, offs, above, obj, right, left, up, down, *refs):
+    out = refs[-1]
     tx, ty = lax.axis_index("tx"), lax.axis_index("ty")
     n_tx, n_ty = lax.axis_size("tx"), lax.axis_size("ty")
     cols = obj.shape[2]
@@ -261,7 +273,6 @@
         one_right = jnp.where(lane == cols - 1, after, pltpu.roll(x, cols - 1, 1))
         return one_left, one_right
 
-    spot = place(offs, lax.axis_index("mode"))
     x = obj[c]
     after = jnp.where(ty == n_ty - 1, 0.0, right[:, 0:1])
     edge = jnp.broadcast_to(left[c : c + 1, :], (128, W)).T
@@ -272,7 +283,7 @@
         whole = jnp.concatenate([rim[k : k + 1, :] for k in range(4)], axis=1)
         return whole, rim[5:6, at : at + 1], rim[4:5, 0:1]
 
-    u_mid, u_left, u_right = line(up[W : W + 8, :], tx == 0, W - 1)
+    u_mid, u_left, u_right = line(up[8 * c : 8 * c + 8, :], tx == 0, W - 1)
     d_mid, d_left, d_right = line(down[W + 8 * c : W + 8 * c + 8, :], tx == n_tx - 1, 0)
     xl, xr = beside(x, before, after)
 
@@ -303,23 +314,13 @@
         in_row & in_col, g[3][0] * xul + g[3][1] * xu + g[3][2] * xl + g[3][3] * x, 0.0
     )
     out[...] = x - step_size * total
-    take(out, own, spot, iota(0) >= spot[0])
-    spot = place(above, lax.axis_index("mode"))
-    take(out, up, spot, (iota(0) < spot[0]) & (tx > 0))
-
-
-def fold_body(offs, above, base, own_p, up_p, out):
-    slot = 1 - lax.axis_index("mode")
-    row = iota(0)
-    mine, over = place(offs, slot), place(above, slot)
-    out[...] = base[...]
-    take(out, own_p, mine, row >= mine[0])
-    take(out, up_p, over, (row < over[0]) & (lax.axis_index("tx") > 0))
+    take_all(out, offs, above, refs[:-1])
 
 
 def mid_body(offs, above, base, own_p, up_p, left_0, done, out, first):
     part = out.at[0]
-    fold_body(offs, above, base, own_p, up_p, part)
+    part[...] = base[...]
+    take_all(part, offs, above, (own_p, up_p), 1)
     first[0] = part[:, 0:W] - step_size * jnp.where(lax.axis_index("ty") > 0, left_0[...], 0.0)
     out[1] = done[...]
     first[1] = done[:, 0:W]
@@ -374,28 +375,35 @@
         functools.partial(send_body, 0), piece, [SMEM] + [VMEM] * 2, 8, 1 << 20, 2 << 20
     )(above, obj, right[0])
     below_0 = go(up_0, "up")
-    up_1 = call(
-        functools.partial(send_body, 1), (W + 16, W), [SMEM] + [VMEM] * 4, 8, 1 << 20, 2 << 20
+    up_1, rim = call(
+        functools.partial(send_body, 1),
+        [(W + 16, W), (16, W)],
+        [SMEM] + [VMEM] * 4,
+        8,
+        1 << 20,
+        2 << 20,
     )(above, obj, *right, left)
     below_1 = go(up_1, "up")
+    over = go(rim, "down")
     g0, g1 = call(
         main_body,
-        [(W + 8, W)] * 2,
-        [SMEM, SMEM] + [VMEM] * 18,
+        [piece] * 2,
+        [SMEM, SMEM] + [VMEM] * 17,
         16,
         5 << 30,
         12 << 20,
         [pltpu.VMEM((4, 2, W, W), f32)],
-    )(offs, counts, obj, left, *right, below_0, below_1, probe, probe_b, probe_c, meas, *tabs)
+    )(offs, counts, obj, *right, below_0, below_1, probe, probe_b, probe_c, meas, *tabs)
     p1, b0 = go(g1, "swap"), go(g0, "down")
     p0, b1 = go(g0, "swap"), go(g1, "down")
-    base = [
-        call(
-            functools.partial(prior_body, c), (rows, cols), [SMEM] * 3 + [VMEM] * 6, 12, 1 << 27, 8 << 20
-        )(filt, offs, above, obj, right[c], left, b, below_1, g)
-        for c, g, b in ((0, g0, b0), (1, g1, b1))
-    ]
     c1, c0 = go(p1, "down"), go(p0, "down")
+
+    def prior(c, *args):
+        specs = [SMEM] * 3 + [VMEM] * (5 + len(args))
+        kernel = call(functools.partial(prior_body, c), (rows, cols), specs, 12, 1 << 27, 8 << 20)
+        return kernel(filt, offs, above, obj, right[c], left, over, below_1, *args)
+
+    base = [prior(0, g0, b0), prior(1, g1, p1, b1, c1)]
 
     def spill(n, *args):
         specs = [SMEM, SMEM] + [VMEM] * (2 * n)
@@ -406,12 +414,9 @@
     left_p0 = go(left_m0, "swap")
     left_1 = go(spill(2, g1, p1, b1, c1), "right")
     any_space = pl.BlockSpec(memory_space=pl.ANY)
-    fold = call(fold_body, (rows, cols), [SMEM, SMEM] + [VMEM] * 3, 8, 1 << 20, 4 << 20)(
-        offs, above, base[1], p1, c1
-    )
     mid, first = call(
         mid_body, [whole, (2, W, W)], [SMEM, SMEM] + [VMEM] * 5, 12, 1 << 24, 10 << 20
-    )(offs, above, base[0], p0, c0, left_m0, fold)
+    )(offs, above, base[0], p0, c0, left_m0, base[1])
     return call(
         final_body,
         whole,

time: 74.8 us -> 76.7 us (1.025)
  the two profiles are of different devices: /device:TPU:120 before, /device:TPU:4 now
where the time goes in v2:
time: 76.7 us; the launch traced here: 76.5 us
  waiting for transfers between devices  38 us (50%)
  Pallas kernels  19.4 us (25%)
  starting transfers between devices  14.8 us (19%)
  local copies, waits for them, and re-layouts  3.24 us (4%)
  between operations  1.08 us (1%)
    ppermute x18, waiting for transfers between devices, go(): return lax.ppermute(value, axes, ring[where])  38 us
    ppermute x18, starting transfers between devices, go(): return lax.ppermute(value, axes, ring[where])  14.8 us
    pallas_call x1, Pallas kernels, local(): call(main_body, [piece] * 2, [SMEM, SMEM] + [VMEM] * 17, 16, 5 << 30, 12...  6.86 us
    pallas_call x2, Pallas kernels, prior(): return kernel(filt, offs, above, obj, right[c], left, over, below_1, *args)  5.9 us
    pallas_call x1, Pallas kernels, local(): call(mid_body, [whole, (2, W, W)], [SMEM, SMEM] + [VMEM] * 5, 12, 1 << 24...  2.35 us
  transfers between devices with their start and end apart: 18, of which 10 were waited for; matrix products, arithmetic and copies ran while one was open for 3% of the time, Pallas kernels for 15%

profile of v2, /device:TPU:4, one launch (start us, length us, event | category | flops | bytes accessed | tf_op | source)
XLA Modules:
  0.0 76.5 jit_solution(7487933907566222162)
XLA Ops:
  0.0 1.2 %constant_dynamic-slice_fusion = f32[1,2,256,256]{3,2,1,0:T(8,128)S(1)} fusion(f32[2,2,256,256]{3,2,1,0:T(8,128)} %probe_a.1, s32[]{:T(128)S(6)} %select_n.3), kind=kLoop, calls=%fused_computation.2 | loop fusion | bytes 1048580 | tf_op jit(solution)/shard_map/dynamic_slice | solution.py:367
  1.2 1.3 %collective-permute-start.7 = (f32[1,2,256,256]{3,2,1,0:T(8,128)S(1)}, f32[1,2,256,256]{3,2,1,0:T(8,128)S(1)}, u32[]{:S(2)}, u32[]{:S(2)}) collective-permute-start(f32[1,2,256,256]{3,2,1,0:T(8,128)S(1)} %constant_dynamic-slice_fusion), channel_id=1, source_target_pairs={{0,1},{1,0},{2,3},{3,2},{4,5},{5,4},{6,7},{7,6},{8,9},{9,8},{10,11... | collective-permute-start | bytes 1572872 | tf_op jit(solution)/shard_map/ppermute | solution.py:356
  2.5 1.0 %slice_bitcast_fusion.1 = f32[256,256]{1,0:T(8,128)S(1)} fusion(f32[2,256,1024]{2,1,0:T(8,128)} %obj.11), kind=kLoop, calls=%fused_computation.1 | loop fusion | bytes 524288 | tf_op jit(solution)/shard_map/squeeze | solution.py:364
  3.5 2.4 %collective-permute-start.1 = (f32[256,256]{1,0:T(8,128)S(1)}, f32[256,256]{1,0:T(8,128)S(1)}, u32[]{:S(2)}, u32[]{:S(2)}) collective-permute-start(f32[256,256]{1,0:T(8,128)S(1)} %slice_bitcast_fusion.1), channel_id=1, source_target_pairs={{0,15},{1,14},{2,0},{3,1},{4,2},{5,3},{6,4},{7,5},{8,7},{9,6},{10,... | collective-permute-start | bytes 786440 | tf_op jit(solution)/shard_map/ppermute | solution.py:356
  5.9 1.0 %slice_bitcast_fusion = f32[256,256]{1,0:T(8,128)S(1)} fusion(f32[2,256,1024]{2,1,0:T(8,128)} %obj.11), kind=kLoop, calls=%fused_computation | loop fusion | bytes 524288 | tf_op jit(solution)/shard_map/squeeze | solution.py:365
  6.9 0.8 %collective-permute-start.3 = (f32[256,256]{1,0:T(8,128)S(1)}, f32[256,256]{1,0:T(8,128)S(1)}, u32[]{:S(2)}, u32[]{:S(2)}) collective-permute-start(f32[256,256]{1,0:T(8,128)S(1)} %slice_bitcast_fusion), channel_id=1, source_target_pairs={{0,15},{1,14},{2,0},{3,1},{4,2},{5,3},{6,4},{7,5},{8,7},{9,6},{10,... | collective-permute-start | bytes 786440 | tf_op jit(solution)/shard_map/ppermute | solution.py:356
  7.7 7.3 %collective-permute-done.7.probe_b = f32[1,2,256,256]{3,2,1,0:T(8,128)S(1)} collective-permute-done((f32[1,2,256,256]{3,2,1,0:T(8,128)S(1)}, f32[1,2,256,256]{3,2,1,0:T(8,128)S(1)}, u32[]{:S(2)}, u32[]{:S(2)}) %collective-permute-start.7) | collective-permute-done | bytes 524320 | tf_op jit(solution)/shard_map/ppermute | solution.py:356
  15.0 0.1 shard_map.136
  15.1 1.7 %collective-permute-start.2 = (f32[8,256]{1,0:T(8,128)S(1)}, f32[8,256]{1,0:T(8,128)S(1)}, u32[]{:S(2)}, u32[]{:S(2)}) collective-permute-start(f32[8,256]{1,0:T(8,128)S(1)} %shard_map.136), channel_id=1, source_target_pairs={{0,2},{1,3},{2,4},{3,5},{4,6},{5,7},{6,9},{7,8},{8,10},{9,11},{10,... | collective-permute-start | bytes 24584 | tf_op jit(solution)/shard_map/ppermute | solution.py:356
  16.8 0.2 collective-permute-start
  17.0 6.7 %collective-permute-done.above = s32[2,2]{1,0:T(2,128)S(1)} collective-permute-done((s32[2,2]{1,0:T(2,128)S(1)}, s32[2,2]{1,0:T(2,128)S(1)}, u32[]{:S(2)}, u32[]{:S(2)}) %collective-permute-start) | collective-permute-done | bytes 48 | tf_op jit(solution)/shard_map/ppermute | solution.py:356
  23.7 0.0 collective-permute-done.1.refs_0_.right_0.right
  23.7 0.0 collective-permute-done.3.refs_1_.right_1.right
  23.7 0.6 shard_map.137
  24.4 0.0 copy-start.2
  24.4 0.0 copy-start.5
  24.4 0.0 copy-start.6
  24.4 0.0 copy-start.7
  24.4 0.0 copy-start.8
  24.4 0.0 copy-start.9
  24.4 0.0 copy-start.10
  24.5 0.0 copy-start.11
  24.5 0.0 copy-start.12
  24.5 2.1 %collective-permute-start.5 = (f32[272,256]{1,0:T(8,128)S(1)}, f32[272,256]{1,0:T(8,128)S(1)}, u32[]{:S(2)}, u32[]{:S(2)}) collective-permute-start(f32[272,256]{1,0:T(8,128)S(1)} %get-tuple-element.12), channel_id=1, source_target_pairs={{0,240},{1,241},{2,242},{3,243},{4,244},{5,245},{6,246},{7,247},{8... | collective-permute-start | bytes 835592 | tf_op jit(solution)/shard_map/ppermute | solution.py:356
  26.5 0.6 shard_map.138
  27.2 1.2 %collective-permute-start.6 = (f32[256,256]{1,0:T(8,128)S(1)}, f32[256,256]{1,0:T(8,128)S(1)}, u32[]{:S(2)}, u32[]{:S(2)}) collective-permute-start(f32[256,256]{1,0:T(8,128)S(1)} %shard_map.138), channel_id=1, source_target_pairs={{0,240},{1,241},{2,242},{3,243},{4,244},{5,245},{6,246},{7,247},{8... | collective-permute-start | bytes 786440 | tf_op jit(solution)/shard_map/ppermute | solution.py:356
  29.0 0.7 shard_map.139.meas
  29.7 3.7 %collective-permute-done.6.below_0 = f32[256,256]{1,0:T(8,128)S(1)} collective-permute-done((f32[256,256]{1,0:T(8,128)S(1)}, f32[256,256]{1,0:T(8,128)S(1)}, u32[]{:S(2)}, u32[]{:S(2)}) %collective-permute-start.6) | collective-permute-done | bytes 262176 | tf_op jit(solution)/shard_map/ppermute | solution.py:356
  33.5 6.9 %shard_map.140 = (f32[256,256]{1,0:T(8,128)S(1)}, f32[256,256]{1,0:T(8,128)S(1)}) custom-call(s32[2,2]{1,0:T(2,128)S(1)} %bitcast.7, s32[1,1]{1,0:T(1,128)S(6)} %copy.17.counts, f32[2,256,1024]{2,1,0:T(8,128)S(1)} %copy-done, f32[256,256]{1,0:T(8,128)S(1)} %collective-permute-done.1.refs_0_.right_0.right, ...), custom_call_target="tpu_custom_call" | custom-call | flops 5368709120 | bytes 12582912 | tf_op jit(solution)/shard_map/pallas_call | solution.py:388
  40.4 0.0 copy-start.4
  40.4 2.5 %collective-permute-start.13 = (f32[256,256]{1,0:T(8,128)S(1)}, f32[256,256]{1,0:T(8,128)S(1)}, u32[]{:S(2)}, u32[]{:S(2)}) collective-permute-start(f32[256,256]{1,0:T(8,128)S(1)} %get-tuple-element.14.refs_0_), channel_id=1, source_target_pairs={{0,1},{1,0},{2,3},{3,2},{4,5},{5,4},{6,7},{7,6},{8,9},{9,8},{10,11... | collective-permute-start | bytes 786440 | tf_op jit(solution)/shard_map/ppermute | solution.py:356
  42.9 0.1 collective-permute-start.10
  43.0 6.5 %collective-permute-done.13.refs_1_ = f32[256,256]{1,0:T(8,128)S(1)} collective-permute-done((f32[256,256]{1,0:T(8,128)S(1)}, f32[256,256]{1,0:T(8,128)S(1)}, u32[]{:S(2)}, u32[]{:S(2)}) %collective-permute-start.13) | collective-permute-done | bytes 262176 | tf_op jit(solution)/shard_map/ppermute | solution.py:356
  49.6 0.3 collective-permute-done.9.refs_1_
  49.9 0.6 shard_map.142
  50.5 0.1 collective-permute-start.12
  50.6 1.7 %collective-permute-done.10.own_p = f32[256,256]{1,0:T(8,128)S(1)} collective-permute-done((f32[256,256]{1,0:T(8,128)S(1)}, f32[256,256]{1,0:T(8,128)S(1)}, u32[]{:S(2)}, u32[]{:S(2)}) %collective-permute-start.10) | collective-permute-done | bytes 262176 | tf_op jit(solution)/shard_map/ppermute | solution.py:356
  52.4 0.3 collective-permute-done.14.refs_2_
  52.7 3.9 %collective-permute-done.15.refs_3_ = f32[256,256]{1,0:T(8,128)S(1)} collective-permute-done((f32[256,256]{1,0:T(8,128)S(1)}, f32[256,256]{1,0:T(8,128)S(1)}, u32[]{:S(2)}, u32[]{:S(2)}) %collective-permute-start.15) | collective-permute-done | bytes 262176 | tf_op jit(solution)/shard_map/ppermute | solution.py:356
  56.6 0.7 shard_map.145
  57.3 0.3 collective-permute-start.17
  57.6 3.1 %collective-permute-done.12.left_0 = f32[256,256]{1,0:T(8,128)S(1)} collective-permute-done((f32[256,256]{1,0:T(8,128)S(1)}, f32[256,256]{1,0:T(8,128)S(1)}, u32[]{:S(2)}, u32[]{:S(2)}) %collective-permute-start.12) | collective-permute-done | bytes 262176 | tf_op jit(solution)/shard_map/ppermute | solution.py:356
  60.6 2.2 %collective-permute-start.16 = (f32[256,256]{1,0:T(8,128)S(1)}, f32[256,256]{1,0:T(8,128)S(1)}, u32[]{:S(2)}, u32[]{:S(2)}) collective-permute-start(f32[256,256]{1,0:T(8,128)S(1)} %collective-permute-done.12.left_0), channel_id=1, source_target_pairs={{0,1},{1,0},{2,3},{3,2},{4,5},{5,4},{6,7},{7,6},{8,9},{9,8},{10,11... | collective-permute-start | bytes 786440 | tf_op jit(solution)/shard_map/ppermute | solution.py:356
  62.9 4.4 %collective-permute-done.4.up = f32[16,256]{1,0:T(8,128)S(1)} collective-permute-done((f32[16,256]{1,0:T(8,128)S(1)}, f32[16,256]{1,0:T(8,128)S(1)}, u32[]{:S(2)}, u32[]{:S(2)}) %collective-permute-start.4) | collective-permute-done | bytes 16416 | tf_op jit(solution)/shard_map/ppermute | solution.py:356
  67.2 2.8 %shard_map.141.base = f32[256,1024]{1,0:T(8,128)S(1)} custom-call(f32[4,16]{1,0:T(4,128)S(1)} %bitcast.13, s32[2,2]{1,0:T(2,128)S(1)} %bitcast.10, s32[2,2]{1,0:T(2,128)S(1)} %collective-permute-done.above, f32[2,256,1024]{2,1,0:T(8,128)S(1)} %copy-done, f32[256,256]{1,0:T(8,128)S(1)} %collective-permute-done.1.refs_0_.right_0.right, ...), custom_call_target="tpu_custom_call" | custom-call | flops 134217728 | bytes 8388608 | tf_op jit(solution)/shard_map/pallas_call | solution.py:404
  70.0 3.1 %shard_map.143.done = f32[256,1024]{1,0:T(8,128)S(1)} custom-call(f32[4,16]{1,0:T(4,128)S(1)} %bitcast.14, s32[2,2]{1,0:T(2,128)S(1)} %bitcast.11, s32[2,2]{1,0:T(2,128)S(1)} %collective-permute-done.above, f32[2,256,1024]{2,1,0:T(8,128)S(1)} %copy-done, f32[256,256]{1,0:T(8,128)S(1)} %collective-permute-done.3.refs_1_.right_1.right, ...), custom_call_target="tpu_custom_call" | custom-call | flops 134217728 | bytes 8388608 | tf_op jit(solution)/shard_map/pallas_call | solution.py:404
  73.2 2.3 %shard_map.144 = (f32[2,256,1024]{2,1,0:T(8,128)}, f32[2,256,256]{2,1,0:T(8,128)S(1)}) custom-call(s32[2,2]{1,0:T(2,128)S(1)} %bitcast.12, s32[2,2]{1,0:T(2,128)S(1)} %collective-permute-done.above, f32[256,1024]{1,0:T(8,128)S(1)} %shard_map.141.base, f32[256,256]{1,0:T(8,128)S(1)} %collective-permute-done.10.own_p, ...), custom_call_target="tpu_custom_call" | custom-call | flops 16777216 | bytes 10485760 | tf_op jit(solution)/shard_map/pallas_call | solution.py:417
  75.5 0.8 %shard_map.146 = f32[2,256,1024]{2,1,0:T(8,128)} custom-call(f32[2,256,1024]{2,1,0:T(8,128)} %get-tuple-element.15.mid, f32[2,256,256]{2,1,0:T(8,128)S(1)} %get-tuple-element.16.first, f32[256,256]{1,0:T(8,128)S(1)} %collective-permute-done.16.left_0, f32[256,256]{1,0:T(8,128)S(1)} %collective-permute-done.17.left_1), custom_call_target="tpu_custom_call", output_to_operand_aliasing={{}: (0, {})} | custom-call | flops 262144 | bytes 2097152 | tf_op jit(solution)/shard_map/pallas_call | solution.py:420
  (28 shorter events, 0.1 us)
Async XLA Ops:
  0.0 15.0 %copy-start = (f32[2,256,1024]{2,1,0:T(8,128)S(1)}, f32[2,256,1024]{2,1,0:T(8,128)}, u32[]{:S(2)}) copy-start(f32[2,256,1024]{2,1,0:T(8,128)} %obj.11) | copy-start | bytes 6291460
  0.0 16.8 %copy-start.3 = (s32[1,1,2,2]{3,2,1,0:T(2,128)S(1)}, s32[1,1,2,2]{3,2,1,0:T(2,128)}, u32[]{:S(2)}) copy-start(s32[1,1,2,2]{3,2,1,0:T(2,128)} %param.17) | copy-start | bytes 52
  1.2 13.8 %collective-permute-start.7 = (f32[1,2,256,256]{3,2,1,0:T(8,128)S(1)}, f32[1,2,256,256]{3,2,1,0:T(8,128)S(1)}, u32[]{:S(2)}, u32[]{:S(2)}) collective-permute-start(f32[1,2,256,256]{3,2,1,0:T(8,128)S(1)} %constant_dynamic-slice_fusion), channel_id=1, source_target_pairs={{0,1},{1,0},{2,3},{3,2},{4,5},{5,4},{6,7},{7,6},{8,9},{9,8},{10,11... | collective-permute-start | bytes 1572872 | tf_op jit(solution)/shard_map/ppermute | solution.py:356
  3.5 20.2 %collective-permute-start.1 = (f32[256,256]{1,0:T(8,128)S(1)}, f32[256,256]{1,0:T(8,128)S(1)}, u32[]{:S(2)}, u32[]{:S(2)}) collective-permute-start(f32[256,256]{1,0:T(8,128)S(1)} %slice_bitcast_fusion.1), channel_id=1, source_target_pairs={{0,15},{1,14},{2,0},{3,1},{4,2},{5,3},{6,4},{7,5},{8,7},{9,6},{10,... | collective-permute-start | bytes 786440 | tf_op jit(solution)/shard_map/ppermute | solution.py:356
  6.9 16.9 %collective-permute-start.3 = (f32[256,256]{1,0:T(8,128)S(1)}, f32[256,256]{1,0:T(8,128)S(1)}, u32[]{:S(2)}, u32[]{:S(2)}) collective-permute-start(f32[256,256]{1,0:T(8,128)S(1)} %slice_bitcast_fusion), channel_id=1, source_target_pairs={{0,15},{1,14},{2,0},{3,1},{4,2},{5,3},{6,4},{7,5},{8,7},{9,6},{10,... | collective-permute-start | bytes 786440 | tf_op jit(solution)/shard_map/ppermute | solution.py:356
  15.0 18.4 %collective-permute-start.8 = (f32[1,2,256,256]{3,2,1,0:T(8,128)S(1)}, f32[1,2,256,256]{3,2,1,0:T(8,128)S(1)}, u32[]{:S(2)}, u32[]{:S(2)}) collective-permute-start(f32[1,2,256,256]{3,2,1,0:T(8,128)S(1)} %collective-permute-done.7.probe_b), channel_id=1, source_target_pairs={{0,16},{1,17},{2,18},{3,19},{4,20},{5,21},{6,22},{7,23},{8,24},{9,... | collective-permute-start | bytes 1572872 | tf_op jit(solution)/shard_map/ppermute | solution.py:356
  15.1 8.6 %collective-permute-start.2 = (f32[8,256]{1,0:T(8,128)S(1)}, f32[8,256]{1,0:T(8,128)S(1)}, u32[]{:S(2)}, u32[]{:S(2)}) collective-permute-start(f32[8,256]{1,0:T(8,128)S(1)} %shard_map.136), channel_id=1, source_target_pairs={{0,2},{1,3},{2,4},{3,5},{4,6},{5,7},{6,9},{7,8},{8,10},{9,11},{10,... | collective-permute-start | bytes 24584 | tf_op jit(solution)/shard_map/ppermute | solution.py:356
  16.8 12.2 %copy-start.1 = (f32[1,1,2,256,256]{4,3,2,1,0:T(8,128)S(1)}, f32[1,1,2,256,256]{4,3,2,1,0:T(8,128)}, u32[]{:S(2)}) copy-start(f32[1,1,2,256,256]{4,3,2,1,0:T(8,128)} %meas.1) | copy-start | bytes 1572868
  16.8 6.9 %collective-permute-start = (s32[2,2]{1,0:T(2,128)S(1)}, s32[2,2]{1,0:T(2,128)S(1)}, u32[]{:S(2)}, u32[]{:S(2)}) collective-permute-start(s32[2,2]{1,0:T(2,128)S(1)} %bitcast.6), channel_id=1, source_target_pairs={{0,16},{1,17},{2,18},{3,19},{4,20},{5,21},{6,22},{7,23},{8,24},{9,... | collective-permute-start | bytes 56 | tf_op jit(solution)/shard_map/ppermute | solution.py:356
  24.4 9.1 %copy-start.2 = (f32[2,2,256,256]{3,2,1,0:T(8,128)S(1)}, f32[2,2,256,256]{3,2,1,0:T(8,128)}, u32[]{:S(2)}) copy-start(f32[2,2,256,256]{3,2,1,0:T(8,128)} %probe_a.1) | copy-start | bytes 3145732
  24.4 9.0 %copy-start.5 = (bf16[256,256]{1,0:T(8,128)(2,1)S(1)}, bf16[256,256]{1,0:T(8,128)(2,1)}, u32[]{:S(2)}) copy-start(bf16[256,256]{1,0:T(8,128)(2,1)} %constant.28.clone.refs_0_) | copy-start | bytes 393220
  24.4 9.0 %copy-start.6 = (bf16[256,256]{1,0:T(8,128)(2,1)S(1)}, bf16[256,256]{1,0:T(8,128)(2,1)}, u32[]{:S(2)}) copy-start(bf16[256,256]{1,0:T(8,128)(2,1)} %constant.29.clone.refs_1_) | copy-start | bytes 393220
  24.4 9.0 %copy-start.7 = (bf16[256,256]{1,0:T(8,128)(2,1)S(1)}, bf16[256,256]{1,0:T(8,128)(2,1)}, u32[]{:S(2)}) copy-start(bf16[256,256]{1,0:T(8,128)(2,1)} %constant.30.clone.refs_2_) | copy-start | bytes 393220
  24.4 9.0 %copy-start.8 = (bf16[256,256]{1,0:T(8,128)(2,1)S(1)}, bf16[256,256]{1,0:T(8,128)(2,1)}, u32[]{:S(2)}) copy-start(bf16[256,256]{1,0:T(8,128)(2,1)} %constant.31.clone.refs_3_) | copy-start | bytes 393220
  24.4 9.0 %copy-start.9 = (bf16[256,256]{1,0:T(8,128)(2,1)S(1)}, bf16[256,256]{1,0:T(8,128)(2,1)}, u32[]{:S(2)}) copy-start(bf16[256,256]{1,0:T(8,128)(2,1)} %constant.32.clone.refs_4_) | copy-start | bytes 393220
  24.4 9.0 %copy-start.10 = (bf16[256,256]{1,0:T(8,128)(2,1)S(1)}, bf16[256,256]{1,0:T(8,128)(2,1)}, u32[]{:S(2)}) copy-start(bf16[256,256]{1,0:T(8,128)(2,1)} %constant.33.clone.refs_5_) | copy-start | bytes 393220
  24.5 9.0 %copy-start.11 = (bf16[256,256]{1,0:T(8,128)(2,1)S(1)}, bf16[256,256]{1,0:T(8,128)(2,1)}, u32[]{:S(2)}) copy-start(bf16[256,256]{1,0:T(8,128)(2,1)} %constant.34.clone.refs_6_) | copy-start | bytes 393220
  24.5 9.0 %copy-start.12 = (bf16[256,256]{1,0:T(8,128)(2,1)S(1)}, bf16[256,256]{1,0:T(8,128)(2,1)}, u32[]{:S(2)}) copy-start(bf16[256,256]{1,0:T(8,128)(2,1)} %constant.35.clone.refs_7_) | copy-start | bytes 393220
  24.5 8.9 %collective-permute-start.5 = (f32[272,256]{1,0:T(8,128)S(1)}, f32[272,256]{1,0:T(8,128)S(1)}, u32[]{:S(2)}, u32[]{:S(2)}) collective-permute-start(f32[272,256]{1,0:T(8,128)S(1)} %get-tuple-element.12), channel_id=1, source_target_pairs={{0,240},{1,241},{2,242},{3,243},{4,244},{5,245},{6,246},{7,247},{8... | collective-permute-start | bytes 835592 | tf_op jit(solution)/shard_map/ppermute | solution.py:356
  27.2 6.3 %collective-permute-start.6 = (f32[256,256]{1,0:T(8,128)S(1)}, f32[256,256]{1,0:T(8,128)S(1)}, u32[]{:S(2)}, u32[]{:S(2)}) collective-permute-start(f32[256,256]{1,0:T(8,128)S(1)} %shard_map.138), channel_id=1, source_target_pairs={{0,240},{1,241},{2,242},{3,243},{4,244},{5,245},{6,246},{7,247},{8... | collective-permute-start | bytes 786440 | tf_op jit(solution)/shard_map/ppermute | solution.py:356
  40.4 26.8 %copy-start.4 = (f32[16,4]{0,1:T(4,128)S(1)}, f32[16,4]{0,1:T(4,128)}, u32[]{:S(2)}) copy-start(f32[16,4]{0,1:T(4,128)} %param.19) | copy-start | bytes 772
  40.4 9.2 %collective-permute-start.13 = (f32[256,256]{1,0:T(8,128)S(1)}, f32[256,256]{1,0:T(8,128)S(1)}, u32[]{:S(2)}, u32[]{:S(2)}) collective-permute-start(f32[256,256]{1,0:T(8,128)S(1)} %get-tuple-element.14.refs_0_), channel_id=1, source_target_pairs={{0,1},{1,0},{2,3},{3,2},{4,5},{5,4},{6,7},{7,6},{8,9},{9,8},{10,11... | collective-permute-start | bytes 786440 | tf_op jit(solution)/shard_map/ppermute | solution.py:356
  42.9 7.0 %collective-permute-start.9 = (f32[256,256]{1,0:T(8,128)S(1)}, f32[256,256]{1,0:T(8,128)S(1)}, u32[]{:S(2)}, u32[]{:S(2)}) collective-permute-start(f32[256,256]{1,0:T(8,128)S(1)} %get-tuple-element.13.refs_0_), channel_id=1, source_target_pairs={{0,16},{1,17},{2,18},{3,19},{4,20},{5,21},{6,22},{7,23},{8,24},{9,... | collective-permute-start | bytes 786440 | tf_op jit(solution)/shard_map/ppermute | solution.py:356
  42.9 9.5 %collective-permute-start.10 = (f32[256,256]{1,0:T(8,128)S(1)}, f32[256,256]{1,0:T(8,128)S(1)}, u32[]{:S(2)}, u32[]{:S(2)}) collective-permute-start(f32[256,256]{1,0:T(8,128)S(1)} %get-tuple-element.13.refs_0_), channel_id=1, source_target_pairs={{0,1},{1,0},{2,3},{3,2},{4,5},{5,4},{6,7},{7,6},{8,9},{9,8},{10,11... | collective-permute-start | bytes 786440 | tf_op jit(solution)/shard_map/ppermute | solution.py:356
  43.0 9.7 %collective-permute-start.14 = (f32[256,256]{1,0:T(8,128)S(1)}, f32[256,256]{1,0:T(8,128)S(1)}, u32[]{:S(2)}, u32[]{:S(2)}) collective-permute-start(f32[256,256]{1,0:T(8,128)S(1)} %get-tuple-element.14.refs_0_), channel_id=1, source_target_pairs={{0,16},{1,17},{2,18},{3,19},{4,20},{5,21},{6,22},{7,23},{8,24},{9,... | collective-permute-start | bytes 786440 | tf_op jit(solution)/shard_map/ppermute | solution.py:356
  49.6 7.0 %collective-permute-start.15 = (f32[256,256]{1,0:T(8,128)S(1)}, f32[256,256]{1,0:T(8,128)S(1)}, u32[]{:S(2)}, u32[]{:S(2)}) collective-permute-start(f32[256,256]{1,0:T(8,128)S(1)} %collective-permute-done.13.refs_1_), channel_id=1, source_target_pairs={{0,16},{1,17},{2,18},{3,19},{4,20},{5,21},{6,22},{7,23},{8,24},{9,... | collective-permute-start | bytes 786440 | tf_op jit(solution)/shard_map/ppermute | solution.py:356
  50.5 10.1 %collective-permute-start.12 = (f32[256,256]{1,0:T(8,128)S(1)}, f32[256,256]{1,0:T(8,128)S(1)}, u32[]{:S(2)}, u32[]{:S(2)}) collective-permute-start(f32[256,256]{1,0:T(8,128)S(1)} %shard_map.142), channel_id=1, source_target_pairs={{0,2},{1,3},{2,4},{3,5},{4,6},{5,7},{6,9},{7,8},{8,10},{9,11},{10,... | collective-permute-start | bytes 786440 | tf_op jit(solution)/shard_map/ppermute | solution.py:356
  52.4 20.8 %collective-permute-start.11 = (f32[256,256]{1,0:T(8,128)S(1)}, f32[256,256]{1,0:T(8,128)S(1)}, u32[]{:S(2)}, u32[]{:S(2)}) collective-permute-start(f32[256,256]{1,0:T(8,128)S(1)} %collective-permute-done.10.own_p), channel_id=1, source_target_pairs={{0,16},{1,17},{2,18},{3,19},{4,20},{5,21},{6,22},{7,23},{8,24},{9,... | collective-permute-start | bytes 786440 | tf_op jit(solution)/shard_map/ppermute | solution.py:356
  57.3 18.2 %collective-permute-start.17 = (f32[256,256]{1,0:T(8,128)S(1)}, f32[256,256]{1,0:T(8,128)S(1)}, u32[]{:S(2)}, u32[]{:S(2)}) collective-permute-start(f32[256,256]{1,0:T(8,128)S(1)} %shard_map.145), channel_id=1, source_target_pairs={{0,2},{1,3},{2,4},{3,5},{4,6},{5,7},{6,9},{7,8},{8,10},{9,11},{10,... | collective-permute-start | bytes 786440 | tf_op jit(solution)/shard_map/ppermute | solution.py:356
  60.6 14.9 %collective-permute-start.16 = (f32[256,256]{1,0:T(8,128)S(1)}, f32[256,256]{1,0:T(8,128)S(1)}, u32[]{:S(2)}, u32[]{:S(2)}) collective-permute-start(f32[256,256]{1,0:T(8,128)S(1)} %collective-permute-done.12.left_0), channel_id=1, source_target_pairs={{0,1},{1,0},{2,3},{3,2},{4,5},{5,4},{6,7},{7,6},{8,9},{9,8},{10,11... | collective-permute-start | bytes 786440 | tf_op jit(solution)/shard_map/ppermute | solution.py:356
  62.9 4.4 %collective-permute-start.4 = (f32[16,256]{1,0:T(8,128)S(1)}, f32[16,256]{1,0:T(8,128)S(1)}, u32[]{:S(2)}, u32[]{:S(2)}) collective-permute-start(f32[16,256]{1,0:T(8,128)S(1)} %get-tuple-element.11), channel_id=1, source_target_pairs={{0,16},{1,17},{2,18},{3,19},{4,20},{5,21},{6,22},{7,23},{8,24},{9,... | collective-permute-start | bytes 49160 | tf_op jit(solution)/shard_map/ppermute | solution.py:356

commit v3 on v2

--- a/solution.py
+++ b/solution.py
@@ -27,12 +27,11 @@
         return (a * n_ty + b) * 2 + m
 
     def perm(move):
-        return [
-            (lin(a, b, m), lin(*move(a, b, m)))
-            for a in range(n_tx)
-            for b in range(n_ty)
-            for m in range(2)
+        pairs = [
+            ((a, b, m), move(a, b, m)) for a in range(n_tx) for b in range(n_ty) for m in range(2)
         ]
+        near = [(s, t) for s, t in pairs if abs(s[0] - t[0]) <= 1 and abs(s[1] - t[1]) <= 1]
+        return [(lin(*s), lin(*t)) for s, t in near]
 
     def side(b, d, m):
         other = (b + d) % n_ty
@@ -246,19 +245,7 @@
     out[:, nxt] = out[:, nxt] - step_size * jnp.where(keep, value, 0.0)
 
 
-def take_all(out, offs, above, refs, skip=0):
-    m = lax.axis_index("mode")
-    row = iota(0)
-    n = len(refs) // 2
-    for k, slot in enumerate((m, 1 - m)[skip : skip + n]):
-        spot = place(offs, slot)
-        take(out, refs[k], spot, row >= spot[0])
-        spot = place(above, slot)
-        take(out, refs[n + k], spot, (row < spot[0]) & (lax.axis_index("tx") > 0))
-
-
-def prior_body(c, filt, offs, above, obj, right, left, up, down, *refs):
-    out = refs[-1]
+def prior_body(c, filt, offs, obj, right, left, up, down, own, out):
     tx, ty = lax.axis_index("tx"), lax.axis_index("ty")
     n_tx, n_ty = lax.axis_size("tx"), lax.axis_size("ty")
     cols = obj.shape[2]
@@ -273,6 +260,7 @@
         one_right = jnp.where(lane == cols - 1, after, pltpu.roll(x, cols - 1, 1))
         return one_left, one_right
 
+    spot = place(offs, lax.axis_index("mode"))
     x = obj[c]
     after = jnp.where(ty == n_ty - 1, 0.0, right[:, 0:1])
     edge = jnp.broadcast_to(left[c : c + 1, :], (128, W)).T
@@ -314,13 +302,23 @@
         in_row & in_col, g[3][0] * xul + g[3][1] * xu + g[3][2] * xl + g[3][3] * x, 0.0
     )
     out[...] = x - step_size * total
-    take_all(out, offs, above, refs[:-1])
-
-
-def mid_body(offs, above, base, own_p, up_p, left_0, done, out, first):
+    take(out, own, spot, iota(0) >= spot[0])
+
+
+def fold_body(offs, above, base, own_p, up_m, up_p, out):
+    m = lax.axis_index("mode")
+    row = iota(0)
+    mine = place(offs, 1 - m)
+    out[...] = base[...]
+    take(out, own_p, mine, row >= mine[0])
+    for ref, slot in ((up_m, m), (up_p, 1 - m)):
+        over = place(above, slot)
+        take(out, ref, over, (row < over[0]) & (lax.axis_index("tx") > 0))
+
+
+def mid_body(offs, above, base, own_p, up_m, up_p, left_0, done, out, first):
     part = out.at[0]
-    part[...] = base[...]
-    take_all(part, offs, above, (own_p, up_p), 1)
+    fold_body(offs, above, base, own_p, up_m, up_p, part)
     first[0] = part[:, 0:W] - step_size * jnp.where(lax.axis_index("ty") > 0, left_0[...], 0.0)
     out[1] = done[...]
     first[1] = done[:, 0:W]
@@ -396,14 +394,13 @@
     )(offs, counts, obj, *right, below_0, below_1, probe, probe_b, probe_c, meas, *tabs)
     p1, b0 = go(g1, "swap"), go(g0, "down")
     p0, b1 = go(g0, "swap"), go(g1, "down")
+    base = [
+        call(
+            functools.partial(prior_body, c), (rows, cols), [SMEM] * 2 + [VMEM] * 6, 12, 1 << 27, 8 << 20
+        )(filt, offs, obj, right[c], left, over, below_1, g)
+        for c, g in ((0, g0), (1, g1))
+    ]
     c1, c0 = go(p1, "down"), go(p0, "down")
-
-    def prior(c, *args):
-        specs = [SMEM] * 3 + [VMEM] * (5 + len(args))
-        kernel = call(functools.partial(prior_body, c), (rows, cols), specs, 12, 1 << 27, 8 << 20)
-        return kernel(filt, offs, above, obj, right[c], left, over, below_1, *args)
-
-    base = [prior(0, g0, b0), prior(1, g1, p1, b1, c1)]
 
     def spill(n, *args):
         specs = [SMEM, SMEM] + [VMEM] * (2 * n)
@@ -414,9 +411,12 @@
     left_p0 = go(left_m0, "swap")
     left_1 = go(spill(2, g1, p1, b1, c1), "right")
     any_space = pl.BlockSpec(memory_space=pl.ANY)
+    fold = call(fold_body, (rows, cols), [SMEM, SMEM] + [VMEM] * 4, 8, 1 << 20, 4 << 20)(
+        offs, above, base[1], p1, b1, c1
+    )
     mid, first = call(
-        mid_body, [whole, (2, W, W)], [SMEM, SMEM] + [VMEM] * 5, 12, 1 << 24, 10 << 20
-    )(offs, above, base[0], p0, c0, left_m0, base[1])
+        mid_body, [whole, (2, W, W)], [SMEM, SMEM] + [VMEM] * 6, 12, 1 << 24, 10 << 20
+    )(offs, above, base[0], p0, b0, c0, left_m0, fold)
     return call(
         final_body,
         whole,

time: 76.7 us -> 86.4 us (1.13)
  the two profiles are of different devices: /device:TPU:4 before, /device:TPU:132 now
where the time goes in v3:
time: 86.4 us; the launch traced here: 85.9 us
  starting transfers between devices  43.1 us (50%)
  Pallas kernels  19.9 us (23%)
  waiting for transfers between devices  18.4 us (21%)
  local copies, waits for them, and re-layouts  3.24 us (4%)
  between operations  1.2 us (1%)
    ppermute x18, starting transfers between devices, go(): return lax.ppermute(value, axes, ring[where])  43.1 us
    ppermute x18, waiting for transfers between devices, go(): return lax.ppermute(value, axes, ring[where])  18.4 us
    pallas_call x1, Pallas kernels, local(): call(main_body, [piece] * 2, [SMEM, SMEM] + [VMEM] * 17, 16, 5 << 30, 12...  6.93 us
    pallas_call x2, Pallas kernels, local(): call(functools.partial(prior_body, c), (rows, cols), [SMEM] * 2 + [VMEM]...  5.2 us
    pallas_call x1, Pallas kernels, local(): call(mid_body, [whole, (2, W, W)], [SMEM, SMEM] + [VMEM] * 6, 12, 1 << 24...  2.49 us
  transfers between devices with their start and end apart: 18, of which 6 were waited for; matrix products, arithmetic and copies ran while one was open for 2% of the time, Pallas kernels for 14%

profile of v3, /device:TPU:132, one launch (start us, length us, event | category | flops | bytes accessed | tf_op | source)
XLA Modules:
  0.0 85.9 jit_solution(10652918420014470843)
XLA Ops:
  0.0 1.2 %constant_dynamic-slice_fusion = f32[1,2,256,256]{3,2,1,0:T(8,128)S(1)} fusion(f32[2,2,256,256]{3,2,1,0:T(8,128)} %probe_a.1, s32[]{:T(128)S(6)} %select_n.3), kind=kLoop, calls=%fused_computation.2 | loop fusion | bytes 1048580 | tf_op jit(solution)/shard_map/dynamic_slice | solution.py:365
  1.2 1.3 %collective-permute-start.7 = (f32[1,2,256,256]{3,2,1,0:T(8,128)S(1)}, f32[1,2,256,256]{3,2,1,0:T(8,128)S(1)}, u32[]{:S(2)}, u32[]{:S(2)}) collective-permute-start(f32[1,2,256,256]{3,2,1,0:T(8,128)S(1)} %constant_dynamic-slice_fusion), channel_id=1, source_target_pairs={{0,1},{1,0},{2,3},{3,2},{4,5},{5,4},{6,7},{7,6},{8,9},{9,8},{10,11... | collective-permute-start | bytes 1572872 | tf_op jit(solution)/shard_map/ppermute | solution.py:354
  2.5 1.0 %slice_bitcast_fusion.1 = f32[256,256]{1,0:T(8,128)S(1)} fusion(f32[2,256,1024]{2,1,0:T(8,128)} %obj.11), kind=kLoop, calls=%fused_computation.1 | loop fusion | bytes 524288 | tf_op jit(solution)/shard_map/squeeze | solution.py:362
  3.5 4.2 %collective-permute-start.1 = (f32[256,256]{1,0:T(8,128)S(1)}, f32[256,256]{1,0:T(8,128)S(1)}, u32[]{:S(2)}, u32[]{:S(2)}) collective-permute-start(f32[256,256]{1,0:T(8,128)S(1)} %slice_bitcast_fusion.1), channel_id=1, source_target_pairs={{2,0},{3,1},{4,2},{5,3},{6,4},{7,5},{8,7},{9,6},{10,8},{11,9},{12,... | collective-permute-start | bytes 786440 | tf_op jit(solution)/shard_map/ppermute | solution.py:354
  7.7 1.0 %slice_bitcast_fusion = f32[256,256]{1,0:T(8,128)S(1)} fusion(f32[2,256,1024]{2,1,0:T(8,128)} %obj.11), kind=kLoop, calls=%fused_computation | loop fusion | bytes 524288 | tf_op jit(solution)/shard_map/squeeze | solution.py:363
  8.7 2.7 %collective-permute-start.3 = (f32[256,256]{1,0:T(8,128)S(1)}, f32[256,256]{1,0:T(8,128)S(1)}, u32[]{:S(2)}, u32[]{:S(2)}) collective-permute-start(f32[256,256]{1,0:T(8,128)S(1)} %slice_bitcast_fusion), channel_id=1, source_target_pairs={{2,0},{3,1},{4,2},{5,3},{6,4},{7,5},{8,7},{9,6},{10,8},{11,9},{12,... | collective-permute-start | bytes 786440 | tf_op jit(solution)/shard_map/ppermute | solution.py:354
  11.4 3.6 %collective-permute-done.7.probe_b = f32[1,2,256,256]{3,2,1,0:T(8,128)S(1)} collective-permute-done((f32[1,2,256,256]{3,2,1,0:T(8,128)S(1)}, f32[1,2,256,256]{3,2,1,0:T(8,128)S(1)}, u32[]{:S(2)}, u32[]{:S(2)}) %collective-permute-start.7) | collective-permute-done | bytes 524320 | tf_op jit(solution)/shard_map/ppermute | solution.py:354
  15.0 0.1 shard_map.136
  15.1 3.5 %collective-permute-start.2 = (f32[8,256]{1,0:T(8,128)S(1)}, f32[8,256]{1,0:T(8,128)S(1)}, u32[]{:S(2)}, u32[]{:S(2)}) collective-permute-start(f32[8,256]{1,0:T(8,128)S(1)} %shard_map.136), channel_id=1, source_target_pairs={{0,2},{1,3},{2,4},{3,5},{4,6},{5,7},{6,9},{7,8},{8,10},{9,11},{10,... | collective-permute-start | bytes 24584 | tf_op jit(solution)/shard_map/ppermute | solution.py:354
  18.6 0.0 copy-start.1
  18.6 2.3 %collective-permute-start = (s32[2,2]{1,0:T(2,128)S(1)}, s32[2,2]{1,0:T(2,128)S(1)}, u32[]{:S(2)}, u32[]{:S(2)}) collective-permute-start(s32[2,2]{1,0:T(2,128)S(1)} %bitcast.6), channel_id=1, source_target_pairs={{0,16},{1,17},{2,18},{3,19},{4,20},{5,21},{6,22},{7,23},{8,24},{9,... | collective-permute-start | bytes 56 | tf_op jit(solution)/shard_map/ppermute | solution.py:354
  20.9 4.0 %collective-permute-done.above = s32[2,2]{1,0:T(2,128)S(1)} collective-permute-done((s32[2,2]{1,0:T(2,128)S(1)}, s32[2,2]{1,0:T(2,128)S(1)}, u32[]{:S(2)}, u32[]{:S(2)}) %collective-permute-start) | collective-permute-done | bytes 48 | tf_op jit(solution)/shard_map/ppermute | solution.py:354
  24.9 0.6 shard_map.137
  25.5 0.0 copy-start.5
  25.5 0.0 copy-start.6
  25.6 0.0 copy-start.7
  25.6 0.0 copy-start.8
  25.6 0.0 copy-start.9
  25.6 0.0 copy-start.10
  25.6 0.0 copy-start.11
  25.6 0.0 copy-start.12
  25.6 2.1 %collective-permute-start.5 = (f32[272,256]{1,0:T(8,128)S(1)}, f32[272,256]{1,0:T(8,128)S(1)}, u32[]{:S(2)}, u32[]{:S(2)}) collective-permute-start(f32[272,256]{1,0:T(8,128)S(1)} %get-tuple-element.12), channel_id=1, source_target_pairs={{16,0},{17,1},{18,2},{19,3},{20,4},{21,5},{22,6},{23,7},{24,8},{25... | collective-permute-start | bytes 835592 | tf_op jit(solution)/shard_map/ppermute | solution.py:354
  27.7 0.6 shard_map.138
  28.3 1.9 %collective-permute-start.6 = (f32[256,256]{1,0:T(8,128)S(1)}, f32[256,256]{1,0:T(8,128)S(1)}, u32[]{:S(2)}, u32[]{:S(2)}) collective-permute-start(f32[256,256]{1,0:T(8,128)S(1)} %shard_map.138), channel_id=1, source_target_pairs={{16,0},{17,1},{18,2},{19,3},{20,4},{21,5},{22,6},{23,7},{24,8},{25... | collective-permute-start | bytes 786440 | tf_op jit(solution)/shard_map/ppermute | solution.py:354
  30.9 0.7 shard_map.139.meas
  31.6 3.0 %collective-permute-done.6.below_0 = f32[256,256]{1,0:T(8,128)S(1)} collective-permute-done((f32[256,256]{1,0:T(8,128)S(1)}, f32[256,256]{1,0:T(8,128)S(1)}, u32[]{:S(2)}, u32[]{:S(2)}) %collective-permute-start.6) | collective-permute-done | bytes 262176 | tf_op jit(solution)/shard_map/ppermute | solution.py:354
  34.6 6.9 %shard_map.140 = (f32[256,256]{1,0:T(8,128)S(1)}, f32[256,256]{1,0:T(8,128)S(1)}) custom-call(s32[2,2]{1,0:T(2,128)S(1)} %bitcast.7, s32[1,1]{1,0:T(1,128)S(6)} %copy.17.counts, f32[2,256,1024]{2,1,0:T(8,128)S(1)} %copy-done, f32[256,256]{1,0:T(8,128)S(1)} %collective-permute-done.1.refs_0_.right_0.right, ...), custom_call_target="tpu_custom_call" | custom-call | flops 5368709120 | bytes 12582912 | tf_op jit(solution)/shard_map/pallas_call | solution.py:386
  41.6 0.0 copy-start.4
  41.6 1.3 %collective-permute-start.13 = (f32[256,256]{1,0:T(8,128)S(1)}, f32[256,256]{1,0:T(8,128)S(1)}, u32[]{:S(2)}, u32[]{:S(2)}) collective-permute-start(f32[256,256]{1,0:T(8,128)S(1)} %get-tuple-element.14.own.refs_0_), channel_id=1, source_target_pairs={{0,1},{1,0},{2,3},{3,2},{4,5},{5,4},{6,7},{7,6},{8,9},{9,8},{10,11... | collective-permute-start | bytes 786440 | tf_op jit(solution)/shard_map/ppermute | solution.py:354
  42.9 3.6 %collective-permute-start.10 = (f32[256,256]{1,0:T(8,128)S(1)}, f32[256,256]{1,0:T(8,128)S(1)}, u32[]{:S(2)}, u32[]{:S(2)}) collective-permute-start(f32[256,256]{1,0:T(8,128)S(1)} %get-tuple-element.13.own.refs_0_), channel_id=1, source_target_pairs={{0,16},{1,17},{2,18},{3,19},{4,20},{5,21},{6,22},{7,23},{8,24},{9,... | collective-permute-start | bytes 786440 | tf_op jit(solution)/shard_map/ppermute | solution.py:354
  46.5 0.9 %collective-permute-start.9 = (f32[256,256]{1,0:T(8,128)S(1)}, f32[256,256]{1,0:T(8,128)S(1)}, u32[]{:S(2)}, u32[]{:S(2)}) collective-permute-start(f32[256,256]{1,0:T(8,128)S(1)} %get-tuple-element.13.own.refs_0_), channel_id=1, source_target_pairs={{0,1},{1,0},{2,3},{3,2},{4,5},{5,4},{6,7},{7,6},{8,9},{9,8},{10,11... | collective-permute-start | bytes 786440 | tf_op jit(solution)/shard_map/ppermute | solution.py:354
  47.4 1.9 %collective-permute-start.14 = (f32[256,256]{1,0:T(8,128)S(1)}, f32[256,256]{1,0:T(8,128)S(1)}, u32[]{:S(2)}, u32[]{:S(2)}) collective-permute-start(f32[256,256]{1,0:T(8,128)S(1)} %get-tuple-element.14.own.refs_0_), channel_id=1, source_target_pairs={{0,16},{1,17},{2,18},{3,19},{4,20},{5,21},{6,22},{7,23},{8,24},{9,... | collective-permute-start | bytes 786440 | tf_op jit(solution)/shard_map/ppermute | solution.py:354
  49.3 0.6 collective-permute-done.13.own_p.refs_1_
  49.9 3.7 %collective-permute-start.15 = (f32[256,256]{1,0:T(8,128)S(1)}, f32[256,256]{1,0:T(8,128)S(1)}, u32[]{:S(2)}, u32[]{:S(2)}) collective-permute-start(f32[256,256]{1,0:T(8,128)S(1)} %collective-permute-done.13.own_p.refs_1_), channel_id=1, source_target_pairs={{0,16},{1,17},{2,18},{3,19},{4,20},{5,21},{6,22},{7,23},{8,24},{9,... | collective-permute-start | bytes 786440 | tf_op jit(solution)/shard_map/ppermute | solution.py:354
  53.6 0.7 shard_map.142
  54.3 3.5 %collective-permute-start.12 = (f32[256,256]{1,0:T(8,128)S(1)}, f32[256,256]{1,0:T(8,128)S(1)}, u32[]{:S(2)}, u32[]{:S(2)}) collective-permute-start(f32[256,256]{1,0:T(8,128)S(1)} %shard_map.142), channel_id=1, source_target_pairs={{0,2},{1,3},{2,4},{3,5},{4,6},{5,7},{6,9},{7,8},{8,10},{9,11},{10,... | collective-permute-start | bytes 786440 | tf_op jit(solution)/shard_map/ppermute | solution.py:354
  57.8 2.5 %collective-permute-start.11 = (f32[256,256]{1,0:T(8,128)S(1)}, f32[256,256]{1,0:T(8,128)S(1)}, u32[]{:S(2)}, u32[]{:S(2)}) collective-permute-start(f32[256,256]{1,0:T(8,128)S(1)} %collective-permute-done.9.own_p), channel_id=1, source_target_pairs={{0,16},{1,17},{2,18},{3,19},{4,20},{5,21},{6,22},{7,23},{8,24},{9,... | collective-permute-start | bytes 786440 | tf_op jit(solution)/shard_map/ppermute | solution.py:354
  60.4 0.7 shard_map.146
  61.1 3.2 %collective-permute-start.17 = (f32[256,256]{1,0:T(8,128)S(1)}, f32[256,256]{1,0:T(8,128)S(1)}, u32[]{:S(2)}, u32[]{:S(2)}) collective-permute-start(f32[256,256]{1,0:T(8,128)S(1)} %shard_map.146), channel_id=1, source_target_pairs={{0,2},{1,3},{2,4},{3,5},{4,6},{5,7},{6,9},{7,8},{8,10},{9,11},{10,... | collective-permute-start | bytes 786440 | tf_op jit(solution)/shard_map/ppermute | solution.py:354
  64.3 3.1 %collective-permute-done.12.left_0 = f32[256,256]{1,0:T(8,128)S(1)} collective-permute-done((f32[256,256]{1,0:T(8,128)S(1)}, f32[256,256]{1,0:T(8,128)S(1)}, u32[]{:S(2)}, u32[]{:S(2)}) %collective-permute-start.12) | collective-permute-done | bytes 262176 | tf_op jit(solution)/shard_map/ppermute | solution.py:354
  67.4 2.4 %collective-permute-start.16 = (f32[256,256]{1,0:T(8,128)S(1)}, f32[256,256]{1,0:T(8,128)S(1)}, u32[]{:S(2)}, u32[]{:S(2)}) collective-permute-start(f32[256,256]{1,0:T(8,128)S(1)} %collective-permute-done.12.left_0), channel_id=1, source_target_pairs={{0,1},{1,0},{2,3},{3,2},{4,5},{5,4},{6,7},{7,6},{8,9},{9,8},{10,11... | collective-permute-start | bytes 786440 | tf_op jit(solution)/shard_map/ppermute | solution.py:354
  69.8 2.1 %collective-permute-start.4 = (f32[16,256]{1,0:T(8,128)S(1)}, f32[16,256]{1,0:T(8,128)S(1)}, u32[]{:S(2)}, u32[]{:S(2)}) collective-permute-start(f32[16,256]{1,0:T(8,128)S(1)} %get-tuple-element.11), channel_id=1, source_target_pairs={{0,16},{1,17},{2,18},{3,19},{4,20},{5,21},{6,22},{7,23},{8,24},{9,... | collective-permute-start | bytes 49160 | tf_op jit(solution)/shard_map/ppermute | solution.py:354
  71.9 4.2 %collective-permute-done.4.up = f32[16,256]{1,0:T(8,128)S(1)} collective-permute-done((f32[16,256]{1,0:T(8,128)S(1)}, f32[16,256]{1,0:T(8,128)S(1)}, u32[]{:S(2)}, u32[]{:S(2)}) %collective-permute-start.4) | collective-permute-done | bytes 16416 | tf_op jit(solution)/shard_map/ppermute | solution.py:354
  76.1 2.6 %shard_map.143.base = f32[256,1024]{1,0:T(8,128)S(1)} custom-call(f32[4,16]{1,0:T(4,128)S(1)} %bitcast.14, s32[2,2]{1,0:T(2,128)S(1)} %bitcast.10, f32[2,256,1024]{2,1,0:T(8,128)S(1)} %copy-done, f32[256,256]{1,0:T(8,128)S(1)} %collective-permute-done.3.refs_1_.right_1.right, f32[8,256]{1,0:T(8,128)S(1)} %collective-permute-done.2.refs_2_.left, ...), custom_call_target="tpu_custom_call" | custom-call | flops 134217728 | bytes 8388608 | tf_op jit(solution)/shard_map/pallas_call | solution.py:398
  78.7 2.6 %shard_map.141.base = f32[256,1024]{1,0:T(8,128)S(1)} custom-call(f32[4,16]{1,0:T(4,128)S(1)} %bitcast.15, s32[2,2]{1,0:T(2,128)S(1)} %bitcast.11, f32[2,256,1024]{2,1,0:T(8,128)S(1)} %copy-done, f32[256,256]{1,0:T(8,128)S(1)} %collective-permute-done.1.refs_0_.right_0.right, f32[8,256]{1,0:T(8,128)S(1)} %collective-permute-done.2.refs_2_.left, ...), custom_call_target="tpu_custom_call" | custom-call | flops 134217728 | bytes 8388608 | tf_op jit(solution)/shard_map/pallas_call | solution.py:398
  81.3 1.0 %shard_map.144.done = f32[256,1024]{1,0:T(8,128)S(1)} custom-call(s32[2,2]{1,0:T(2,128)S(1)} %bitcast.12, s32[2,2]{1,0:T(2,128)S(1)} %collective-permute-done.above, f32[256,1024]{1,0:T(8,128)S(1)} %shard_map.143.base, f32[256,256]{1,0:T(8,128)S(1)} %collective-permute-done.13.own_p.refs_1_, f32[256,256]{1,0:T(8,128)S(1)} %collective-permute-done.14.up_m.refs_2_, ...), custom_call_target="tpu_custom_call" | custom-call | flops 1048576 | bytes 4194304 | tf_op jit(solution)/shard_map/pallas_call | solution.py:414
  82.4 2.5 %shard_map.145 = (f32[2,256,1024]{2,1,0:T(8,128)}, f32[2,256,256]{2,1,0:T(8,128)S(1)}) custom-call(s32[2,2]{1,0:T(2,128)S(1)} %bitcast.13, s32[2,2]{1,0:T(2,128)S(1)} %collective-permute-done.above, f32[256,1024]{1,0:T(8,128)S(1)} %shard_map.141.base, f32[256,256]{1,0:T(8,128)S(1)} %collective-permute-done.9.own_p, ...), custom_call_target="tpu_custom_call" | custom-call | flops 16777216 | bytes 10485760 | tf_op jit(solution)/shard_map/pallas_call | solution.py:417
  84.9 0.8 shard_map.147
  (29 shorter events, 0.1 us)
Async XLA Ops:
  0.0 15.0 %copy-start = (f32[2,256,1024]{2,1,0:T(8,128)S(1)}, f32[2,256,1024]{2,1,0:T(8,128)}, u32[]{:S(2)}) copy-start(f32[2,256,1024]{2,1,0:T(8,128)} %obj.11) | copy-start | bytes 6291460
  0.0 18.6 %copy-start.3 = (s32[1,1,2,2]{3,2,1,0:T(2,128)S(1)}, s32[1,1,2,2]{3,2,1,0:T(2,128)}, u32[]{:S(2)}) copy-start(s32[1,1,2,2]{3,2,1,0:T(2,128)} %param.17) | copy-start | bytes 52
  1.2 13.8 %collective-permute-start.7 = (f32[1,2,256,256]{3,2,1,0:T(8,128)S(1)}, f32[1,2,256,256]{3,2,1,0:T(8,128)S(1)}, u32[]{:S(2)}, u32[]{:S(2)}) collective-permute-start(f32[1,2,256,256]{3,2,1,0:T(8,128)S(1)} %constant_dynamic-slice_fusion), channel_id=1, source_target_pairs={{0,1},{1,0},{2,3},{3,2},{4,5},{5,4},{6,7},{7,6},{8,9},{9,8},{10,11... | collective-permute-start | bytes 1572872 | tf_op jit(solution)/shard_map/ppermute | solution.py:354
  3.5 21.4 %collective-permute-start.1 = (f32[256,256]{1,0:T(8,128)S(1)}, f32[256,256]{1,0:T(8,128)S(1)}, u32[]{:S(2)}, u32[]{:S(2)}) collective-permute-start(f32[256,256]{1,0:T(8,128)S(1)} %slice_bitcast_fusion.1), channel_id=1, source_target_pairs={{2,0},{3,1},{4,2},{5,3},{6,4},{7,5},{8,7},{9,6},{10,8},{11,9},{12,... | collective-permute-start | bytes 786440 | tf_op jit(solution)/shard_map/ppermute | solution.py:354
  8.7 16.2 %collective-permute-start.3 = (f32[256,256]{1,0:T(8,128)S(1)}, f32[256,256]{1,0:T(8,128)S(1)}, u32[]{:S(2)}, u32[]{:S(2)}) collective-permute-start(f32[256,256]{1,0:T(8,128)S(1)} %slice_bitcast_fusion), channel_id=1, source_target_pairs={{2,0},{3,1},{4,2},{5,3},{6,4},{7,5},{8,7},{9,6},{10,8},{11,9},{12,... | collective-permute-start | bytes 786440 | tf_op jit(solution)/shard_map/ppermute | solution.py:354
  15.0 19.6 %collective-permute-start.8 = (f32[1,2,256,256]{3,2,1,0:T(8,128)S(1)}, f32[1,2,256,256]{3,2,1,0:T(8,128)S(1)}, u32[]{:S(2)}, u32[]{:S(2)}) collective-permute-start(f32[1,2,256,256]{3,2,1,0:T(8,128)S(1)} %collective-permute-done.7.probe_b), channel_id=1, source_target_pairs={{0,16},{1,17},{2,18},{3,19},{4,20},{5,21},{6,22},{7,23},{8,24},{9,... | collective-permute-start | bytes 1572872 | tf_op jit(solution)/shard_map/ppermute | solution.py:354
  15.1 9.8 %collective-permute-start.2 = (f32[8,256]{1,0:T(8,128)S(1)}, f32[8,256]{1,0:T(8,128)S(1)}, u32[]{:S(2)}, u32[]{:S(2)}) collective-permute-start(f32[8,256]{1,0:T(8,128)S(1)} %shard_map.136), channel_id=1, source_target_pairs={{0,2},{1,3},{2,4},{3,5},{4,6},{5,7},{6,9},{7,8},{8,10},{9,11},{10,... | collective-permute-start | bytes 24584 | tf_op jit(solution)/shard_map/ppermute | solution.py:354
  18.6 12.3 %copy-start.1 = (f32[1,1,2,256,256]{4,3,2,1,0:T(8,128)S(1)}, f32[1,1,2,256,256]{4,3,2,1,0:T(8,128)}, u32[]{:S(2)}) copy-start(f32[1,1,2,256,256]{4,3,2,1,0:T(8,128)} %meas.1) | copy-start | bytes 1572868
  18.6 6.2 %collective-permute-start = (s32[2,2]{1,0:T(2,128)S(1)}, s32[2,2]{1,0:T(2,128)S(1)}, u32[]{:S(2)}, u32[]{:S(2)}) collective-permute-start(s32[2,2]{1,0:T(2,128)S(1)} %bitcast.6), channel_id=1, source_target_pairs={{0,16},{1,17},{2,18},{3,19},{4,20},{5,21},{6,22},{7,23},{8,24},{9,... | collective-permute-start | bytes 56 | tf_op jit(solution)/shard_map/ppermute | solution.py:354
  25.5 9.0 %copy-start.2 = (f32[2,2,256,256]{3,2,1,0:T(8,128)S(1)}, f32[2,2,256,256]{3,2,1,0:T(8,128)}, u32[]{:S(2)}) copy-start(f32[2,2,256,256]{3,2,1,0:T(8,128)} %probe_a.1) | copy-start | bytes 3145732
  25.5 9.0 %copy-start.5 = (bf16[256,256]{1,0:T(8,128)(2,1)S(1)}, bf16[256,256]{1,0:T(8,128)(2,1)}, u32[]{:S(2)}) copy-start(bf16[256,256]{1,0:T(8,128)(2,1)} %constant.28.clone.refs_0_) | copy-start | bytes 393220
  25.5 9.0 %copy-start.6 = (bf16[256,256]{1,0:T(8,128)(2,1)S(1)}, bf16[256,256]{1,0:T(8,128)(2,1)}, u32[]{:S(2)}) copy-start(bf16[256,256]{1,0:T(8,128)(2,1)} %constant.29.clone.refs_1_) | copy-start | bytes 393220
  25.6 9.0 %copy-start.7 = (bf16[256,256]{1,0:T(8,128)(2,1)S(1)}, bf16[256,256]{1,0:T(8,128)(2,1)}, u32[]{:S(2)}) copy-start(bf16[256,256]{1,0:T(8,128)(2,1)} %constant.30.clone.refs_2_) | copy-start | bytes 393220
  25.6 9.0 %copy-start.8 = (bf16[256,256]{1,0:T(8,128)(2,1)S(1)}, bf16[256,256]{1,0:T(8,128)(2,1)}, u32[]{:S(2)}) copy-start(bf16[256,256]{1,0:T(8,128)(2,1)} %constant.31.clone.refs_3_) | copy-start | bytes 393220
  25.6 9.0 %copy-start.9 = (bf16[256,256]{1,0:T(8,128)(2,1)S(1)}, bf16[256,256]{1,0:T(8,128)(2,1)}, u32[]{:S(2)}) copy-start(bf16[256,256]{1,0:T(8,128)(2,1)} %constant.32.clone.refs_4_) | copy-start | bytes 393220
  25.6 9.0 %copy-start.10 = (bf16[256,256]{1,0:T(8,128)(2,1)S(1)}, bf16[256,256]{1,0:T(8,128)(2,1)}, u32[]{:S(2)}) copy-start(bf16[256,256]{1,0:T(8,128)(2,1)} %constant.33.clone.refs_5_) | copy-start | bytes 393220
  25.6 9.0 %copy-start.11 = (bf16[256,256]{1,0:T(8,128)(2,1)S(1)}, bf16[256,256]{1,0:T(8,128)(2,1)}, u32[]{:S(2)}) copy-start(bf16[256,256]{1,0:T(8,128)(2,1)} %constant.34.clone.refs_6_) | copy-start | bytes 393220
  25.6 9.0 %copy-start.12 = (bf16[256,256]{1,0:T(8,128)(2,1)S(1)}, bf16[256,256]{1,0:T(8,128)(2,1)}, u32[]{:S(2)}) copy-start(bf16[256,256]{1,0:T(8,128)(2,1)} %constant.35.clone.refs_7_) | copy-start | bytes 393220
  25.6 8.9 %collective-permute-start.5 = (f32[272,256]{1,0:T(8,128)S(1)}, f32[272,256]{1,0:T(8,128)S(1)}, u32[]{:S(2)}, u32[]{:S(2)}) collective-permute-start(f32[272,256]{1,0:T(8,128)S(1)} %get-tuple-element.12), channel_id=1, source_target_pairs={{16,0},{17,1},{18,2},{19,3},{20,4},{21,5},{22,6},{23,7},{24,8},{25... | collective-permute-start | bytes 835592 | tf_op jit(solution)/shard_map/ppermute | solution.py:354
  28.3 6.2 %collective-permute-start.6 = (f32[256,256]{1,0:T(8,128)S(1)}, f32[256,256]{1,0:T(8,128)S(1)}, u32[]{:S(2)}, u32[]{:S(2)}) collective-permute-start(f32[256,256]{1,0:T(8,128)S(1)} %shard_map.138), channel_id=1, source_target_pairs={{16,0},{17,1},{18,2},{19,3},{20,4},{21,5},{22,6},{23,7},{24,8},{25... | collective-permute-start | bytes 786440 | tf_op jit(solution)/shard_map/ppermute | solution.py:354
  41.6 34.5 %copy-start.4 = (f32[16,4]{0,1:T(4,128)S(1)}, f32[16,4]{0,1:T(4,128)}, u32[]{:S(2)}) copy-start(f32[16,4]{0,1:T(4,128)} %param.19) | copy-start | bytes 772
  41.6 8.3 %collective-permute-start.13 = (f32[256,256]{1,0:T(8,128)S(1)}, f32[256,256]{1,0:T(8,128)S(1)}, u32[]{:S(2)}, u32[]{:S(2)}) collective-permute-start(f32[256,256]{1,0:T(8,128)S(1)} %get-tuple-element.14.own.refs_0_), channel_id=1, source_target_pairs={{0,1},{1,0},{2,3},{3,2},{4,5},{5,4},{6,7},{7,6},{8,9},{9,8},{10,11... | collective-permute-start | bytes 786440 | tf_op jit(solution)/shard_map/ppermute | solution.py:354
  42.9 10.7 %collective-permute-start.10 = (f32[256,256]{1,0:T(8,128)S(1)}, f32[256,256]{1,0:T(8,128)S(1)}, u32[]{:S(2)}, u32[]{:S(2)}) collective-permute-start(f32[256,256]{1,0:T(8,128)S(1)} %get-tuple-element.13.own.refs_0_), channel_id=1, source_target_pairs={{0,16},{1,17},{2,18},{3,19},{4,20},{5,21},{6,22},{7,23},{8,24},{9,... | collective-permute-start | bytes 786440 | tf_op jit(solution)/shard_map/ppermute | solution.py:354
  46.5 11.3 %collective-permute-start.9 = (f32[256,256]{1,0:T(8,128)S(1)}, f32[256,256]{1,0:T(8,128)S(1)}, u32[]{:S(2)}, u32[]{:S(2)}) collective-permute-start(f32[256,256]{1,0:T(8,128)S(1)} %get-tuple-element.13.own.refs_0_), channel_id=1, source_target_pairs={{0,1},{1,0},{2,3},{3,2},{4,5},{5,4},{6,7},{7,6},{8,9},{9,8},{10,11... | collective-permute-start | bytes 786440 | tf_op jit(solution)/shard_map/ppermute | solution.py:354
  47.4 13.0 %collective-permute-start.14 = (f32[256,256]{1,0:T(8,128)S(1)}, f32[256,256]{1,0:T(8,128)S(1)}, u32[]{:S(2)}, u32[]{:S(2)}) collective-permute-start(f32[256,256]{1,0:T(8,128)S(1)} %get-tuple-element.14.own.refs_0_), channel_id=1, source_target_pairs={{0,16},{1,17},{2,18},{3,19},{4,20},{5,21},{6,22},{7,23},{8,24},{9,... | collective-permute-start | bytes 786440 | tf_op jit(solution)/shard_map/ppermute | solution.py:354
  49.9 10.5 %collective-permute-start.15 = (f32[256,256]{1,0:T(8,128)S(1)}, f32[256,256]{1,0:T(8,128)S(1)}, u32[]{:S(2)}, u32[]{:S(2)}) collective-permute-start(f32[256,256]{1,0:T(8,128)S(1)} %collective-permute-done.13.own_p.refs_1_), channel_id=1, source_target_pairs={{0,16},{1,17},{2,18},{3,19},{4,20},{5,21},{6,22},{7,23},{8,24},{9,... | collective-permute-start | bytes 786440 | tf_op jit(solution)/shard_map/ppermute | solution.py:354
  54.3 13.2 %collective-permute-start.12 = (f32[256,256]{1,0:T(8,128)S(1)}, f32[256,256]{1,0:T(8,128)S(1)}, u32[]{:S(2)}, u32[]{:S(2)}) collective-permute-start(f32[256,256]{1,0:T(8,128)S(1)} %shard_map.142), channel_id=1, source_target_pairs={{0,2},{1,3},{2,4},{3,5},{4,6},{5,7},{6,9},{7,8},{8,10},{9,11},{10,... | collective-permute-start | bytes 786440 | tf_op jit(solution)/shard_map/ppermute | solution.py:354
  57.8 24.6 %collective-permute-start.11 = (f32[256,256]{1,0:T(8,128)S(1)}, f32[256,256]{1,0:T(8,128)S(1)}, u32[]{:S(2)}, u32[]{:S(2)}) collective-permute-start(f32[256,256]{1,0:T(8,128)S(1)} %collective-permute-done.9.own_p), channel_id=1, source_target_pairs={{0,16},{1,17},{2,18},{3,19},{4,20},{5,21},{6,22},{7,23},{8,24},{9,... | collective-permute-start | bytes 786440 | tf_op jit(solution)/shard_map/ppermute | solution.py:354
  61.1 23.8 %collective-permute-start.17 = (f32[256,256]{1,0:T(8,128)S(1)}, f32[256,256]{1,0:T(8,128)S(1)}, u32[]{:S(2)}, u32[]{:S(2)}) collective-permute-start(f32[256,256]{1,0:T(8,128)S(1)} %shard_map.146), channel_id=1, source_target_pairs={{0,2},{1,3},{2,4},{3,5},{4,6},{5,7},{6,9},{7,8},{8,10},{9,11},{10,... | collective-permute-start | bytes 786440 | tf_op jit(solution)/shard_map/ppermute | solution.py:354
  67.4 17.4 %collective-permute-start.16 = (f32[256,256]{1,0:T(8,128)S(1)}, f32[256,256]{1,0:T(8,128)S(1)}, u32[]{:S(2)}, u32[]{:S(2)}) collective-permute-start(f32[256,256]{1,0:T(8,128)S(1)} %collective-permute-done.12.left_0), channel_id=1, source_target_pairs={{0,1},{1,0},{2,3},{3,2},{4,5},{5,4},{6,7},{7,6},{8,9},{9,8},{10,11... | collective-permute-start | bytes 786440 | tf_op jit(solution)/shard_map/ppermute | solution.py:354
  69.8 6.3 %collective-permute-start.4 = (f32[16,256]{1,0:T(8,128)S(1)}, f32[16,256]{1,0:T(8,128)S(1)}, u32[]{:S(2)}, u32[]{:S(2)}) collective-permute-start(f32[16,256]{1,0:T(8,128)S(1)} %get-tuple-element.11), channel_id=1, source_target_pairs={{0,16},{1,17},{2,18},{3,19},{4,20},{5,21},{6,22},{7,23},{8,24},{9,... | collective-permute-start | bytes 49160 | tf_op jit(solution)/shard_map/ppermute | solution.py:354

commit v4 on v3

--- a/solution.py
+++ b/solution.py
@@ -27,11 +27,12 @@
         return (a * n_ty + b) * 2 + m
 
     def perm(move):
-        pairs = [
-            ((a, b, m), move(a, b, m)) for a in range(n_tx) for b in range(n_ty) for m in range(2)
+        return [
+            (lin(a, b, m), lin(*move(a, b, m)))
+            for a in range(n_tx)
+            for b in range(n_ty)
+            for m in range(2)
         ]
-        near = [(s, t) for s, t in pairs if abs(s[0] - t[0]) <= 1 and abs(s[1] - t[1]) <= 1]
-        return [(lin(*s), lin(*t)) for s, t in near]
 
     def side(b, d, m):
         other = (b + d) % n_ty
@@ -305,30 +306,37 @@
     take(out, own, spot, iota(0) >= spot[0])
 
 
-def fold_body(offs, above, base, own_p, up_m, up_p, out):
+def fold(c, offs, above, base, own_p, up_m, up_p, out, first, buf, sem):
     m = lax.axis_index("mode")
+    tx = lax.axis_index("tx")
     row = iota(0)
     mine = place(offs, 1 - m)
-    out[...] = base[...]
-    take(out, own_p, mine, row >= mine[0])
+    buf[...] = base[...]
+    take(buf, own_p, mine, row >= mine[0])
     for ref, slot in ((up_m, m), (up_p, 1 - m)):
         over = place(above, slot)
-        take(out, ref, over, (row < over[0]) & (lax.axis_index("tx") > 0))
-
-
-def mid_body(offs, above, base, own_p, up_m, up_p, left_0, done, out, first):
-    part = out.at[0]
-    fold_body(offs, above, base, own_p, up_m, up_p, part)
-    first[0] = part[:, 0:W] - step_size * jnp.where(lax.axis_index("ty") > 0, left_0[...], 0.0)
-    out[1] = done[...]
-    first[1] = done[:, 0:W]
-
-
-def final_body(mid, first, left_0, left_1, out, buf, sems):
+        take(buf, ref, over, (row < over[0]) & (tx > 0))
+    store = pltpu.make_async_copy(buf.at[:, W:], out.at[c, :, W:], sem)
+    store.start()
+    first[...] = buf[:, 0:W]
+    store.wait()
+
+
+def fold_body(*refs):
+    fold(1, *refs)
+
+
+def mid_body(whole, left_0, *refs):
+    fold(0, *refs)
+    first = refs[-3]
+    first[...] = first[...] - step_size * jnp.where(lax.axis_index("ty") > 0, left_0[...], 0.0)
+
+
+def final_body(mid, first_0, first_1, left_0, left_1, out, buf, sems):
     ty = lax.axis_index("ty")
     stores = [pltpu.make_async_copy(buf.at[c], out.at[c, :, 0:W], sems.at[c]) for c in range(2)]
-    for c, left in enumerate((left_0, left_1)):
-        buf[c] = first[c] - step_size * jnp.where(ty > 0, left[...], 0.0)
+    for c, (first, left) in enumerate(((first_0, left_0), (first_1, left_1))):
+        buf[c] = first[...] - step_size * jnp.where(ty > 0, left[...], 0.0)
         stores[c].start()
     for store in stores:
         store.wait()
@@ -341,7 +349,7 @@
         body,
         out_shape=outs if many else outs[0],
         in_specs=in_specs,
-        out_specs=[out_spec] * len(outs) if many else out_spec,
+        out_specs=out_spec if isinstance(out_spec, list) else ([out_spec] * len(outs) if many else out_spec),
         scratch_shapes=list(scratch),
         input_output_aliases=aliases,
         compiler_params=pltpu.CompilerParams(vmem_limit_bytes=limit << 20),
@@ -411,23 +419,33 @@
     left_p0 = go(left_m0, "swap")
     left_1 = go(spill(2, g1, p1, b1, c1), "right")
     any_space = pl.BlockSpec(memory_space=pl.ANY)
-    fold = call(fold_body, (rows, cols), [SMEM, SMEM] + [VMEM] * 4, 8, 1 << 20, 4 << 20)(
-        offs, above, base[1], p1, b1, c1
-    )
-    mid, first = call(
-        mid_body, [whole, (2, W, W)], [SMEM, SMEM] + [VMEM] * 6, 12, 1 << 24, 10 << 20
-    )(offs, above, base[0], p0, b0, c0, left_m0, fold)
+    store = [pltpu.VMEM((rows, cols), f32), pltpu.SemaphoreType.DMA]
+    spaces = [any_space, VMEM]
+    fold, first_1 = call(
+        fold_body, [whole, piece], [SMEM, SMEM] + [VMEM] * 4, 8, 1 << 20, 4 << 20, store, spaces
+    )(offs, above, base[1], p1, b1, c1)
+    mid, first_0 = call(
+        mid_body,
+        [whole, piece],
+        [any_space, VMEM, SMEM, SMEM] + [VMEM] * 4,
+        8,
+        1 << 24,
+        5 << 20,
+        store,
+        spaces,
+        {0: 0},
+    )(fold, left_m0, offs, above, base[0], p0, b0, c0)
     return call(
         final_body,
         whole,
-        [any_space] + [VMEM] * 3,
+        [any_space] + [VMEM] * 4,
         8,
         1 << 18,
         2 << 20,
         [pltpu.VMEM((2, W, W), f32), pltpu.SemaphoreType.DMA((2,))],
         any_space,
         {0: 0},
-    )(mid, first, left_p0, left_1)
+    )(mid, first_0, first_1, left_p0, left_1)
 
 
 def solution(mesh):

time: 86.4 us -> 77.5 us (0.90)
  the two profiles are of different devices: /device:TPU:132 before, /device:TPU:4 now
where the time goes in v4:
time: 77.5 us; the launch traced here: 77.4 us
  waiting for transfers between devices  38 us (49%)
  Pallas kernels  20.2 us (26%)
  starting transfers between devices  14.8 us (19%)
  local copies, waits for them, and re-layouts  3.24 us (4%)
  between operations  1.11 us (1%)
    ppermute x18, waiting for transfers between devices, go(): return lax.ppermute(value, axes, ring[where])  38 us
    ppermute x18, starting transfers between devices, go(): return lax.ppermute(value, axes, ring[where])  14.8 us
    pallas_call x1, Pallas kernels, local(): call(main_body, [piece] * 2, [SMEM, SMEM] + [VMEM] * 17, 16, 5 << 30, 12...  6.81 us
    pallas_call x2, Pallas kernels, local(): call(functools.partial(prior_body, c), (rows, cols), [SMEM] * 2 + [VMEM]...  5.2 us
    pallas_call x1, Pallas kernels, local(): call(mid_body, [whole, piece], [any_space, VMEM, SMEM, SMEM] + [VMEM] * 4...  1.96 us
    pallas_call x1, Pallas kernels, local(): call(fold_body, [whole, piece], [SMEM, SMEM] + [VMEM] * 4, 8, 1 << 20, 4...  1.93 us
  transfers between devices with their start and end apart: 18, of which 10 were waited for; matrix products, arithmetic and copies ran while one was open for 2% of the time, Pallas kernels for 16%

profile of v4, /device:TPU:4, one launch (start us, length us, event | category | flops | bytes accessed | tf_op | source)
XLA Modules:
  0.0 77.4 jit_solution(1607401391130930530)
XLA Ops:
  0.0 1.2 %constant_dynamic-slice_fusion = f32[1,2,256,256]{3,2,1,0:T(8,128)S(1)} fusion(f32[2,2,256,256]{3,2,1,0:T(8,128)} %probe_a.1, s32[]{:T(128)S(6)} %select_n.3), kind=kLoop, calls=%fused_computation.2 | loop fusion | bytes 1048580 | tf_op jit(solution)/shard_map/dynamic_slice | solution.py:373
  1.2 1.3 %collective-permute-start.7 = (f32[1,2,256,256]{3,2,1,0:T(8,128)S(1)}, f32[1,2,256,256]{3,2,1,0:T(8,128)S(1)}, u32[]{:S(2)}, u32[]{:S(2)}) collective-permute-start(f32[1,2,256,256]{3,2,1,0:T(8,128)S(1)} %constant_dynamic-slice_fusion), channel_id=1, source_target_pairs={{0,1},{1,0},{2,3},{3,2},{4,5},{5,4},{6,7},{7,6},{8,9},{9,8},{10,11... | collective-permute-start | bytes 1572872 | tf_op jit(solution)/shard_map/ppermute | solution.py:362
  2.5 1.0 %slice_bitcast_fusion.1 = f32[256,256]{1,0:T(8,128)S(1)} fusion(f32[2,256,1024]{2,1,0:T(8,128)} %obj.11), kind=kLoop, calls=%fused_computation.1 | loop fusion | bytes 524288 | tf_op jit(solution)/shard_map/squeeze | solution.py:370
  3.5 2.4 %collective-permute-start.3 = (f32[256,256]{1,0:T(8,128)S(1)}, f32[256,256]{1,0:T(8,128)S(1)}, u32[]{:S(2)}, u32[]{:S(2)}) collective-permute-start(f32[256,256]{1,0:T(8,128)S(1)} %slice_bitcast_fusion.1), channel_id=1, source_target_pairs={{0,15},{1,14},{2,0},{3,1},{4,2},{5,3},{6,4},{7,5},{8,7},{9,6},{10,... | collective-permute-start | bytes 786440 | tf_op jit(solution)/shard_map/ppermute | solution.py:362
  5.9 1.0 %slice_bitcast_fusion = f32[256,256]{1,0:T(8,128)S(1)} fusion(f32[2,256,1024]{2,1,0:T(8,128)} %obj.11), kind=kLoop, calls=%fused_computation | loop fusion | bytes 524288 | tf_op jit(solution)/shard_map/squeeze | solution.py:371
  6.9 0.8 %collective-permute-start.1 = (f32[256,256]{1,0:T(8,128)S(1)}, f32[256,256]{1,0:T(8,128)S(1)}, u32[]{:S(2)}, u32[]{:S(2)}) collective-permute-start(f32[256,256]{1,0:T(8,128)S(1)} %slice_bitcast_fusion), channel_id=1, source_target_pairs={{0,15},{1,14},{2,0},{3,1},{4,2},{5,3},{6,4},{7,5},{8,7},{9,6},{10,... | collective-permute-start | bytes 786440 | tf_op jit(solution)/shard_map/ppermute | solution.py:362
  7.7 7.3 %collective-permute-done.7.probe_b = f32[1,2,256,256]{3,2,1,0:T(8,128)S(1)} collective-permute-done((f32[1,2,256,256]{3,2,1,0:T(8,128)S(1)}, f32[1,2,256,256]{3,2,1,0:T(8,128)S(1)}, u32[]{:S(2)}, u32[]{:S(2)}) %collective-permute-start.7) | collective-permute-done | bytes 524320 | tf_op jit(solution)/shard_map/ppermute | solution.py:362
  15.0 0.1 shard_map.136
  15.1 1.7 %collective-permute-start.2 = (f32[8,256]{1,0:T(8,128)S(1)}, f32[8,256]{1,0:T(8,128)S(1)}, u32[]{:S(2)}, u32[]{:S(2)}) collective-permute-start(f32[8,256]{1,0:T(8,128)S(1)} %shard_map.136), channel_id=1, source_target_pairs={{0,2},{1,3},{2,4},{3,5},{4,6},{5,7},{6,9},{7,8},{8,10},{9,11},{10,... | collective-permute-start | bytes 24584 | tf_op jit(solution)/shard_map/ppermute | solution.py:362
  16.8 0.2 collective-permute-start
  17.0 6.7 %collective-permute-done.above.refs_1_ = s32[2,2]{1,0:T(2,128)S(1)} collective-permute-done((s32[2,2]{1,0:T(2,128)S(1)}, s32[2,2]{1,0:T(2,128)S(1)}, u32[]{:S(2)}, u32[]{:S(2)}) %collective-permute-start) | collective-permute-done | bytes 48 | tf_op jit(solution)/shard_map/ppermute | solution.py:362
  23.7 0.0 collective-permute-done.3.refs_0_.right_0.right
  23.7 0.6 shard_map.137
  24.4 0.0 copy-start.2
  24.4 0.0 copy-start.5
  24.4 0.0 copy-start.6
  24.4 0.0 copy-start.7
  24.4 0.0 copy-start.8
  24.4 0.0 copy-start.9
  24.4 0.0 copy-start.10
  24.5 0.0 copy-start.11
  24.5 0.0 copy-start.12
  24.5 2.1 %collective-permute-start.5 = (f32[272,256]{1,0:T(8,128)S(1)}, f32[272,256]{1,0:T(8,128)S(1)}, u32[]{:S(2)}, u32[]{:S(2)}) collective-permute-start(f32[272,256]{1,0:T(8,128)S(1)} %get-tuple-element.14), channel_id=1, source_target_pairs={{0,240},{1,241},{2,242},{3,243},{4,244},{5,245},{6,246},{7,247},{8... | collective-permute-start | bytes 835592 | tf_op jit(solution)/shard_map/ppermute | solution.py:362
  26.5 0.6 shard_map.138
  27.2 1.2 %collective-permute-start.6 = (f32[256,256]{1,0:T(8,128)S(1)}, f32[256,256]{1,0:T(8,128)S(1)}, u32[]{:S(2)}, u32[]{:S(2)}) collective-permute-start(f32[256,256]{1,0:T(8,128)S(1)} %shard_map.138), channel_id=1, source_target_pairs={{0,240},{1,241},{2,242},{3,243},{4,244},{5,245},{6,246},{7,247},{8... | collective-permute-start | bytes 786440 | tf_op jit(solution)/shard_map/ppermute | solution.py:362
  29.0 0.7 shard_map.139.meas
  29.7 3.7 %collective-permute-done.6.below_0 = f32[256,256]{1,0:T(8,128)S(1)} collective-permute-done((f32[256,256]{1,0:T(8,128)S(1)}, f32[256,256]{1,0:T(8,128)S(1)}, u32[]{:S(2)}, u32[]{:S(2)}) %collective-permute-start.6) | collective-permute-done | bytes 262176 | tf_op jit(solution)/shard_map/ppermute | solution.py:362
  33.5 6.8 %shard_map.140 = (f32[256,256]{1,0:T(8,128)S(1)}, f32[256,256]{1,0:T(8,128)S(1)}) custom-call(s32[2,2]{1,0:T(2,128)S(1)} %bitcast.7, s32[1,1]{1,0:T(1,128)S(6)} %copy.19.counts, f32[2,256,1024]{2,1,0:T(8,128)S(1)} %copy-done, f32[256,256]{1,0:T(8,128)S(1)} %collective-permute-done.3.refs_0_.right_0.right, ...), custom_call_target="tpu_custom_call" | custom-call | flops 5368709120 | bytes 12582912 | tf_op jit(solution)/shard_map/pallas_call | solution.py:394
  40.3 0.0 copy-start.4
  40.3 2.5 %collective-permute-start.9 = (f32[256,256]{1,0:T(8,128)S(1)}, f32[256,256]{1,0:T(8,128)S(1)}, u32[]{:S(2)}, u32[]{:S(2)}) collective-permute-start(f32[256,256]{1,0:T(8,128)S(1)} %get-tuple-element.15.own.refs_0_), channel_id=1, source_target_pairs={{0,1},{1,0},{2,3},{3,2},{4,5},{5,4},{6,7},{7,6},{8,9},{9,8},{10,11... | collective-permute-start | bytes 786440 | tf_op jit(solution)/shard_map/ppermute | solution.py:362
  42.8 0.1 collective-permute-start.14
  43.0 6.5 %collective-permute-done.9.refs_3_.refs_1_ = f32[256,256]{1,0:T(8,128)S(1)} collective-permute-done((f32[256,256]{1,0:T(8,128)S(1)}, f32[256,256]{1,0:T(8,128)S(1)}, u32[]{:S(2)}, u32[]{:S(2)}) %collective-permute-start.9) | collective-permute-done | bytes 262176 | tf_op jit(solution)/shard_map/ppermute | solution.py:362
  49.5 0.3 collective-permute-done.12.refs_1_.refs_4_
  49.9 0.6 shard_map.143
  50.5 0.1 collective-permute-start.13
  50.6 1.7 %collective-permute-done.14.refs_3_ = f32[256,256]{1,0:T(8,128)S(1)} collective-permute-done((f32[256,256]{1,0:T(8,128)S(1)}, f32[256,256]{1,0:T(8,128)S(1)}, u32[]{:S(2)}, u32[]{:S(2)}) %collective-permute-start.14) | collective-permute-done | bytes 262176 | tf_op jit(solution)/shard_map/ppermute | solution.py:362
  52.3 0.3 collective-permute-done.10.refs_4_.refs_2_
  52.7 3.9 %collective-permute-done.11.refs_5_.refs_3_ = f32[256,256]{1,0:T(8,128)S(1)} collective-permute-done((f32[256,256]{1,0:T(8,128)S(1)}, f32[256,256]{1,0:T(8,128)S(1)}, u32[]{:S(2)}, u32[]{:S(2)}) %collective-permute-start.11) | collective-permute-done | bytes 262176 | tf_op jit(solution)/shard_map/ppermute | solution.py:362
  56.5 0.7 shard_map.146
  57.2 0.3 collective-permute-start.17
  57.5 3.1 %collective-permute-done.13.left_0 = f32[256,256]{1,0:T(8,128)S(1)} collective-permute-done((f32[256,256]{1,0:T(8,128)S(1)}, f32[256,256]{1,0:T(8,128)S(1)}, u32[]{:S(2)}, u32[]{:S(2)}) %collective-permute-start.13) | collective-permute-done | bytes 262176 | tf_op jit(solution)/shard_map/ppermute | solution.py:362
  60.6 2.2 %collective-permute-start.16 = (f32[256,256]{1,0:T(8,128)S(1)}, f32[256,256]{1,0:T(8,128)S(1)}, u32[]{:S(2)}, u32[]{:S(2)}) collective-permute-start(f32[256,256]{1,0:T(8,128)S(1)} %collective-permute-done.13.left_0), channel_id=1, source_target_pairs={{0,1},{1,0},{2,3},{3,2},{4,5},{5,4},{6,7},{7,6},{8,9},{9,8},{10,11... | collective-permute-start | bytes 786440 | tf_op jit(solution)/shard_map/ppermute | solution.py:362
  62.8 4.4 %collective-permute-done.4.up = f32[16,256]{1,0:T(8,128)S(1)} collective-permute-done((f32[16,256]{1,0:T(8,128)S(1)}, f32[16,256]{1,0:T(8,128)S(1)}, u32[]{:S(2)}, u32[]{:S(2)}) %collective-permute-start.4) | collective-permute-done | bytes 16416 | tf_op jit(solution)/shard_map/ppermute | solution.py:362
  67.2 2.6 %shard_map.144.refs_2_ = f32[256,1024]{1,0:T(8,128)S(1)} custom-call(f32[4,16]{1,0:T(4,128)S(1)} %bitcast.14, s32[2,2]{1,0:T(2,128)S(1)} %bitcast.10, f32[2,256,1024]{2,1,0:T(8,128)S(1)} %copy-done, f32[256,256]{1,0:T(8,128)S(1)} %collective-permute-done.3.refs_0_.right_0.right, f32[8,256]{1,0:T(8,128)S(1)} %collective-permute-done.2.refs_2_.left, ...), custom_call_target="tpu_custom_call" | custom-call | flops 134217728 | bytes 8388608 | tf_op jit(solution)/shard_map/pallas_call | solution.py:406
  69.8 2.6 %shard_map.141.refs_2_ = f32[256,1024]{1,0:T(8,128)S(1)} custom-call(f32[4,16]{1,0:T(4,128)S(1)} %bitcast.15, s32[2,2]{1,0:T(2,128)S(1)} %bitcast.11, f32[2,256,1024]{2,1,0:T(8,128)S(1)} %copy-done, f32[256,256]{1,0:T(8,128)S(1)} %collective-permute-done.1.refs_1_.right_1.right, f32[8,256]{1,0:T(8,128)S(1)} %collective-permute-done.2.refs_2_.left, ...), custom_call_target="tpu_custom_call" | custom-call | flops 134217728 | bytes 8388608 | tf_op jit(solution)/shard_map/pallas_call | solution.py:406
  72.4 1.9 %shard_map.142 = (f32[2,256,1024]{2,1,0:T(8,128)}, f32[256,256]{1,0:T(8,128)S(1)}) custom-call(s32[2,2]{1,0:T(2,128)S(1)} %bitcast.12, s32[2,2]{1,0:T(2,128)S(1)} %collective-permute-done.above.refs_1_, f32[256,1024]{1,0:T(8,128)S(1)} %shard_map.141.refs_2_, f32[256,256]{1,0:T(8,128)S(1)} %collective-permute-done.9.refs_3_.refs_1_, ...), custom_call_target="tpu_custom_call" | custom-call | flops 1048576 | bytes 4194304 | tf_op jit(solution)/shard_map/pallas_call | solution.py:424
  74.4 2.0 %shard_map.145 = (f32[2,256,1024]{2,1,0:T(8,128)}, f32[256,256]{1,0:T(8,128)S(1)}) custom-call(f32[2,256,1024]{2,1,0:T(8,128)} %get-tuple-element.16.whole, f32[256,256]{1,0:T(8,128)S(1)} %collective-permute-done.13.left_0, s32[2,2]{1,0:T(2,128)S(1)} %bitcast.13, s32[2,2]{1,0:T(2,128)S(1)} %collective-permute-done.above.refs_1_, ...), custom_call_target="tpu_custom_call", output_to_operand_aliasing={{0}: (0, {})} | custom-call | flops 16777216 | bytes 5242880 | tf_op jit(solution)/shard_map/pallas_call | solution.py:427
  76.4 0.9 %shard_map.147 = f32[2,256,1024]{2,1,0:T(8,128)} custom-call(f32[2,256,1024]{2,1,0:T(8,128)} %get-tuple-element.18.mid, f32[256,256]{1,0:T(8,128)S(1)} %get-tuple-element.19.first_0, f32[256,256]{1,0:T(8,128)S(1)} %get-tuple-element.20.first_1, f32[256,256]{1,0:T(8,128)S(1)} %collective-permute-done.16.left_0, ...), custom_call_target="tpu_custom_call", output_to_operand_aliasing={{}: (0, {})} | custom-call | flops 262144 | bytes 2097152 | tf_op jit(solution)/shard_map/pallas_call | solution.py:438
  (29 shorter events, 0.1 us)
Async XLA Ops:
  0.0 15.0 %copy-start = (f32[2,256,1024]{2,1,0:T(8,128)S(1)}, f32[2,256,1024]{2,1,0:T(8,128)}, u32[]{:S(2)}) copy-start(f32[2,256,1024]{2,1,0:T(8,128)} %obj.11) | copy-start | bytes 6291460
  0.0 16.8 %copy-start.3 = (s32[1,1,2,2]{3,2,1,0:T(2,128)S(1)}, s32[1,1,2,2]{3,2,1,0:T(2,128)}, u32[]{:S(2)}) copy-start(s32[1,1,2,2]{3,2,1,0:T(2,128)} %param.17) | copy-start | bytes 52
  1.2 13.8 %collective-permute-start.7 = (f32[1,2,256,256]{3,2,1,0:T(8,128)S(1)}, f32[1,2,256,256]{3,2,1,0:T(8,128)S(1)}, u32[]{:S(2)}, u32[]{:S(2)}) collective-permute-start(f32[1,2,256,256]{3,2,1,0:T(8,128)S(1)} %constant_dynamic-slice_fusion), channel_id=1, source_target_pairs={{0,1},{1,0},{2,3},{3,2},{4,5},{5,4},{6,7},{7,6},{8,9},{9,8},{10,11... | collective-permute-start | bytes 1572872 | tf_op jit(solution)/shard_map/ppermute | solution.py:362
  3.5 20.2 %collective-permute-start.3 = (f32[256,256]{1,0:T(8,128)S(1)}, f32[256,256]{1,0:T(8,128)S(1)}, u32[]{:S(2)}, u32[]{:S(2)}) collective-permute-start(f32[256,256]{1,0:T(8,128)S(1)} %slice_bitcast_fusion.1), channel_id=1, source_target_pairs={{0,15},{1,14},{2,0},{3,1},{4,2},{5,3},{6,4},{7,5},{8,7},{9,6},{10,... | collective-permute-start | bytes 786440 | tf_op jit(solution)/shard_map/ppermute | solution.py:362
  6.9 16.9 %collective-permute-start.1 = (f32[256,256]{1,0:T(8,128)S(1)}, f32[256,256]{1,0:T(8,128)S(1)}, u32[]{:S(2)}, u32[]{:S(2)}) collective-permute-start(f32[256,256]{1,0:T(8,128)S(1)} %slice_bitcast_fusion), channel_id=1, source_target_pairs={{0,15},{1,14},{2,0},{3,1},{4,2},{5,3},{6,4},{7,5},{8,7},{9,6},{10,... | collective-permute-start | bytes 786440 | tf_op jit(solution)/shard_map/ppermute | solution.py:362
  15.0 18.4 %collective-permute-start.8 = (f32[1,2,256,256]{3,2,1,0:T(8,128)S(1)}, f32[1,2,256,256]{3,2,1,0:T(8,128)S(1)}, u32[]{:S(2)}, u32[]{:S(2)}) collective-permute-start(f32[1,2,256,256]{3,2,1,0:T(8,128)S(1)} %collective-permute-done.7.probe_b), channel_id=1, source_target_pairs={{0,16},{1,17},{2,18},{3,19},{4,20},{5,21},{6,22},{7,23},{8,24},{9,... | collective-permute-start | bytes 1572872 | tf_op jit(solution)/shard_map/ppermute | solution.py:362
  15.1 8.6 %collective-permute-start.2 = (f32[8,256]{1,0:T(8,128)S(1)}, f32[8,256]{1,0:T(8,128)S(1)}, u32[]{:S(2)}, u32[]{:S(2)}) collective-permute-start(f32[8,256]{1,0:T(8,128)S(1)} %shard_map.136), channel_id=1, source_target_pairs={{0,2},{1,3},{2,4},{3,5},{4,6},{5,7},{6,9},{7,8},{8,10},{9,11},{10,... | collective-permute-start | bytes 24584 | tf_op jit(solution)/shard_map/ppermute | solution.py:362
  16.8 12.2 %copy-start.1 = (f32[1,1,2,256,256]{4,3,2,1,0:T(8,128)S(1)}, f32[1,1,2,256,256]{4,3,2,1,0:T(8,128)}, u32[]{:S(2)}) copy-start(f32[1,1,2,256,256]{4,3,2,1,0:T(8,128)} %meas.1) | copy-start | bytes 1572868
  16.8 6.9 %collective-permute-start = (s32[2,2]{1,0:T(2,128)S(1)}, s32[2,2]{1,0:T(2,128)S(1)}, u32[]{:S(2)}, u32[]{:S(2)}) collective-permute-start(s32[2,2]{1,0:T(2,128)S(1)} %bitcast.6), channel_id=1, source_target_pairs={{0,16},{1,17},{2,18},{3,19},{4,20},{5,21},{6,22},{7,23},{8,24},{9,... | collective-permute-start | bytes 56 | tf_op jit(solution)/shard_map/ppermute | solution.py:362
  24.4 9.1 %copy-start.2 = (f32[2,2,256,256]{3,2,1,0:T(8,128)S(1)}, f32[2,2,256,256]{3,2,1,0:T(8,128)}, u32[]{:S(2)}) copy-start(f32[2,2,256,256]{3,2,1,0:T(8,128)} %probe_a.1) | copy-start | bytes 3145732
  24.4 9.0 %copy-start.5 = (bf16[256,256]{1,0:T(8,128)(2,1)S(1)}, bf16[256,256]{1,0:T(8,128)(2,1)}, u32[]{:S(2)}) copy-start(bf16[256,256]{1,0:T(8,128)(2,1)} %constant.28.clone.refs_0_) | copy-start | bytes 393220
  24.4 9.0 %copy-start.6 = (bf16[256,256]{1,0:T(8,128)(2,1)S(1)}, bf16[256,256]{1,0:T(8,128)(2,1)}, u32[]{:S(2)}) copy-start(bf16[256,256]{1,0:T(8,128)(2,1)} %constant.29.clone.refs_1_) | copy-start | bytes 393220
  24.4 9.0 %copy-start.7 = (bf16[256,256]{1,0:T(8,128)(2,1)S(1)}, bf16[256,256]{1,0:T(8,128)(2,1)}, u32[]{:S(2)}) copy-start(bf16[256,256]{1,0:T(8,128)(2,1)} %constant.30.clone.refs_2_) | copy-start | bytes 393220
  24.4 9.0 %copy-start.8 = (bf16[256,256]{1,0:T(8,128)(2,1)S(1)}, bf16[256,256]{1,0:T(8,128)(2,1)}, u32[]{:S(2)}) copy-start(bf16[256,256]{1,0:T(8,128)(2,1)} %constant.31.clone.refs_3_) | copy-start | bytes 393220
  24.4 9.0 %copy-start.9 = (bf16[256,256]{1,0:T(8,128)(2,1)S(1)}, bf16[256,256]{1,0:T(8,128)(2,1)}, u32[]{:S(2)}) copy-start(bf16[256,256]{1,0:T(8,128)(2,1)} %constant.32.clone.refs_4_) | copy-start | bytes 393220
  24.4 9.0 %copy-start.10 = (bf16[256,256]{1,0:T(8,128)(2,1)S(1)}, bf16[256,256]{1,0:T(8,128)(2,1)}, u32[]{:S(2)}) copy-start(bf16[256,256]{1,0:T(8,128)(2,1)} %constant.33.clone.refs_5_) | copy-start | bytes 393220
  24.5 9.0 %copy-start.11 = (bf16[256,256]{1,0:T(8,128)(2,1)S(1)}, bf16[256,256]{1,0:T(8,128)(2,1)}, u32[]{:S(2)}) copy-start(bf16[256,256]{1,0:T(8,128)(2,1)} %constant.34.clone.refs_6_) | copy-start | bytes 393220
  24.5 9.0 %copy-start.12 = (bf16[256,256]{1,0:T(8,128)(2,1)S(1)}, bf16[256,256]{1,0:T(8,128)(2,1)}, u32[]{:S(2)}) copy-start(bf16[256,256]{1,0:T(8,128)(2,1)} %constant.35.clone.refs_7_) | copy-start | bytes 393220
  24.5 8.9 %collective-permute-start.5 = (f32[272,256]{1,0:T(8,128)S(1)}, f32[272,256]{1,0:T(8,128)S(1)}, u32[]{:S(2)}, u32[]{:S(2)}) collective-permute-start(f32[272,256]{1,0:T(8,128)S(1)} %get-tuple-element.14), channel_id=1, source_target_pairs={{0,240},{1,241},{2,242},{3,243},{4,244},{5,245},{6,246},{7,247},{8... | collective-permute-start | bytes 835592 | tf_op jit(solution)/shard_map/ppermute | solution.py:362
  27.2 6.3 %collective-permute-start.6 = (f32[256,256]{1,0:T(8,128)S(1)}, f32[256,256]{1,0:T(8,128)S(1)}, u32[]{:S(2)}, u32[]{:S(2)}) collective-permute-start(f32[256,256]{1,0:T(8,128)S(1)} %shard_map.138), channel_id=1, source_target_pairs={{0,240},{1,241},{2,242},{3,243},{4,244},{5,245},{6,246},{7,247},{8... | collective-permute-start | bytes 786440 | tf_op jit(solution)/shard_map/ppermute | solution.py:362
  40.3 26.9 %copy-start.4 = (f32[16,4]{0,1:T(4,128)S(1)}, f32[16,4]{0,1:T(4,128)}, u32[]{:S(2)}) copy-start(f32[16,4]{0,1:T(4,128)} %param.19) | copy-start | bytes 772
  40.3 9.2 %collective-permute-start.9 = (f32[256,256]{1,0:T(8,128)S(1)}, f32[256,256]{1,0:T(8,128)S(1)}, u32[]{:S(2)}, u32[]{:S(2)}) collective-permute-start(f32[256,256]{1,0:T(8,128)S(1)} %get-tuple-element.15.own.refs_0_), channel_id=1, source_target_pairs={{0,1},{1,0},{2,3},{3,2},{4,5},{5,4},{6,7},{7,6},{8,9},{9,8},{10,11... | collective-permute-start | bytes 786440 | tf_op jit(solution)/shard_map/ppermute | solution.py:362
  42.8 7.0 %collective-permute-start.12 = (f32[256,256]{1,0:T(8,128)S(1)}, f32[256,256]{1,0:T(8,128)S(1)}, u32[]{:S(2)}, u32[]{:S(2)}) collective-permute-start(f32[256,256]{1,0:T(8,128)S(1)} %get-tuple-element.17.refs_0_.own), channel_id=1, source_target_pairs={{0,16},{1,17},{2,18},{3,19},{4,20},{5,21},{6,22},{7,23},{8,24},{9,... | collective-permute-start | bytes 786440 | tf_op jit(solution)/shard_map/ppermute | solution.py:362
  42.8 9.5 %collective-permute-start.14 = (f32[256,256]{1,0:T(8,128)S(1)}, f32[256,256]{1,0:T(8,128)S(1)}, u32[]{:S(2)}, u32[]{:S(2)}) collective-permute-start(f32[256,256]{1,0:T(8,128)S(1)} %get-tuple-element.17.refs_0_.own), channel_id=1, source_target_pairs={{0,1},{1,0},{2,3},{3,2},{4,5},{5,4},{6,7},{7,6},{8,9},{9,8},{10,11... | collective-permute-start | bytes 786440 | tf_op jit(solution)/shard_map/ppermute | solution.py:362
  43.0 9.7 %collective-permute-start.10 = (f32[256,256]{1,0:T(8,128)S(1)}, f32[256,256]{1,0:T(8,128)S(1)}, u32[]{:S(2)}, u32[]{:S(2)}) collective-permute-start(f32[256,256]{1,0:T(8,128)S(1)} %get-tuple-element.15.own.refs_0_), channel_id=1, source_target_pairs={{0,16},{1,17},{2,18},{3,19},{4,20},{5,21},{6,22},{7,23},{8,24},{9,... | collective-permute-start | bytes 786440 | tf_op jit(solution)/shard_map/ppermute | solution.py:362
  49.5 7.0 %collective-permute-start.11 = (f32[256,256]{1,0:T(8,128)S(1)}, f32[256,256]{1,0:T(8,128)S(1)}, u32[]{:S(2)}, u32[]{:S(2)}) collective-permute-start(f32[256,256]{1,0:T(8,128)S(1)} %collective-permute-done.9.refs_3_.refs_1_), channel_id=1, source_target_pairs={{0,16},{1,17},{2,18},{3,19},{4,20},{5,21},{6,22},{7,23},{8,24},{9,... | collective-permute-start | bytes 786440 | tf_op jit(solution)/shard_map/ppermute | solution.py:362
  50.5 10.1 %collective-permute-start.13 = (f32[256,256]{1,0:T(8,128)S(1)}, f32[256,256]{1,0:T(8,128)S(1)}, u32[]{:S(2)}, u32[]{:S(2)}) collective-permute-start(f32[256,256]{1,0:T(8,128)S(1)} %shard_map.143), channel_id=1, source_target_pairs={{0,2},{1,3},{2,4},{3,5},{4,6},{5,7},{6,9},{7,8},{8,10},{9,11},{10,... | collective-permute-start | bytes 786440 | tf_op jit(solution)/shard_map/ppermute | solution.py:362
  52.3 22.0 %collective-permute-start.15 = (f32[256,256]{1,0:T(8,128)S(1)}, f32[256,256]{1,0:T(8,128)S(1)}, u32[]{:S(2)}, u32[]{:S(2)}) collective-permute-start(f32[256,256]{1,0:T(8,128)S(1)} %collective-permute-done.14.refs_3_), channel_id=1, source_target_pairs={{0,16},{1,17},{2,18},{3,19},{4,20},{5,21},{6,22},{7,23},{8,24},{9,... | collective-permute-start | bytes 786440 | tf_op jit(solution)/shard_map/ppermute | solution.py:362
  57.2 19.1 %collective-permute-start.17 = (f32[256,256]{1,0:T(8,128)S(1)}, f32[256,256]{1,0:T(8,128)S(1)}, u32[]{:S(2)}, u32[]{:S(2)}) collective-permute-start(f32[256,256]{1,0:T(8,128)S(1)} %shard_map.146), channel_id=1, source_target_pairs={{0,2},{1,3},{2,4},{3,5},{4,6},{5,7},{6,9},{7,8},{8,10},{9,11},{10,... | collective-permute-start | bytes 786440 | tf_op jit(solution)/shard_map/ppermute | solution.py:362
  60.6 15.7 %collective-permute-start.16 = (f32[256,256]{1,0:T(8,128)S(1)}, f32[256,256]{1,0:T(8,128)S(1)}, u32[]{:S(2)}, u32[]{:S(2)}) collective-permute-start(f32[256,256]{1,0:T(8,128)S(1)} %collective-permute-done.13.left_0), channel_id=1, source_target_pairs={{0,1},{1,0},{2,3},{3,2},{4,5},{5,4},{6,7},{7,6},{8,9},{9,8},{10,11... | collective-permute-start | bytes 786440 | tf_op jit(solution)/shard_map/ppermute | solution.py:362
  62.8 4.4 %collective-permute-start.4 = (f32[16,256]{1,0:T(8,128)S(1)}, f32[16,256]{1,0:T(8,128)S(1)}, u32[]{:S(2)}, u32[]{:S(2)}) collective-permute-start(f32[16,256]{1,0:T(8,128)S(1)} %get-tuple-element.13), channel_id=1, source_target_pairs={{0,16},{1,17},{2,18},{3,19},{4,20},{5,21},{6,22},{7,23},{8,24},{9,... | collective-permute-start | bytes 49160 | tf_op jit(solution)/shard_map/ppermute | solution.py:362

commit v5 on v3

--- a/solution.py
+++ b/solution.py
@@ -27,11 +27,12 @@
         return (a * n_ty + b) * 2 + m
 
     def perm(move):
-        pairs = [
-            ((a, b, m), move(a, b, m)) for a in range(n_tx) for b in range(n_ty) for m in range(2)
+        return [
+            (lin(a, b, m), lin(*move(a, b, m)))
+            for a in range(n_tx)
+            for b in range(n_ty)
+            for m in range(2)
         ]
-        near = [(s, t) for s, t in pairs if abs(s[0] - t[0]) <= 1 and abs(s[1] - t[1]) <= 1]
-        return [(lin(*s), lin(*t)) for s, t in near]
 
     def side(b, d, m):
         other = (b + d) % n_ty

time: 86.4 us -> 77.3 us (0.89)
  the two profiles are of different devices: /device:TPU:132 before, /device:TPU:4 now
where the time goes in v5:
time: 77.3 us; the launch traced here: 77.1 us
  waiting for transfers between devices  38 us (49%)
  Pallas kernels  19.9 us (26%)
  starting transfers between devices  14.8 us (19%)
  local copies, waits for them, and re-layouts  3.24 us (4%)
  between operations  1.08 us (1%)
    ppermute x18, waiting for transfers between devices, go(): return lax.ppermute(value, axes, ring[where])  38 us
    ppermute x18, starting transfers between devices, go(): return lax.ppermute(value, axes, ring[where])  14.8 us
    pallas_call x1, Pallas kernels, local(): call(main_body, [piece] * 2, [SMEM, SMEM] + [VMEM] * 17, 16, 5 << 30, 12...  6.94 us
    pallas_call x2, Pallas kernels, local(): call(functools.partial(prior_body, c), (rows, cols), [SMEM] * 2 + [VMEM]...  5.2 us
    pallas_call x1, Pallas kernels, local(): call(mid_body, [whole, (2, W, W)], [SMEM, SMEM] + [VMEM] * 6, 12, 1 << 24...  2.49 us
  transfers between devices with their start and end apart: 18, of which 10 were waited for; matrix products, arithmetic and copies ran while one was open for 3% of the time, Pallas kernels for 16%

profile of v5, /device:TPU:4, one launch (start us, length us, event | category | flops | bytes accessed | tf_op | source)
XLA Modules:
  0.0 77.1 jit_solution(10201010212711429341)
XLA Ops:
  0.0 1.2 %constant_dynamic-slice_fusion = f32[1,2,256,256]{3,2,1,0:T(8,128)S(1)} fusion(f32[2,2,256,256]{3,2,1,0:T(8,128)} %probe_a.1, s32[]{:T(128)S(6)} %select_n.3), kind=kLoop, calls=%fused_computation.2 | loop fusion | bytes 1048580 | tf_op jit(solution)/shard_map/dynamic_slice | solution.py:366
  1.2 1.3 %collective-permute-start.7 = (f32[1,2,256,256]{3,2,1,0:T(8,128)S(1)}, f32[1,2,256,256]{3,2,1,0:T(8,128)S(1)}, u32[]{:S(2)}, u32[]{:S(2)}) collective-permute-start(f32[1,2,256,256]{3,2,1,0:T(8,128)S(1)} %constant_dynamic-slice_fusion), channel_id=1, source_target_pairs={{0,1},{1,0},{2,3},{3,2},{4,5},{5,4},{6,7},{7,6},{8,9},{9,8},{10,11... | collective-permute-start | bytes 1572872 | tf_op jit(solution)/shard_map/ppermute | solution.py:355
  2.5 1.0 %slice_bitcast_fusion.1 = f32[256,256]{1,0:T(8,128)S(1)} fusion(f32[2,256,1024]{2,1,0:T(8,128)} %obj.11), kind=kLoop, calls=%fused_computation.1 | loop fusion | bytes 524288 | tf_op jit(solution)/shard_map/squeeze | solution.py:363
  3.5 2.4 %collective-permute-start.1 = (f32[256,256]{1,0:T(8,128)S(1)}, f32[256,256]{1,0:T(8,128)S(1)}, u32[]{:S(2)}, u32[]{:S(2)}) collective-permute-start(f32[256,256]{1,0:T(8,128)S(1)} %slice_bitcast_fusion.1), channel_id=1, source_target_pairs={{0,15},{1,14},{2,0},{3,1},{4,2},{5,3},{6,4},{7,5},{8,7},{9,6},{10,... | collective-permute-start | bytes 786440 | tf_op jit(solution)/shard_map/ppermute | solution.py:355
  5.9 1.0 %slice_bitcast_fusion = f32[256,256]{1,0:T(8,128)S(1)} fusion(f32[2,256,1024]{2,1,0:T(8,128)} %obj.11), kind=kLoop, calls=%fused_computation | loop fusion | bytes 524288 | tf_op jit(solution)/shard_map/squeeze | solution.py:364
  6.9 0.8 %collective-permute-start.3 = (f32[256,256]{1,0:T(8,128)S(1)}, f32[256,256]{1,0:T(8,128)S(1)}, u32[]{:S(2)}, u32[]{:S(2)}) collective-permute-start(f32[256,256]{1,0:T(8,128)S(1)} %slice_bitcast_fusion), channel_id=1, source_target_pairs={{0,15},{1,14},{2,0},{3,1},{4,2},{5,3},{6,4},{7,5},{8,7},{9,6},{10,... | collective-permute-start | bytes 786440 | tf_op jit(solution)/shard_map/ppermute | solution.py:355
  7.7 7.3 %collective-permute-done.7.probe_b = f32[1,2,256,256]{3,2,1,0:T(8,128)S(1)} collective-permute-done((f32[1,2,256,256]{3,2,1,0:T(8,128)S(1)}, f32[1,2,256,256]{3,2,1,0:T(8,128)S(1)}, u32[]{:S(2)}, u32[]{:S(2)}) %collective-permute-start.7) | collective-permute-done | bytes 524320 | tf_op jit(solution)/shard_map/ppermute | solution.py:355
  15.0 0.1 shard_map.136
  15.1 1.7 %collective-permute-start.2 = (f32[8,256]{1,0:T(8,128)S(1)}, f32[8,256]{1,0:T(8,128)S(1)}, u32[]{:S(2)}, u32[]{:S(2)}) collective-permute-start(f32[8,256]{1,0:T(8,128)S(1)} %shard_map.136), channel_id=1, source_target_pairs={{0,2},{1,3},{2,4},{3,5},{4,6},{5,7},{6,9},{7,8},{8,10},{9,11},{10,... | collective-permute-start | bytes 24584 | tf_op jit(solution)/shard_map/ppermute | solution.py:355
  16.8 0.2 collective-permute-start
  17.0 6.7 %collective-permute-done.above = s32[2,2]{1,0:T(2,128)S(1)} collective-permute-done((s32[2,2]{1,0:T(2,128)S(1)}, s32[2,2]{1,0:T(2,128)S(1)}, u32[]{:S(2)}, u32[]{:S(2)}) %collective-permute-start) | collective-permute-done | bytes 48 | tf_op jit(solution)/shard_map/ppermute | solution.py:355
  23.7 0.0 collective-permute-done.1.refs_0_.right_0.right
  23.7 0.6 shard_map.137
  24.4 0.0 copy-start.2
  24.4 0.0 copy-start.5
  24.4 0.0 copy-start.6
  24.4 0.0 copy-start.7
  24.4 0.0 copy-start.8
  24.4 0.0 copy-start.9
  24.4 0.0 copy-start.10
  24.5 0.0 copy-start.11
  24.5 0.0 copy-start.12
  24.5 2.1 %collective-permute-start.5 = (f32[272,256]{1,0:T(8,128)S(1)}, f32[272,256]{1,0:T(8,128)S(1)}, u32[]{:S(2)}, u32[]{:S(2)}) collective-permute-start(f32[272,256]{1,0:T(8,128)S(1)} %get-tuple-element.12), channel_id=1, source_target_pairs={{0,240},{1,241},{2,242},{3,243},{4,244},{5,245},{6,246},{7,247},{8... | collective-permute-start | bytes 835592 | tf_op jit(solution)/shard_map/ppermute | solution.py:355
  26.5 0.6 shard_map.138
  27.2 1.2 %collective-permute-start.6 = (f32[256,256]{1,0:T(8,128)S(1)}, f32[256,256]{1,0:T(8,128)S(1)}, u32[]{:S(2)}, u32[]{:S(2)}) collective-permute-start(f32[256,256]{1,0:T(8,128)S(1)} %shard_map.138), channel_id=1, source_target_pairs={{0,240},{1,241},{2,242},{3,243},{4,244},{5,245},{6,246},{7,247},{8... | collective-permute-start | bytes 786440 | tf_op jit(solution)/shard_map/ppermute | solution.py:355
  29.0 0.7 shard_map.139.meas
  29.7 3.7 %collective-permute-done.6.below_0 = f32[256,256]{1,0:T(8,128)S(1)} collective-permute-done((f32[256,256]{1,0:T(8,128)S(1)}, f32[256,256]{1,0:T(8,128)S(1)}, u32[]{:S(2)}, u32[]{:S(2)}) %collective-permute-start.6) | collective-permute-done | bytes 262176 | tf_op jit(solution)/shard_map/ppermute | solution.py:355
  33.5 6.9 %shard_map.140 = (f32[256,256]{1,0:T(8,128)S(1)}, f32[256,256]{1,0:T(8,128)S(1)}) custom-call(s32[2,2]{1,0:T(2,128)S(1)} %bitcast.7, s32[1,1]{1,0:T(1,128)S(6)} %copy.17.counts, f32[2,256,1024]{2,1,0:T(8,128)S(1)} %copy-done, f32[256,256]{1,0:T(8,128)S(1)} %collective-permute-done.1.refs_0_.right_0.right, ...), custom_call_target="tpu_custom_call" | custom-call | flops 5368709120 | bytes 12582912 | tf_op jit(solution)/shard_map/pallas_call | solution.py:387
  40.5 0.0 copy-start.4
  40.5 2.5 %collective-permute-start.13 = (f32[256,256]{1,0:T(8,128)S(1)}, f32[256,256]{1,0:T(8,128)S(1)}, u32[]{:S(2)}, u32[]{:S(2)}) collective-permute-start(f32[256,256]{1,0:T(8,128)S(1)} %get-tuple-element.14.own.refs_0_), channel_id=1, source_target_pairs={{0,1},{1,0},{2,3},{3,2},{4,5},{5,4},{6,7},{7,6},{8,9},{9,8},{10,11... | collective-permute-start | bytes 786440 | tf_op jit(solution)/shard_map/ppermute | solution.py:355
  43.0 0.1 collective-permute-start.9
  43.1 6.5 %collective-permute-done.13.own_p.refs_1_ = f32[256,256]{1,0:T(8,128)S(1)} collective-permute-done((f32[256,256]{1,0:T(8,128)S(1)}, f32[256,256]{1,0:T(8,128)S(1)}, u32[]{:S(2)}, u32[]{:S(2)}) %collective-permute-start.13) | collective-permute-done | bytes 262176 | tf_op jit(solution)/shard_map/ppermute | solution.py:355
  49.6 0.3 collective-permute-done.10.refs_1_.up_m
  50.0 0.6 shard_map.142
  50.6 0.1 collective-permute-start.12
  50.7 1.7 %collective-permute-done.9.own_p = f32[256,256]{1,0:T(8,128)S(1)} collective-permute-done((f32[256,256]{1,0:T(8,128)S(1)}, f32[256,256]{1,0:T(8,128)S(1)}, u32[]{:S(2)}, u32[]{:S(2)}) %collective-permute-start.9) | collective-permute-done | bytes 262176 | tf_op jit(solution)/shard_map/ppermute | solution.py:355
  52.4 0.3 collective-permute-done.14.up_m.refs_2_
  52.8 3.9 %collective-permute-done.15.up_p.refs_3_ = f32[256,256]{1,0:T(8,128)S(1)} collective-permute-done((f32[256,256]{1,0:T(8,128)S(1)}, f32[256,256]{1,0:T(8,128)S(1)}, u32[]{:S(2)}, u32[]{:S(2)}) %collective-permute-start.15) | collective-permute-done | bytes 262176 | tf_op jit(solution)/shard_map/ppermute | solution.py:355
  56.6 0.7 shard_map.146
  57.4 0.3 collective-permute-start.17
  57.6 3.1 %collective-permute-done.12.left_0 = f32[256,256]{1,0:T(8,128)S(1)} collective-permute-done((f32[256,256]{1,0:T(8,128)S(1)}, f32[256,256]{1,0:T(8,128)S(1)}, u32[]{:S(2)}, u32[]{:S(2)}) %collective-permute-start.12) | collective-permute-done | bytes 262176 | tf_op jit(solution)/shard_map/ppermute | solution.py:355
  60.7 2.2 %collective-permute-start.16 = (f32[256,256]{1,0:T(8,128)S(1)}, f32[256,256]{1,0:T(8,128)S(1)}, u32[]{:S(2)}, u32[]{:S(2)}) collective-permute-start(f32[256,256]{1,0:T(8,128)S(1)} %collective-permute-done.12.left_0), channel_id=1, source_target_pairs={{0,1},{1,0},{2,3},{3,2},{4,5},{5,4},{6,7},{7,6},{8,9},{9,8},{10,11... | collective-permute-start | bytes 786440 | tf_op jit(solution)/shard_map/ppermute | solution.py:355
  63.0 4.4 %collective-permute-done.4.up = f32[16,256]{1,0:T(8,128)S(1)} collective-permute-done((f32[16,256]{1,0:T(8,128)S(1)}, f32[16,256]{1,0:T(8,128)S(1)}, u32[]{:S(2)}, u32[]{:S(2)}) %collective-permute-start.4) | collective-permute-done | bytes 16416 | tf_op jit(solution)/shard_map/ppermute | solution.py:355
  67.3 2.6 %shard_map.143.base = f32[256,1024]{1,0:T(8,128)S(1)} custom-call(f32[4,16]{1,0:T(4,128)S(1)} %bitcast.14, s32[2,2]{1,0:T(2,128)S(1)} %bitcast.10, f32[2,256,1024]{2,1,0:T(8,128)S(1)} %copy-done, f32[256,256]{1,0:T(8,128)S(1)} %collective-permute-done.3.refs_1_.right_1.right, f32[8,256]{1,0:T(8,128)S(1)} %collective-permute-done.2.refs_2_.left, ...), custom_call_target="tpu_custom_call" | custom-call | flops 134217728 | bytes 8388608 | tf_op jit(solution)/shard_map/pallas_call | solution.py:399
  69.9 2.6 %shard_map.141.base = f32[256,1024]{1,0:T(8,128)S(1)} custom-call(f32[4,16]{1,0:T(4,128)S(1)} %bitcast.15, s32[2,2]{1,0:T(2,128)S(1)} %bitcast.11, f32[2,256,1024]{2,1,0:T(8,128)S(1)} %copy-done, f32[256,256]{1,0:T(8,128)S(1)} %collective-permute-done.1.refs_0_.right_0.right, f32[8,256]{1,0:T(8,128)S(1)} %collective-permute-done.2.refs_2_.left, ...), custom_call_target="tpu_custom_call" | custom-call | flops 134217728 | bytes 8388608 | tf_op jit(solution)/shard_map/pallas_call | solution.py:399
  72.5 1.0 %shard_map.144.done = f32[256,1024]{1,0:T(8,128)S(1)} custom-call(s32[2,2]{1,0:T(2,128)S(1)} %bitcast.12, s32[2,2]{1,0:T(2,128)S(1)} %collective-permute-done.above, f32[256,1024]{1,0:T(8,128)S(1)} %shard_map.143.base, f32[256,256]{1,0:T(8,128)S(1)} %collective-permute-done.13.own_p.refs_1_, f32[256,256]{1,0:T(8,128)S(1)} %collective-permute-done.14.up_m.refs_2_, ...), custom_call_target="tpu_custom_call" | custom-call | flops 1048576 | bytes 4194304 | tf_op jit(solution)/shard_map/pallas_call | solution.py:415
  73.6 2.5 %shard_map.145 = (f32[2,256,1024]{2,1,0:T(8,128)}, f32[2,256,256]{2,1,0:T(8,128)S(1)}) custom-call(s32[2,2]{1,0:T(2,128)S(1)} %bitcast.13, s32[2,2]{1,0:T(2,128)S(1)} %collective-permute-done.above, f32[256,1024]{1,0:T(8,128)S(1)} %shard_map.141.base, f32[256,256]{1,0:T(8,128)S(1)} %collective-permute-done.9.own_p, ...), custom_call_target="tpu_custom_call" | custom-call | flops 16777216 | bytes 10485760 | tf_op jit(solution)/shard_map/pallas_call | solution.py:418
  76.1 0.8 %shard_map.147 = f32[2,256,1024]{2,1,0:T(8,128)} custom-call(f32[2,256,1024]{2,1,0:T(8,128)} %get-tuple-element.15.mid, f32[2,256,256]{2,1,0:T(8,128)S(1)} %get-tuple-element.16.first, f32[256,256]{1,0:T(8,128)S(1)} %collective-permute-done.16.left_0, f32[256,256]{1,0:T(8,128)S(1)} %collective-permute-done.17.left_1), custom_call_target="tpu_custom_call", output_to_operand_aliasing={{}: (0, {})} | custom-call | flops 262144 | bytes 2097152 | tf_op jit(solution)/shard_map/pallas_call | solution.py:421
  (29 shorter events, 0.1 us)
Async XLA Ops:
  0.0 15.0 %copy-start = (f32[2,256,1024]{2,1,0:T(8,128)S(1)}, f32[2,256,1024]{2,1,0:T(8,128)}, u32[]{:S(2)}) copy-start(f32[2,256,1024]{2,1,0:T(8,128)} %obj.11) | copy-start | bytes 6291460
  0.0 16.8 %copy-start.3 = (s32[1,1,2,2]{3,2,1,0:T(2,128)S(1)}, s32[1,1,2,2]{3,2,1,0:T(2,128)}, u32[]{:S(2)}) copy-start(s32[1,1,2,2]{3,2,1,0:T(2,128)} %param.17) | copy-start | bytes 52
  1.2 13.8 %collective-permute-start.7 = (f32[1,2,256,256]{3,2,1,0:T(8,128)S(1)}, f32[1,2,256,256]{3,2,1,0:T(8,128)S(1)}, u32[]{:S(2)}, u32[]{:S(2)}) collective-permute-start(f32[1,2,256,256]{3,2,1,0:T(8,128)S(1)} %constant_dynamic-slice_fusion), channel_id=1, source_target_pairs={{0,1},{1,0},{2,3},{3,2},{4,5},{5,4},{6,7},{7,6},{8,9},{9,8},{10,11... | collective-permute-start | bytes 1572872 | tf_op jit(solution)/shard_map/ppermute | solution.py:355
  3.5 20.2 %collective-permute-start.1 = (f32[256,256]{1,0:T(8,128)S(1)}, f32[256,256]{1,0:T(8,128)S(1)}, u32[]{:S(2)}, u32[]{:S(2)}) collective-permute-start(f32[256,256]{1,0:T(8,128)S(1)} %slice_bitcast_fusion.1), channel_id=1, source_target_pairs={{0,15},{1,14},{2,0},{3,1},{4,2},{5,3},{6,4},{7,5},{8,7},{9,6},{10,... | collective-permute-start | bytes 786440 | tf_op jit(solution)/shard_map/ppermute | solution.py:355
  6.9 16.9 %collective-permute-start.3 = (f32[256,256]{1,0:T(8,128)S(1)}, f32[256,256]{1,0:T(8,128)S(1)}, u32[]{:S(2)}, u32[]{:S(2)}) collective-permute-start(f32[256,256]{1,0:T(8,128)S(1)} %slice_bitcast_fusion), channel_id=1, source_target_pairs={{0,15},{1,14},{2,0},{3,1},{4,2},{5,3},{6,4},{7,5},{8,7},{9,6},{10,... | collective-permute-start | bytes 786440 | tf_op jit(solution)/shard_map/ppermute | solution.py:355
  15.0 18.4 %collective-permute-start.8 = (f32[1,2,256,256]{3,2,1,0:T(8,128)S(1)}, f32[1,2,256,256]{3,2,1,0:T(8,128)S(1)}, u32[]{:S(2)}, u32[]{:S(2)}) collective-permute-start(f32[1,2,256,256]{3,2,1,0:T(8,128)S(1)} %collective-permute-done.7.probe_b), channel_id=1, source_target_pairs={{0,16},{1,17},{2,18},{3,19},{4,20},{5,21},{6,22},{7,23},{8,24},{9,... | collective-permute-start | bytes 1572872 | tf_op jit(solution)/shard_map/ppermute | solution.py:355
  15.1 8.6 %collective-permute-start.2 = (f32[8,256]{1,0:T(8,128)S(1)}, f32[8,256]{1,0:T(8,128)S(1)}, u32[]{:S(2)}, u32[]{:S(2)}) collective-permute-start(f32[8,256]{1,0:T(8,128)S(1)} %shard_map.136), channel_id=1, source_target_pairs={{0,2},{1,3},{2,4},{3,5},{4,6},{5,7},{6,9},{7,8},{8,10},{9,11},{10,... | collective-permute-start | bytes 24584 | tf_op jit(solution)/shard_map/ppermute | solution.py:355
  16.8 12.2 %copy-start.1 = (f32[1,1,2,256,256]{4,3,2,1,0:T(8,128)S(1)}, f32[1,1,2,256,256]{4,3,2,1,0:T(8,128)}, u32[]{:S(2)}) copy-start(f32[1,1,2,256,256]{4,3,2,1,0:T(8,128)} %meas.1) | copy-start | bytes 1572868
  16.8 6.9 %collective-permute-start = (s32[2,2]{1,0:T(2,128)S(1)}, s32[2,2]{1,0:T(2,128)S(1)}, u32[]{:S(2)}, u32[]{:S(2)}) collective-permute-start(s32[2,2]{1,0:T(2,128)S(1)} %bitcast.6), channel_id=1, source_target_pairs={{0,16},{1,17},{2,18},{3,19},{4,20},{5,21},{6,22},{7,23},{8,24},{9,... | collective-permute-start | bytes 56 | tf_op jit(solution)/shard_map/ppermute | solution.py:355
  24.4 9.1 %copy-start.2 = (f32[2,2,256,256]{3,2,1,0:T(8,128)S(1)}, f32[2,2,256,256]{3,2,1,0:T(8,128)}, u32[]{:S(2)}) copy-start(f32[2,2,256,256]{3,2,1,0:T(8,128)} %probe_a.1) | copy-start | bytes 3145732
  24.4 9.0 %copy-start.5 = (bf16[256,256]{1,0:T(8,128)(2,1)S(1)}, bf16[256,256]{1,0:T(8,128)(2,1)}, u32[]{:S(2)}) copy-start(bf16[256,256]{1,0:T(8,128)(2,1)} %constant.28.clone.refs_0_) | copy-start | bytes 393220
  24.4 9.0 %copy-start.6 = (bf16[256,256]{1,0:T(8,128)(2,1)S(1)}, bf16[256,256]{1,0:T(8,128)(2,1)}, u32[]{:S(2)}) copy-start(bf16[256,256]{1,0:T(8,128)(2,1)} %constant.29.clone.refs_1_) | copy-start | bytes 393220
  24.4 9.0 %copy-start.7 = (bf16[256,256]{1,0:T(8,128)(2,1)S(1)}, bf16[256,256]{1,0:T(8,128)(2,1)}, u32[]{:S(2)}) copy-start(bf16[256,256]{1,0:T(8,128)(2,1)} %constant.30.clone.refs_2_) | copy-start | bytes 393220
  24.4 9.0 %copy-start.8 = (bf16[256,256]{1,0:T(8,128)(2,1)S(1)}, bf16[256,256]{1,0:T(8,128)(2,1)}, u32[]{:S(2)}) copy-start(bf16[256,256]{1,0:T(8,128)(2,1)} %constant.31.clone.refs_3_) | copy-start | bytes 393220
  24.4 9.0 %copy-start.9 = (bf16[256,256]{1,0:T(8,128)(2,1)S(1)}, bf16[256,256]{1,0:T(8,128)(2,1)}, u32[]{:S(2)}) copy-start(bf16[256,256]{1,0:T(8,128)(2,1)} %constant.32.clone.refs_4_) | copy-start | bytes 393220
  24.4 9.0 %copy-start.10 = (bf16[256,256]{1,0:T(8,128)(2,1)S(1)}, bf16[256,256]{1,0:T(8,128)(2,1)}, u32[]{:S(2)}) copy-start(bf16[256,256]{1,0:T(8,128)(2,1)} %constant.33.clone.refs_5_) | copy-start | bytes 393220
  24.5 9.0 %copy-start.11 = (bf16[256,256]{1,0:T(8,128)(2,1)S(1)}, bf16[256,256]{1,0:T(8,128)(2,1)}, u32[]{:S(2)}) copy-start(bf16[256,256]{1,0:T(8,128)(2,1)} %constant.34.clone.refs_6_) | copy-start | bytes 393220
  24.5 9.0 %copy-start.12 = (bf16[256,256]{1,0:T(8,128)(2,1)S(1)}, bf16[256,256]{1,0:T(8,128)(2,1)}, u32[]{:S(2)}) copy-start(bf16[256,256]{1,0:T(8,128)(2,1)} %constant.35.clone.refs_7_) | copy-start | bytes 393220
  24.5 8.9 %collective-permute-start.5 = (f32[272,256]{1,0:T(8,128)S(1)}, f32[272,256]{1,0:T(8,128)S(1)}, u32[]{:S(2)}, u32[]{:S(2)}) collective-permute-start(f32[272,256]{1,0:T(8,128)S(1)} %get-tuple-element.12), channel_id=1, source_target_pairs={{0,240},{1,241},{2,242},{3,243},{4,244},{5,245},{6,246},{7,247},{8... | collective-permute-start | bytes 835592 | tf_op jit(solution)/shard_map/ppermute | solution.py:355
  27.2 6.3 %collective-permute-start.6 = (f32[256,256]{1,0:T(8,128)S(1)}, f32[256,256]{1,0:T(8,128)S(1)}, u32[]{:S(2)}, u32[]{:S(2)}) collective-permute-start(f32[256,256]{1,0:T(8,128)S(1)} %shard_map.138), channel_id=1, source_target_pairs={{0,240},{1,241},{2,242},{3,243},{4,244},{5,245},{6,246},{7,247},{8... | collective-permute-start | bytes 786440 | tf_op jit(solution)/shard_map/ppermute | solution.py:355
  40.5 26.9 %copy-start.4 = (f32[16,4]{0,1:T(4,128)S(1)}, f32[16,4]{0,1:T(4,128)}, u32[]{:S(2)}) copy-start(f32[16,4]{0,1:T(4,128)} %param.19) | copy-start | bytes 772
  40.5 9.2 %collective-permute-start.13 = (f32[256,256]{1,0:T(8,128)S(1)}, f32[256,256]{1,0:T(8,128)S(1)}, u32[]{:S(2)}, u32[]{:S(2)}) collective-permute-start(f32[256,256]{1,0:T(8,128)S(1)} %get-tuple-element.14.own.refs_0_), channel_id=1, source_target_pairs={{0,1},{1,0},{2,3},{3,2},{4,5},{5,4},{6,7},{7,6},{8,9},{9,8},{10,11... | collective-permute-start | bytes 786440 | tf_op jit(solution)/shard_map/ppermute | solution.py:355
  43.0 7.0 %collective-permute-start.10 = (f32[256,256]{1,0:T(8,128)S(1)}, f32[256,256]{1,0:T(8,128)S(1)}, u32[]{:S(2)}, u32[]{:S(2)}) collective-permute-start(f32[256,256]{1,0:T(8,128)S(1)} %get-tuple-element.13.own.refs_0_), channel_id=1, source_target_pairs={{0,16},{1,17},{2,18},{3,19},{4,20},{5,21},{6,22},{7,23},{8,24},{9,... | collective-permute-start | bytes 786440 | tf_op jit(solution)/shard_map/ppermute | solution.py:355
  43.0 9.5 %collective-permute-start.9 = (f32[256,256]{1,0:T(8,128)S(1)}, f32[256,256]{1,0:T(8,128)S(1)}, u32[]{:S(2)}, u32[]{:S(2)}) collective-permute-start(f32[256,256]{1,0:T(8,128)S(1)} %get-tuple-element.13.own.refs_0_), channel_id=1, source_target_pairs={{0,1},{1,0},{2,3},{3,2},{4,5},{5,4},{6,7},{7,6},{8,9},{9,8},{10,11... | collective-permute-start | bytes 786440 | tf_op jit(solution)/shard_map/ppermute | solution.py:355
  43.1 9.7 %collective-permute-start.14 = (f32[256,256]{1,0:T(8,128)S(1)}, f32[256,256]{1,0:T(8,128)S(1)}, u32[]{:S(2)}, u32[]{:S(2)}) collective-permute-start(f32[256,256]{1,0:T(8,128)S(1)} %get-tuple-element.14.own.refs_0_), channel_id=1, source_target_pairs={{0,16},{1,17},{2,18},{3,19},{4,20},{5,21},{6,22},{7,23},{8,24},{9,... | collective-permute-start | bytes 786440 | tf_op jit(solution)/shard_map/ppermute | solution.py:355
  49.6 7.0 %collective-permute-start.15 = (f32[256,256]{1,0:T(8,128)S(1)}, f32[256,256]{1,0:T(8,128)S(1)}, u32[]{:S(2)}, u32[]{:S(2)}) collective-permute-start(f32[256,256]{1,0:T(8,128)S(1)} %collective-permute-done.13.own_p.refs_1_), channel_id=1, source_target_pairs={{0,16},{1,17},{2,18},{3,19},{4,20},{5,21},{6,22},{7,23},{8,24},{9,... | collective-permute-start | bytes 786440 | tf_op jit(solution)/shard_map/ppermute | solution.py:355
  50.6 10.1 %collective-permute-start.12 = (f32[256,256]{1,0:T(8,128)S(1)}, f32[256,256]{1,0:T(8,128)S(1)}, u32[]{:S(2)}, u32[]{:S(2)}) collective-permute-start(f32[256,256]{1,0:T(8,128)S(1)} %shard_map.142), channel_id=1, source_target_pairs={{0,2},{1,3},{2,4},{3,5},{4,6},{5,7},{6,9},{7,8},{8,10},{9,11},{10,... | collective-permute-start | bytes 786440 | tf_op jit(solution)/shard_map/ppermute | solution.py:355
  52.4 21.2 %collective-permute-start.11 = (f32[256,256]{1,0:T(8,128)S(1)}, f32[256,256]{1,0:T(8,128)S(1)}, u32[]{:S(2)}, u32[]{:S(2)}) collective-permute-start(f32[256,256]{1,0:T(8,128)S(1)} %collective-permute-done.9.own_p), channel_id=1, source_target_pairs={{0,16},{1,17},{2,18},{3,19},{4,20},{5,21},{6,22},{7,23},{8,24},{9,... | collective-permute-start | bytes 786440 | tf_op jit(solution)/shard_map/ppermute | solution.py:355
  57.4 18.7 %collective-permute-start.17 = (f32[256,256]{1,0:T(8,128)S(1)}, f32[256,256]{1,0:T(8,128)S(1)}, u32[]{:S(2)}, u32[]{:S(2)}) collective-permute-start(f32[256,256]{1,0:T(8,128)S(1)} %shard_map.146), channel_id=1, source_target_pairs={{0,2},{1,3},{2,4},{3,5},{4,6},{5,7},{6,9},{7,8},{8,10},{9,11},{10,... | collective-permute-start | bytes 786440 | tf_op jit(solution)/shard_map/ppermute | solution.py:355
  60.7 15.4 %collective-permute-start.16 = (f32[256,256]{1,0:T(8,128)S(1)}, f32[256,256]{1,0:T(8,128)S(1)}, u32[]{:S(2)}, u32[]{:S(2)}) collective-permute-start(f32[256,256]{1,0:T(8,128)S(1)} %collective-permute-done.12.left_0), channel_id=1, source_target_pairs={{0,1},{1,0},{2,3},{3,2},{4,5},{5,4},{6,7},{7,6},{8,9},{9,8},{10,11... | collective-permute-start | bytes 786440 | tf_op jit(solution)/shard_map/ppermute | solution.py:355
  62.9 4.4 %collective-permute-start.4 = (f32[16,256]{1,0:T(8,128)S(1)}, f32[16,256]{1,0:T(8,128)S(1)}, u32[]{:S(2)}, u32[]{:S(2)}) collective-permute-start(f32[16,256]{1,0:T(8,128)S(1)} %get-tuple-element.11), channel_id=1, source_target_pairs={{0,16},{1,17},{2,18},{3,19},{4,20},{5,21},{6,22},{7,23},{8,24},{9,... | collective-permute-start | bytes 49160 | tf_op jit(solution)/shard_map/ppermute | solution.py:355
